TPU v7x, 128 devices: a whole 4x4x4 slice. The times are simulated.
128 devices in a mesh: cfg: 2 (over core), req: 4 (over y), seq: 16 (over z, x).
Axes of the slice: x: 4, y: 4, z: 4, core: 2. Of those that a mesh axis runs over, the one named last changes fastest.
Arguments:
- img_qkv: bfloat16 [2, 8, 4096, 6144], P('cfg', 'req', 'seq'), may hold values from -4.5 to 4.5
- txt_kv: bfloat16 [2, 8, 512, 4096], P('cfg', 'req', 'seq'), may hold values from -4.5 to 4.5
- text_len: int32 [8], P('req'), may hold values from 77 to 512
- t_index: int32 [8], P('req'), may hold values from 0 to 3
- guidance: float32 [8], P('req'), may hold values from 1.5 to 6
- modulation: float32 [2, 8, 3, 3072], P('cfg', 'req'), may hold values from -4 to 4
- img_hidden: bfloat16 [2, 8, 4096, 3072], P('cfg', 'req', 'seq'), may hold values from -6 to 6
- latents: float32 [8, 4096, 64], P('req', 'seq', 'cfg'), may hold values from -6 to 6
- proj_weight: bfloat16 [2048, 3072], P(('cfg', 'req', 'seq')), may hold values from -0.125 to 0.125
- final_weight: bfloat16 [3072, 64], replicated, may hold values from -0.109375 to 0.109375
Outputs:
- latents_next: float32 [8, 4096, 64], P('req', 'seq', 'cfg')
- vel_norm: float32 [2, 8], P('cfg', 'req')
- max_logit: float32 [2, 8], P('cfg', 'req')
All inputs are finite; a program needn't handle non-finite values.
Results may differ from a plain program's by a relative error of at most 0.0033.
Values may be sent and summed in bfloat16 or wider, within the bound.
A program may use at most 128 MiB of HBM per device.

v0:
```python
import math

import jax
import jax.numpy as jnp
from jax import lax
from jax.sharding import PartitionSpec as P

HEADS = 16
HD = 128
STEPS = 4


time_shift = 1.15
norm_eps = 1e-06


def swapped(value, axis, stride):
    return lax.ppermute(value, axis, [(i, i ^ 1 << stride) for i in range(lax.axis_size(axis))])


def sigma_of(step_index):
    fraction = 1.0 - step_index.astype(jnp.float32) / STEPS
    lifted = fraction * math.exp(time_shift)
    return lifted / (lifted + 1.0 - fraction)


def shards(
    img_qkv,
    txt_kv,
    text_len,
    t_index,
    guidance,
    modulation,
    img_hidden,
    latents,
    proj_weight,
    final_weight,
):
    local_prompts = img_qkv.shape[1]
    img_dev = img_qkv.shape[2]
    txt_dev = txt_kv.shape[2]
    joined = img_qkv[0].reshape(local_prompts, img_dev, 3, HEADS, HD)
    text_rows = txt_kv[0].reshape(local_prompts, txt_dev, 2, HEADS, HD)
    full_img, full_txt = (
        lax.all_to_all(joined, "seq", split_axis=3, concat_axis=1, tiled=True),
        lax.all_to_all(text_rows, "seq", split_axis=3, concat_axis=1, tiled=True),
    )
    img_len = full_img.shape[1]
    txt_len = full_txt.shape[1]
    local_heads = full_img.shape[3]
    block_rows = math.gcd(img_len, 1024)
    mixed_list = []
    max_list = []
    for prompt in range(local_prompts):
        key_rows = jnp.concatenate([full_txt[prompt, :, 0], full_img[prompt, :, 1]], axis=0)
        value_rows = jnp.concatenate([full_txt[prompt, :, 1], full_img[prompt, :, 2]], axis=0)
        key_valid = jnp.concatenate(
            [jnp.arange(txt_len) < text_len[prompt], jnp.ones((img_len,), jnp.bool_)]
        )

        def one_block(query_rows):
            logits = jnp.einsum(
                "qhd,khd->hqk", query_rows, key_rows, preferred_element_type=jnp.float32
            ) * HD ** (-0.5)
            logits = jnp.where(key_valid[None, None, :], logits, -jnp.inf)
            row_max = jnp.max(logits, axis=2, keepdims=True)
            weights = jnp.exp(logits - row_max)
            weights = (weights / jnp.sum(weights, axis=2, keepdims=True)).astype(jnp.bfloat16)
            mixed_rows = jnp.einsum(
                "hqk,khd->qhd", weights, value_rows, preferred_element_type=jnp.float32
            ).astype(jnp.bfloat16)
            return (mixed_rows, jnp.max(row_max))

        mixed_rows, top_logit = lax.map(
            one_block,
            full_img[prompt, :, 0].reshape(img_len // block_rows, block_rows, local_heads, HD),
        )
        mixed_list.append(mixed_rows.reshape(img_len, local_heads, HD))
        max_list.append(jnp.max(top_logit))
    local_max = jnp.stack(max_list)
    head_rows = jnp.stack(mixed_list)
    token_rows = lax.all_to_all(head_rows, "seq", split_axis=1, concat_axis=2, tiled=True)
    attended = token_rows.reshape(local_prompts * img_dev, HEADS * HD)
    projected = jnp.dot(
        attended,
        lax.all_gather(proj_weight, ("cfg", "req", "seq"), axis=0, tiled=True),
        preferred_element_type=jnp.float32,
    )
    projected = projected.reshape(local_prompts, img_dev, projected.shape[1])
    mod_rows = modulation[0]
    hidden = img_hidden[0].astype(jnp.float32) + mod_rows[:, 0][:, None, :] * projected
    average = jnp.mean(hidden, axis=2, keepdims=True)
    centred = hidden - average
    variance = jnp.mean(centred * centred, axis=2, keepdims=True)
    normed = (
        centred / jnp.sqrt(variance + norm_eps) * (1.0 + mod_rows[:, 1][:, None, :])
        + mod_rows[:, 2][:, None, :]
    ).astype(jnp.bfloat16)
    velocity = jnp.einsum("ptd,dc->ptc", normed, final_weight, preferred_element_type=jnp.float32)
    half_chan = latents.shape[2]
    copy_pos = lax.axis_index("cfg")
    own_part = lax.dynamic_slice_in_dim(velocity, copy_pos * half_chan, half_chan, 2)
    other_part = lax.dynamic_slice_in_dim(velocity, (1 - copy_pos) * half_chan, half_chan, 2)
    partner = swapped(other_part, "cfg", 0)
    is_cond = copy_pos == 0
    cond_vel = jnp.where(is_cond, own_part, partner)
    uncond_vel = jnp.where(is_cond, partner, own_part)
    guided = uncond_vel + guidance[:, None, None] * (cond_vel - uncond_vel)
    square_sum = jnp.sum(guided * guided, axis=(1, 2))
    total_sq = lax.psum(square_sum, "seq")
    global_max = lax.pmax(local_max, "seq")
    vel_norm = jnp.sqrt(total_sq / (img_len * half_chan) + norm_eps)
    euler_step = sigma_of(t_index + 1) - sigma_of(t_index)
    advanced = latents + euler_step[:, None, None] * guided
    return (advanced, vel_norm.reshape(1, local_prompts), global_max.reshape(1, local_prompts))


def solution(mesh):
    return jax.shard_map(
        shards,
        mesh=mesh,
        in_specs=(
            P("cfg", "req", "seq", None),
            P("cfg", "req", "seq", None),
            P("req"),
            P("req"),
            P("req"),
            P("cfg", "req", None, None),
            P("cfg", "req", "seq", None),
            P("req", "seq", "cfg"),
            P(("cfg", "req", "seq"), None),
            P(),
        ),
        out_specs=(P("req", "seq", "cfg"), P("cfg", "req"), P("cfg", "req")),
        check_vma=False,
    )
```

profile of v0, /device:TPU:8, one launch (start us, length us, event | category | flops | bytes accessed | tf_op | source)
XLA Modules:
  0.0 548.8 jit_solution(1137736579929246898)
XLA Ops:
  7.2 1.2 copy.41
  8.4 1.0 copy.34
  9.4 7.9 %all-to-all-start.1 = ((bf16[2,32,2,16,128]{4,1,2,0,3:T(8,128)(2,1)}), bf16[2,32,2,16,128]{4,1,2,0,3:T(8,128)(2,1)S(1)}, u32[]{:S(2)}, u32[]{:S(2)}) async-start(bf16[2,32,2,16,128]{4,1,2,0,3:T(8,128)(2,1)} %copy.34), calls=%async_computation.1 | async-start | bytes 1048576 | tf_op jit(solution)/shard_map/all_to_all | solution.py:46
  17.3 8.6 %copy.31 = bf16[1,2,256,6144]{2,3,1,0:T(8,128)(2,1)} copy(bf16[1,2,256,6144]{3,2,1,0:T(8,128)(2,1)} %param.14) | data formatting | bytes 12582912 | tf_op args[0]
  25.9 8.7 %copy.32 = bf16[2,256,3,16,128]{4,1,2,0,3:T(8,128)(2,1)} copy(bf16[2,256,3,16,128]{1,4,3,2,0:T(8,128)(2,1)} %bitcast.151) | data formatting | bytes 12582912 | tf_op jit(solution)/shard_map/reshape;squeeze | solution.py:42
  34.6 7.4 %all-to-all-start = ((bf16[2,256,3,16,128]{4,1,2,0,3:T(8,128)(2,1)}), bf16[2,256,3,16,128]{4,1,2,0,3:T(8,128)(2,1)}, u32[]{:S(2)}, u32[]{:S(2)}) async-start(bf16[2,256,3,16,128]{4,1,2,0,3:T(8,128)(2,1)} %copy.32), calls=%async_computation | async-start | bytes 12582912 | tf_op jit(solution)/shard_map/all_to_all | solution.py:45
  42.1 0.7 all-gather.2.cloned.1.call-update
  43.3 0.6 iota_compare_fusion.1
  44.0 0.7 iota_compare_fusion
  45.3 0.8 slice_bitcast_fusion.6
  46.1 93.6 %all-to-all-done = bf16[2,256,3,16,128]{4,1,2,0,3:T(8,128)(2,1)} async-done(((bf16[2,256,3,16,128]{4,1,2,0,3:T(8,128)(2,1)}), bf16[2,256,3,16,128]{4,1,2,0,3:T(8,128)(2,1)}, u32[]{:S(2)}, u32[]{:S(2)}) %all-to-all-start) | async-done | bytes 6291488 | tf_op jit(solution)/shard_map/all_to_all | solution.py:45
  139.7 3.2 copy.33
  142.9 1.7 slice_bitcast_fusion.2
  144.7 1.2 pad_maximum_fusion.1
  145.8 1.1 broadcast.86.clone.1
  146.9 122.4 %while.24 = (s32[]{:T(128)}, bf16[4,1024,1,128]{3,1,2,0:T(8,128)(2,1)}, f32[4]{0:T(128)S(1)}, pred[4608]{0:T(1024)(128)(4,1)S(1)}, bf16[4,1024,1,128]{3,1,2,0:T(...) while((s32[]{:T(128)}, ...), condition=%wide.region_4.5_spmd, body=%wide.region_0.4_spmd.sunk | while | flops 2477389824 | bytes 59542120 | solution.py:74
  147.0 8.2 %fusion.57 = (f32[1024]{0:T(1024)S(1)}, f32[1024,4608]{1,0:T(8,128)}) fusion(pred[4608]{0:T(1024)(128)(4,1)S(1)} %get-tuple-element.343, bf16[4608,1,128]{2,0,1:T(8,128)(2,1)S(1)} %get-tuple-element.345, bf16[4,1024,1,128]{3,1,2,0:T(8,128)(2,1)S(1)} %get-tuple-element.344, s32[]{:T(128)} %get-tuple-element.332), kind=kOutput, calls=%fused_computation.5.clone.1 | convolution fusion | flops 1222114304 | bytes 20325380 | tf_op jit(solution)/shard_map/while/body/eval_jaxpr/qhd,khd->hqk/dot_general | solution.py:62
  155.2 13.3 %fusion.58 = (f32[]{:T(128)}, f32[1024]{0:T(1024)S(1)}) fusion(f32[1024,4608]{1,0:T(8,128)} %get-tuple-element.285, pred[4608]{0:T(1024)(128)(4,1)S(1)} %get-tuple-element.343, f32[1024]{0:T(1024)S(1)} %get-tuple-element.286), kind=kLoop, calls=%fused_computation.4.clone.1 | loop fusion | flops 23591936 | bytes 18887172 | tf_op jit(solution)/shard_map/while/body/eval_jaxpr/reduce_max | solution.py:72
  168.4 9.6 %fusion.59 = bf16[4,1024,1,128]{3,1,2,0:T(8,128)(2,1)} fusion(bf16[4,1024,1,128]{3,1,2,0:T(8,128)(2,1)} %get-tuple-element.333, s32[]{:T(128)} %get-tuple-element.332, bf16[4608,1,128]{2,0,1:T(8,128)(2,1)} %get-tuple-element.346, f32[1024,4608]{1,0:T(8,128)} %get-tuple-element.285, f32[1024]{0:T(1024)S(1)} %get-tuple-element.287, ...), kind=kOutput, calls=%fused_computation.12.clone.1 | convolution fusion | flops 1231683584 | bytes 20329472 | tf_op jit(solution)/shard_map/while/body/eval_jaxpr/hqk,khd->qhd/dot_general | solution.py:69
  178.0 0.8 dynamic_update_slice.21
  178.8 7.9 %fusion.57 = (f32[1024]{0:T(1024)S(1)}, f32[1024,4608]{1,0:T(8,128)}) fusion(pred[4608]{0:T(1024)(128)(4,1)S(1)} %get-tuple-element.343, bf16[4608,1,128]{2,0,1:T(8,128)(2,1)S(1)} %get-tuple-element.345, bf16[4,1024,1,128]{3,1,2,0:T(8,128)(2,1)S(1)} %get-tuple-element.344, s32[]{:T(128)} %get-tuple-element.332), kind=kOutput, calls=%fused_computation.5.clone.1 | convolution fusion | flops 1222114304 | bytes 20325380 | tf_op jit(solution)/shard_map/while/body/eval_jaxpr/qhd,khd->hqk/dot_general | solution.py:62
  186.6 12.0 %fusion.58 = (f32[]{:T(128)}, f32[1024]{0:T(1024)S(1)}) fusion(f32[1024,4608]{1,0:T(8,128)} %get-tuple-element.285, pred[4608]{0:T(1024)(128)(4,1)S(1)} %get-tuple-element.343, f32[1024]{0:T(1024)S(1)} %get-tuple-element.286), kind=kLoop, calls=%fused_computation.4.clone.1 | loop fusion | flops 23591936 | bytes 18887172 | tf_op jit(solution)/shard_map/while/body/eval_jaxpr/reduce_max | solution.py:72
  198.6 9.6 %fusion.59 = bf16[4,1024,1,128]{3,1,2,0:T(8,128)(2,1)} fusion(bf16[4,1024,1,128]{3,1,2,0:T(8,128)(2,1)} %get-tuple-element.333, s32[]{:T(128)} %get-tuple-element.332, bf16[4608,1,128]{2,0,1:T(8,128)(2,1)} %get-tuple-element.346, f32[1024,4608]{1,0:T(8,128)} %get-tuple-element.285, f32[1024]{0:T(1024)S(1)} %get-tuple-element.287, ...), kind=kOutput, calls=%fused_computation.12.clone.1 | convolution fusion | flops 1231683584 | bytes 20329472 | tf_op jit(solution)/shard_map/while/body/eval_jaxpr/hqk,khd->qhd/dot_general | solution.py:69
  208.2 0.8 dynamic_update_slice.21
  209.0 7.9 %fusion.57 = (f32[1024]{0:T(1024)S(1)}, f32[1024,4608]{1,0:T(8,128)}) fusion(pred[4608]{0:T(1024)(128)(4,1)S(1)} %get-tuple-element.343, bf16[4608,1,128]{2,0,1:T(8,128)(2,1)S(1)} %get-tuple-element.345, bf16[4,1024,1,128]{3,1,2,0:T(8,128)(2,1)S(1)} %get-tuple-element.344, s32[]{:T(128)} %get-tuple-element.332), kind=kOutput, calls=%fused_computation.5.clone.1 | convolution fusion | flops 1222114304 | bytes 20325380 | tf_op jit(solution)/shard_map/while/body/eval_jaxpr/qhd,khd->hqk/dot_general | solution.py:62
  216.8 12.0 %fusion.58 = (f32[]{:T(128)}, f32[1024]{0:T(1024)S(1)}) fusion(f32[1024,4608]{1,0:T(8,128)} %get-tuple-element.285, pred[4608]{0:T(1024)(128)(4,1)S(1)} %get-tuple-element.343, f32[1024]{0:T(1024)S(1)} %get-tuple-element.286), kind=kLoop, calls=%fused_computation.4.clone.1 | loop fusion | flops 23591936 | bytes 18887172 | tf_op jit(solution)/shard_map/while/body/eval_jaxpr/reduce_max | solution.py:72
  228.8 9.6 %fusion.59 = bf16[4,1024,1,128]{3,1,2,0:T(8,128)(2,1)} fusion(bf16[4,1024,1,128]{3,1,2,0:T(8,128)(2,1)} %get-tuple-element.333, s32[]{:T(128)} %get-tuple-element.332, bf16[4608,1,128]{2,0,1:T(8,128)(2,1)} %get-tuple-element.346, f32[1024,4608]{1,0:T(8,128)} %get-tuple-element.285, f32[1024]{0:T(1024)S(1)} %get-tuple-element.287, ...), kind=kOutput, calls=%fused_computation.12.clone.1 | convolution fusion | flops 1231683584 | bytes 20329472 | tf_op jit(solution)/shard_map/while/body/eval_jaxpr/hqk,khd->qhd/dot_general | solution.py:69
  238.4 0.8 dynamic_update_slice.21
  239.2 7.9 %fusion.57 = (f32[1024]{0:T(1024)S(1)}, f32[1024,4608]{1,0:T(8,128)}) fusion(pred[4608]{0:T(1024)(128)(4,1)S(1)} %get-tuple-element.343, bf16[4608,1,128]{2,0,1:T(8,128)(2,1)S(1)} %get-tuple-element.345, bf16[4,1024,1,128]{3,1,2,0:T(8,128)(2,1)S(1)} %get-tuple-element.344, s32[]{:T(128)} %get-tuple-element.332), kind=kOutput, calls=%fused_computation.5.clone.1 | convolution fusion | flops 1222114304 | bytes 20325380 | tf_op jit(solution)/shard_map/while/body/eval_jaxpr/qhd,khd->hqk/dot_general | solution.py:62
  247.0 12.0 %fusion.58 = (f32[]{:T(128)}, f32[1024]{0:T(1024)S(1)}) fusion(f32[1024,4608]{1,0:T(8,128)} %get-tuple-element.285, pred[4608]{0:T(1024)(128)(4,1)S(1)} %get-tuple-element.343, f32[1024]{0:T(1024)S(1)} %get-tuple-element.286), kind=kLoop, calls=%fused_computation.4.clone.1 | loop fusion | flops 23591936 | bytes 18887172 | tf_op jit(solution)/shard_map/while/body/eval_jaxpr/reduce_max | solution.py:72
  259.0 9.6 %fusion.59 = bf16[4,1024,1,128]{3,1,2,0:T(8,128)(2,1)} fusion(bf16[4,1024,1,128]{3,1,2,0:T(8,128)(2,1)} %get-tuple-element.333, s32[]{:T(128)} %get-tuple-element.332, bf16[4608,1,128]{2,0,1:T(8,128)(2,1)} %get-tuple-element.346, f32[1024,4608]{1,0:T(8,128)} %get-tuple-element.285, f32[1024]{0:T(1024)S(1)} %get-tuple-element.287, ...), kind=kOutput, calls=%fused_computation.12.clone.1 | convolution fusion | flops 1231683584 | bytes 20329472 | tf_op jit(solution)/shard_map/while/body/eval_jaxpr/hqk,khd->qhd/dot_general | solution.py:69
  268.6 0.8 dynamic_update_slice.21
  269.4 2.7 pad_maximum_fusion.3
  272.3 122.5 %while.25 = (s32[]{:T(128)}, bf16[4,1024,1,128]{3,1,2,0:T(8,128)(2,1)S(1)}, f32[4]{0:T(128)S(1)}, pred[4608]{0:T(1024)(128)(4,1)S(1)}, bf16[4,1024,1,128]{3,1,2,...) while((s32[]{:T(128)}, ...), condition=%wide.region_9.10_spmd, body=%wide.region_5.9_spmd.sunk | while | flops 2477389824 | bytes 59542120 | solution.py:74
  272.4 8.8 %fusion.61 = (f32[1024]{0:T(1024)S(1)}, f32[1024,4608]{1,0:T(8,128)}) fusion(pred[4608]{0:T(1024)(128)(4,1)S(1)} %get-tuple-element.319, bf16[4608,1,128]{2,0,1:T(8,128)(2,1)S(1)} %get-tuple-element.321, bf16[4,1024,1,128]{3,1,2,0:T(8,128)(2,1)} %get-tuple-element.320, s32[]{:T(128)} %get-tuple-element.308), kind=kOutput, calls=%fused_computation.23.clone.1 | convolution fusion | flops 1222114304 | bytes 20325376 | tf_op jit(solution)/shard_map/while/body/eval_jaxpr/qhd,khd->hqk/dot_general | solution.py:62
  281.3 12.0 %fusion.62 = (f32[]{:T(128)}, f32[1024]{0:T(1024)S(1)}) fusion(f32[1024,4608]{1,0:T(8,128)} %get-tuple-element.296, pred[4608]{0:T(1024)(128)(4,1)S(1)} %get-tuple-element.319, f32[1024]{0:T(1024)S(1)} %get-tuple-element.297), kind=kLoop, calls=%fused_computation.22.clone.1 | loop fusion | flops 23591936 | bytes 18887172 | tf_op jit(solution)/shard_map/while/body/eval_jaxpr/reduce_max | solution.py:72
  293.3 9.0 %fusion.63 = bf16[4,1024,1,128]{3,1,2,0:T(8,128)(2,1)S(1)} fusion(bf16[4,1024,1,128]{3,1,2,0:T(8,128)(2,1)S(1)} %get-tuple-element.309, s32[]{:T(128)} %get-tuple-element.308, bf16[4608,1,128]{2,0,1:T(8,128)(2,1)} %get-tuple-element.322, f32[1024,4608]{1,0:T(8,128)} %get-tuple-element.296, f32[1024]{0:T(1024)S(1)} %get-tuple-element.298, ...), kind=kOutput, calls=%fused_computation.30.clone.1 | convolution fusion | flops 1231683584 | bytes 20329476 | tf_op jit(solution)/shard_map/while/body/eval_jaxpr/hqk,khd->qhd/dot_general | solution.py:69
  302.3 0.8 dynamic_update_slice.23
  303.0 8.8 %fusion.61 = (f32[1024]{0:T(1024)S(1)}, f32[1024,4608]{1,0:T(8,128)}) fusion(pred[4608]{0:T(1024)(128)(4,1)S(1)} %get-tuple-element.319, bf16[4608,1,128]{2,0,1:T(8,128)(2,1)S(1)} %get-tuple-element.321, bf16[4,1024,1,128]{3,1,2,0:T(8,128)(2,1)} %get-tuple-element.320, s32[]{:T(128)} %get-tuple-element.308), kind=kOutput, calls=%fused_computation.23.clone.1 | convolution fusion | flops 1222114304 | bytes 20325376 | tf_op jit(solution)/shard_map/while/body/eval_jaxpr/qhd,khd->hqk/dot_general | solution.py:62
  311.9 12.0 %fusion.62 = (f32[]{:T(128)}, f32[1024]{0:T(1024)S(1)}) fusion(f32[1024,4608]{1,0:T(8,128)} %get-tuple-element.296, pred[4608]{0:T(1024)(128)(4,1)S(1)} %get-tuple-element.319, f32[1024]{0:T(1024)S(1)} %get-tuple-element.297), kind=kLoop, calls=%fused_computation.22.clone.1 | loop fusion | flops 23591936 | bytes 18887172 | tf_op jit(solution)/shard_map/while/body/eval_jaxpr/reduce_max | solution.py:72
  323.8 9.0 %fusion.63 = bf16[4,1024,1,128]{3,1,2,0:T(8,128)(2,1)S(1)} fusion(bf16[4,1024,1,128]{3,1,2,0:T(8,128)(2,1)S(1)} %get-tuple-element.309, s32[]{:T(128)} %get-tuple-element.308, bf16[4608,1,128]{2,0,1:T(8,128)(2,1)} %get-tuple-element.322, f32[1024,4608]{1,0:T(8,128)} %get-tuple-element.296, f32[1024]{0:T(1024)S(1)} %get-tuple-element.298, ...), kind=kOutput, calls=%fused_computation.30.clone.1 | convolution fusion | flops 1231683584 | bytes 20329476 | tf_op jit(solution)/shard_map/while/body/eval_jaxpr/hqk,khd->qhd/dot_general | solution.py:69
  332.8 0.8 dynamic_update_slice.23
  333.6 8.8 %fusion.61 = (f32[1024]{0:T(1024)S(1)}, f32[1024,4608]{1,0:T(8,128)}) fusion(pred[4608]{0:T(1024)(128)(4,1)S(1)} %get-tuple-element.319, bf16[4608,1,128]{2,0,1:T(8,128)(2,1)S(1)} %get-tuple-element.321, bf16[4,1024,1,128]{3,1,2,0:T(8,128)(2,1)} %get-tuple-element.320, s32[]{:T(128)} %get-tuple-element.308), kind=kOutput, calls=%fused_computation.23.clone.1 | convolution fusion | flops 1222114304 | bytes 20325376 | tf_op jit(solution)/shard_map/while/body/eval_jaxpr/qhd,khd->hqk/dot_general | solution.py:62
  342.4 12.0 %fusion.62 = (f32[]{:T(128)}, f32[1024]{0:T(1024)S(1)}) fusion(f32[1024,4608]{1,0:T(8,128)} %get-tuple-element.296, pred[4608]{0:T(1024)(128)(4,1)S(1)} %get-tuple-element.319, f32[1024]{0:T(1024)S(1)} %get-tuple-element.297), kind=kLoop, calls=%fused_computation.22.clone.1 | loop fusion | flops 23591936 | bytes 18887172 | tf_op jit(solution)/shard_map/while/body/eval_jaxpr/reduce_max | solution.py:72
  354.4 9.0 %fusion.63 = bf16[4,1024,1,128]{3,1,2,0:T(8,128)(2,1)S(1)} fusion(bf16[4,1024,1,128]{3,1,2,0:T(8,128)(2,1)S(1)} %get-tuple-element.309, s32[]{:T(128)} %get-tuple-element.308, bf16[4608,1,128]{2,0,1:T(8,128)(2,1)} %get-tuple-element.322, f32[1024,4608]{1,0:T(8,128)} %get-tuple-element.296, f32[1024]{0:T(1024)S(1)} %get-tuple-element.298, ...), kind=kOutput, calls=%fused_computation.30.clone.1 | convolution fusion | flops 1231683584 | bytes 20329476 | tf_op jit(solution)/shard_map/while/body/eval_jaxpr/hqk,khd->qhd/dot_general | solution.py:69
  363.4 0.8 dynamic_update_slice.23
  364.2 8.8 %fusion.61 = (f32[1024]{0:T(1024)S(1)}, f32[1024,4608]{1,0:T(8,128)}) fusion(pred[4608]{0:T(1024)(128)(4,1)S(1)} %get-tuple-element.319, bf16[4608,1,128]{2,0,1:T(8,128)(2,1)S(1)} %get-tuple-element.321, bf16[4,1024,1,128]{3,1,2,0:T(8,128)(2,1)} %get-tuple-element.320, s32[]{:T(128)} %get-tuple-element.308), kind=kOutput, calls=%fused_computation.23.clone.1 | convolution fusion | flops 1222114304 | bytes 20325376 | tf_op jit(solution)/shard_map/while/body/eval_jaxpr/qhd,khd->hqk/dot_general | solution.py:62
  373.0 12.0 %fusion.62 = (f32[]{:T(128)}, f32[1024]{0:T(1024)S(1)}) fusion(f32[1024,4608]{1,0:T(8,128)} %get-tuple-element.296, pred[4608]{0:T(1024)(128)(4,1)S(1)} %get-tuple-element.319, f32[1024]{0:T(1024)S(1)} %get-tuple-element.297), kind=kLoop, calls=%fused_computation.22.clone.1 | loop fusion | flops 23591936 | bytes 18887172 | tf_op jit(solution)/shard_map/while/body/eval_jaxpr/reduce_max | solution.py:72
  385.0 9.0 %fusion.63 = bf16[4,1024,1,128]{3,1,2,0:T(8,128)(2,1)S(1)} fusion(bf16[4,1024,1,128]{3,1,2,0:T(8,128)(2,1)S(1)} %get-tuple-element.309, s32[]{:T(128)} %get-tuple-element.308, bf16[4608,1,128]{2,0,1:T(8,128)(2,1)} %get-tuple-element.322, f32[1024,4608]{1,0:T(8,128)} %get-tuple-element.296, f32[1024]{0:T(1024)S(1)} %get-tuple-element.298, ...), kind=kOutput, calls=%fused_computation.30.clone.1 | convolution fusion | flops 1231683584 | bytes 20329476 | tf_op jit(solution)/shard_map/while/body/eval_jaxpr/hqk,khd->qhd/dot_general | solution.py:69
  394.0 0.8 dynamic_update_slice.23
  394.7 1.5 pad_maximum_fusion
  396.2 18.4 %copy.38 = bf16[2,4096,1,128]{3,0,2,1:T(2,128)(2,1)} copy(bf16[2,4096,1,128]{3,1,2,0:T(8,128)(2,1)S(1)} %pad_maximum_fusion) | data formatting | bytes 4194304 | tf_op jit(solution)/shard_map/stack | solution.py:81
  414.5 5.4 all-to-all-start.2
  420.1 0.6 reduce_max.54
  421.3 27.2 %all-to-all-done.2 = bf16[2,4096,1,128]{3,0,2,1:T(2,128)(2,1)S(1)} async-done(((bf16[2,4096,1,128]{3,0,2,1:T(2,128)(2,1)}), bf16[2,4096,1,128]{3,0,2,1:T(2,128)(2,1)S(1)}, u32[]{:S(2)}, u32[]{:S(2)}) %all-to-all-start.2) | async-done | bytes 2097184 | tf_op jit(solution)/shard_map/all_to_all | solution.py:82
  448.7 1.4 copy.40
  450.1 2.3 dot_general.20
  452.4 10.9 %fusion.46 = (f32[2,256]{1,0:T(2,128)S(1)}, f32[2,256,3072]{2,1,0:T(8,128)S(1)}) fusion(bf16[2,256,2048]{2,1,0:T(8,128)(2,1)} %dot_general.20, bf16[2048,3072]{1,0:T(8,128)(2,1)} %all-gather.2.cloned.1.call-done, f32[2,3072]{1,0:T(2,128)S(1)} %get-tuple-element.189, bf16[1,2,256,3072]{3,2,1,0:T(8,128)(2,1)} %param.20), kind=kOutput, calls=%fused_computation.72 | convolution fusion | flops 6448741888 | bytes 24143872 | tf_op jit(solution)/shard_map/dot_general | solution.py:84
  463.3 0.8 multiply_reduce_fusion
  464.1 1.6 fusion.42
  465.8 1.4 maximum_bitcast_fusion
  467.2 36.1 %pmax.7 = f32[1,2]{1,0:T(1,128)} all-reduce(f32[1,2]{1,0:T(1,128)S(1)} %maximum_bitcast_fusion), channel_id=1, replica_groups=mesh['cfg'=2,'req'=4,'seq'=16] {'seq'}, use_global_device_ids=true, to_apply=%region_16.17 | all-reduce | flops 2 | bytes 16 | tf_op jit(solution)/shard_map/pmax | solution.py:111
  503.3 0.8 multiply_reduce_fusion.1
  504.1 37.3 %psum.7 = f32[2]{0:T(128)S(1)} all-reduce(f32[2]{0:T(128)S(1)} %get-tuple-element.185), channel_id=1, replica_groups=mesh['cfg'=2,'req'=4,'seq'=16] {'seq'}, use_global_device_ids=true, to_apply=%region_13.14 | all-reduce | flops 2 | bytes 16 | tf_op jit(solution)/shard_map/psum | solution.py:110
  (42 shorter events, 3.0 us)
Async XLA Ops:
  7.2 456.9 %copy-start = (bf16[3072,64]{0,1:T(8,128)(2,1)S(1)}, bf16[3072,64]{0,1:T(8,128)(2,1)}, u32[]{:S(2)}) copy-start(bf16[3072,64]{0,1:T(8,128)(2,1)} %param.23) | copy-start | bytes 1179652
  9.4 25.2 %all-to-all-start.1 = ((bf16[2,32,2,16,128]{4,1,2,0,3:T(8,128)(2,1)}), bf16[2,32,2,16,128]{4,1,2,0,3:T(8,128)(2,1)S(1)}, u32[]{:S(2)}, u32[]{:S(2)}) async-start(bf16[2,32,2,16,128]{4,1,2,0,3:T(8,128)(2,1)} %copy.34), calls=%async_computation.1 | async-start | bytes 1048576 | tf_op jit(solution)/shard_map/all_to_all | solution.py:46
  34.6 8.1 %copy-start.6 = (s32[2]{0:T(128)S(1)}, s32[2]{0:T(128)}, u32[]{:S(2)}) copy-start(s32[2]{0:T(128)} %param.16) | copy-start | bytes 28
  34.6 105.1 %all-to-all-start = ((bf16[2,256,3,16,128]{4,1,2,0,3:T(8,128)(2,1)}), bf16[2,256,3,16,128]{4,1,2,0,3:T(8,128)(2,1)}, u32[]{:S(2)}, u32[]{:S(2)}) async-start(bf16[2,256,3,16,128]{4,1,2,0,3:T(8,128)(2,1)} %copy.32), calls=%async_computation | async-start | bytes 12582912 | tf_op jit(solution)/shard_map/all_to_all | solution.py:45
  42.0 410.4 %all-gather.2.cloned.1.call-start = ((), (), s32[]{:S(2)}) async-start(), calls=%async_computation.3 | async-start | bytes 12681216 | tf_op jit(solution)/shard_map/all_gather | solution.py:86
  146.9 122.4 %copy-start.2 = (bf16[512,1,128]{2,0,1:T(8,128)(2,1)S(1)}, bf16[512,1,128]{2,0,1:T(8,128)(2,1)}, u32[]{:S(2)}) copy-start(bf16[512,1,128]{2,0,1:T(8,128)(2,1)} %get-tuple-element.182) | copy-start | bytes 393220
  146.9 122.4 %copy-start.3 = (bf16[512,1,128]{2,0,1:T(8,128)(2,1)S(1)}, bf16[512,1,128]{2,0,1:T(8,128)(2,1)}, u32[]{:S(2)}) copy-start(bf16[512,1,128]{2,0,1:T(8,128)(2,1)} %get-tuple-element.183) | copy-start | bytes 393220
  146.9 125.3 %copy-start.1 = (pred[4608]{0:T(1024)(128)(4,1)S(1)}, pred[4608]{0:T(1024)(128)(4,1)}, u32[]{:S(2)}) copy-start(pred[4608]{0:T(1024)(128)(4,1)} %concatenate.21) | copy-start | bytes 13828
  269.3 2.9 copy-start.9
  394.7 25.3 %copy-start.8 = (s32[2]{0:T(128)S(1)}, s32[2]{0:T(128)}, u32[]{:S(2)}) copy-start(s32[2]{0:T(128)} %param.17) | copy-start | bytes 28
  394.7 25.3 %copy-start.4 = (f32[1,2,3,3072]{3,1,2,0:T(2,128)S(1)}, f32[1,2,3,3072]{3,1,2,0:T(2,128)}, u32[]{:S(2)}) copy-start(f32[1,2,3,3072]{3,1,2,0:T(2,128)} %param.19) | copy-start | bytes 221188
  394.7 25.3 %copy-start.10 = (f32[4]{0:T(128)S(1)}, f32[4]{0:T(128)}, u32[]{:S(2)}) copy-start(f32[4]{0:T(128)} %copy-done.9) | copy-start | bytes 52
  414.5 33.9 %all-to-all-start.2 = ((bf16[2,4096,1,128]{3,0,2,1:T(2,128)(2,1)}), bf16[2,4096,1,128]{3,0,2,1:T(2,128)(2,1)S(1)}, u32[]{:S(2)}, u32[]{:S(2)}) async-start(bf16[2,4096,1,128]{3,0,2,1:T(2,128)(2,1)} %copy.38), calls=%async_computation.2 | async-start | bytes 4194304 | tf_op jit(solution)/shard_map/all_to_all | solution.py:82
  464.1 39.2 %copy-start.5 = (f32[2,256,32]{1,2,0:T(8,128)S(1)}, f32[2,256,32]{1,2,0:T(8,128)}, u32[]{:S(2)}) copy-start(f32[2,256,32]{1,2,0:T(8,128)} %param.21) | copy-start | bytes 196612
  464.1 39.2 %copy-start.7 = (f32[2]{0:T(128)S(1)}, f32[2]{0:T(128)}, u32[]{:S(2)}) copy-start(f32[2]{0:T(128)} %param.18) | copy-start | bytes 28
  465.7 37.5 %collective-permute-start = (f32[2,256,32]{1,2,0:T(8,128)S(1)}, f32[2,256,32]{1,2,0:T(8,128)S(1)}, u32[]{:S(2)}, u32[]{:S(2)}) collective-permute-start(f32[2,256,32]{1,2,0:T(8,128)S(1)} %constant_dynamic-slice_fusion), channel_id=1, source_target_pairs={{0,64},{64,0},{1,65},{65,1},{2,66},{66,2},{3,67},{67,3},{4,68},{68... | collective-permute-start | bytes 196616 | tf_op jit(solution)/shard_map/ppermute | solution.py:18
Sparse Core Ops, SparseCore 0:
  45.9 123.3 all-gather.1
where the time goes:
time: 550 us; the launch traced here: 549 us
  matrix products  154 us (28%)
  waiting for transfers between devices  121 us (22%)
  other arithmetic  108 us (20%)
  blocking collectives  73.4 us (13%)
  local copies, waits for them, and re-layouts  56.1 us (10%)
  starting transfers between devices  20.8 us (4%)
  between operations  14.3 us (3%)
    reduce_max x8, other arithmetic, one_block(): return (mixed_rows, jnp.max(row_max))  97.1 us
    all_to_all x1, waiting for transfers between devices, shards(): lax.all_to_all(joined, 'seq', split_axis=3, concat_axis=1, tiled=True)  93.6 us
    dot_general x8, matrix products, one_block(): jnp.einsum('hqk,khd->qhd', weights, value_rows, preferred_element_type=jn...  74.3 us
    dot_general x8, matrix products, one_block(): jnp.einsum('qhd,khd->hqk', query_rows, key_rows, preferred_element_type=j...  67.2 us
    psum x1, blocking collectives, shards(): total_sq = lax.psum(square_sum, 'seq')  37.3 us
    pmax x1, blocking collectives, shards(): global_max = lax.pmax(local_max, 'seq')  36.1 us
    all_to_all x1, waiting for transfers between devices, shards(): lax.all_to_all(head_rows, 'seq', split_axis=1, concat_axis=2, tiled=True)  27.2 us
    another operation x1, local copies, waits for them, and re-layouts, shards(): head_rows = jnp.stack(mixed_list)  18.4 us
  transfers between devices with their start and end apart: 5, of which 2 were waited for; matrix products, arithmetic and copies ran while one was open for 55% of the time, Pallas kernels for 0%

commit v1 on v0

--- a/solution.py
+++ b/solution.py
@@ -1,13 +1,17 @@
+import functools
 import math
 
 import jax
 import jax.numpy as jnp
 from jax import lax
+from jax.experimental import pallas as pl
+from jax.experimental.pallas import tpu as pltpu
 from jax.sharding import PartitionSpec as P
 
 HEADS = 16
 HD = 128
 STEPS = 4
+BQ = 512
 
 
 time_shift = 1.15
@@ -22,6 +26,67 @@
     fraction = 1.0 - step_index.astype(jnp.float32) / STEPS
     lifted = fraction * math.exp(time_shift)
     return lifted / (lifted + 1.0 - fraction)
+
+
+def attn_kernel(tl_ref, q_ref, kt_ref, vt_ref, ki_ref, vi_ref, o_ref, m_ref):
+    p = pl.program_id(0)
+    q = q_ref[...]
+    dims = (((1,), (1,)), ((), ()))
+    st = lax.dot_general(q, kt_ref[...], dims, preferred_element_type=jnp.float32) * HD ** (-0.5)
+    si = lax.dot_general(q, ki_ref[...], dims, preferred_element_type=jnp.float32) * HD ** (-0.5)
+    col = lax.broadcasted_iota(jnp.int32, st.shape, 1)
+    st = jnp.where(col < tl_ref[p], st, -jnp.inf)
+    m = jnp.maximum(jnp.max(st, axis=1, keepdims=True), jnp.max(si, axis=1, keepdims=True))
+    et = jnp.exp(st - m)
+    ei = jnp.exp(si - m)
+    inv = 1.0 / (jnp.sum(et, axis=1, keepdims=True) + jnp.sum(ei, axis=1, keepdims=True))
+    pt = (et * inv).astype(jnp.bfloat16)
+    pi = (ei * inv).astype(jnp.bfloat16)
+    o = jnp.dot(pt, vt_ref[...], preferred_element_type=jnp.float32)
+    o = o + jnp.dot(pi, vi_ref[...], preferred_element_type=jnp.float32)
+    o_ref[...] = o.astype(o_ref.dtype)
+    m_ref[...] = jnp.full(m_ref.shape, jnp.max(m), jnp.float32)
+
+
+def attention(text_len, img, txt):
+    prompts, img_len, _ = img.shape
+    txt_len = txt.shape[1]
+    nq = img_len // BQ
+    grid_spec = pltpu.PrefetchScalarGridSpec(
+        num_scalar_prefetch=1,
+        grid=(prompts, nq),
+        in_specs=[
+            pl.BlockSpec((None, BQ, HD), lambda p, i, tl: (p, i, 0)),
+            pl.BlockSpec((None, txt_len, HD), lambda p, i, tl: (p, 0, 0)),
+            pl.BlockSpec((None, txt_len, HD), lambda p, i, tl: (p, 0, 1)),
+            pl.BlockSpec((None, img_len, HD), lambda p, i, tl: (p, 0, 1)),
+            pl.BlockSpec((None, img_len, HD), lambda p, i, tl: (p, 0, 2)),
+        ],
+        out_specs=[
+            pl.BlockSpec((None, BQ, HD), lambda p, i, tl: (p, i, 0)),
+            pl.BlockSpec((None, None, 8, 128), lambda p, i, tl: (p, i, 0, 0)),
+        ],
+    )
+    flops = 4 * prompts * img_len * (img_len + txt_len) * HD
+    cost = pl.CostEstimate(
+        flops=flops,
+        transcendentals=prompts * img_len * (img_len + txt_len),
+        bytes_accessed=img.size * 2 + txt.size * 2 + prompts * img_len * HD * 2,
+    )
+    out, top = pl.pallas_call(
+        attn_kernel,
+        grid_spec=grid_spec,
+        out_shape=[
+            jax.ShapeDtypeStruct((prompts, img_len, HD), jnp.bfloat16),
+            jax.ShapeDtypeStruct((prompts, nq, 8, 128), jnp.float32),
+        ],
+        compiler_params=pltpu.CompilerParams(
+            dimension_semantics=("arbitrary", "arbitrary"),
+            vmem_limit_bytes=60 * 1024 * 1024,
+        ),
+        cost_estimate=cost,
+    )(text_len, img, txt, txt, img, img)
+    return out, jnp.max(top, axis=(1, 2, 3))
 
 
 def shards(
@@ -39,46 +104,18 @@
     local_prompts = img_qkv.shape[1]
     img_dev = img_qkv.shape[2]
     txt_dev = txt_kv.shape[2]
+    seq = lax.axis_size("seq")
     joined = img_qkv[0].reshape(local_prompts, img_dev, 3, HEADS, HD)
     text_rows = txt_kv[0].reshape(local_prompts, txt_dev, 2, HEADS, HD)
-    full_img, full_txt = (
-        lax.all_to_all(joined, "seq", split_axis=3, concat_axis=1, tiled=True),
-        lax.all_to_all(text_rows, "seq", split_axis=3, concat_axis=1, tiled=True),
-    )
+    full_img = lax.all_to_all(joined, "seq", split_axis=3, concat_axis=1, tiled=True)
+    full_txt = lax.all_to_all(text_rows, "seq", split_axis=3, concat_axis=1, tiled=True)
     img_len = full_img.shape[1]
     txt_len = full_txt.shape[1]
     local_heads = full_img.shape[3]
-    block_rows = math.gcd(img_len, 1024)
-    mixed_list = []
-    max_list = []
-    for prompt in range(local_prompts):
-        key_rows = jnp.concatenate([full_txt[prompt, :, 0], full_img[prompt, :, 1]], axis=0)
-        value_rows = jnp.concatenate([full_txt[prompt, :, 1], full_img[prompt, :, 2]], axis=0)
-        key_valid = jnp.concatenate(
-            [jnp.arange(txt_len) < text_len[prompt], jnp.ones((img_len,), jnp.bool_)]
-        )
-
-        def one_block(query_rows):
-            logits = jnp.einsum(
-                "qhd,khd->hqk", query_rows, key_rows, preferred_element_type=jnp.float32
-            ) * HD ** (-0.5)
-            logits = jnp.where(key_valid[None, None, :], logits, -jnp.inf)
-            row_max = jnp.max(logits, axis=2, keepdims=True)
-            weights = jnp.exp(logits - row_max)
-            weights = (weights / jnp.sum(weights, axis=2, keepdims=True)).astype(jnp.bfloat16)
-            mixed_rows = jnp.einsum(
-                "hqk,khd->qhd", weights, value_rows, preferred_element_type=jnp.float32
-            ).astype(jnp.bfloat16)
-            return (mixed_rows, jnp.max(row_max))
-
-        mixed_rows, top_logit = lax.map(
-            one_block,
-            full_img[prompt, :, 0].reshape(img_len // block_rows, block_rows, local_heads, HD),
-        )
-        mixed_list.append(mixed_rows.reshape(img_len, local_heads, HD))
-        max_list.append(jnp.max(top_logit))
-    local_max = jnp.stack(max_list)
-    head_rows = jnp.stack(mixed_list)
+    img_flat = full_img.reshape(local_prompts, img_len, 3 * local_heads * HD)
+    txt_flat = full_txt.reshape(local_prompts, txt_len, 2 * local_heads * HD)
+    head_rows, local_max = attention(text_len, img_flat, txt_flat)
+    head_rows = head_rows.reshape(local_prompts, img_len, local_heads, HD)
     token_rows = lax.all_to_all(head_rows, "seq", split_axis=1, concat_axis=2, tiled=True)
     attended = token_rows.reshape(local_prompts * img_dev, HEADS * HD)
     projected = jnp.dot(
@@ -107,8 +144,12 @@
     uncond_vel = jnp.where(is_cond, partner, own_part)
     guided = uncond_vel + guidance[:, None, None] * (cond_vel - uncond_vel)
     square_sum = jnp.sum(guided * guided, axis=(1, 2))
-    total_sq = lax.psum(square_sum, "seq")
-    global_max = lax.pmax(local_max, "seq")
+    stats = jnp.concatenate([square_sum, local_max])
+    gathered = lax.all_to_all(
+        jnp.broadcast_to(stats[None], (seq, stats.shape[0])), "seq", 0, 0, tiled=True
+    )
+    total_sq = jnp.sum(gathered[:, :local_prompts], axis=0)
+    global_max = jnp.max(gathered[:, local_prompts:], axis=0)
     vel_norm = jnp.sqrt(total_sq / (img_len * half_chan) + norm_eps)
     euler_step = sigma_of(t_index + 1) - sigma_of(t_index)
     advanced = latents + euler_step[:, None, None] * guided

time: 550 us -> 371 us (0.67)
  matrix products: 154 us -> 11.9 us
  Pallas kernels: 0 us -> 118 us
  other arithmetic: 108 us -> 2.94 us
  blocking collectives: 73.4 us -> 10.2 us
  waiting for transfers between devices: 121 us -> 132 us
    dot_general x16 -> x0, matrix products: 141 us -> none  [the longest x8 74.3 us: one_block(): jnp.einsum('hqk,khd->qhd', weights, value_rows, preferred_element_type=jn...]
    pallas_call x0 -> x1, Pallas kernels: none -> 118 us  [attention(): pl.pallas_call(attn_kernel, grid_spec=grid_spec, out_shape=[jax.ShapeDtyp...]
    reduce_max x10 -> x2, other arithmetic: 98.3 us -> 0.74 us  [the longest x1 0.63 us: shards(): global_max = jnp.max(gathered[:, local_prompts:], axis=0)]
    psum x1 -> x0, blocking collectives: 37.3 us -> none  [shards(): total_sq = lax.psum(square_sum, 'seq')]
    reshape x0 -> x4, local copies, waits for them, and re-layouts: none -> 36.7 us  [the longest x2 29.7 us: shards(): img_flat = full_img.reshape(local_prompts, img_len, 3 * local_heads * HD)]
    pmax x1 -> x0, blocking collectives: 36.1 us -> none  [shards(): global_max = lax.pmax(local_max, 'seq')]
    another operation x5 -> x0, local copies, waits for them, and re-layouts: 19.6 us -> none  [the longest x1 18.4 us: shards(): head_rows = jnp.stack(mixed_list)]
    all_to_all x1, waiting for transfers between devices: 93.6 us -> 105 us  [shards(): lax.all_to_all(joined, 'seq', split_axis=3, concat_axis=1, tiled=True)]
  transfers between devices with their start and end apart: 5 -> 5, of which waited for: 2 -> 3; matrix products, arithmetic and copies ran while one was open for 55% -> 16% of each run, Pallas kernels for 0% -> 32%
where the time goes in v1:
time: 371 us; the launch traced here: 370 us
  waiting for transfers between devices  132 us (36%)
  Pallas kernels  118 us (32%)
  local copies, waits for them, and re-layouts  60.2 us (16%)
  starting transfers between devices  20 us (5%)
  between operations  14.2 us (4%)
  matrix products  11.9 us (3%)
  blocking collectives  10.2 us (3%)
    pallas_call x1, Pallas kernels, attention(): pl.pallas_call(attn_kernel, grid_spec=grid_spec, out_shape=[jax.ShapeDtyp...  118 us
    all_to_all x1, waiting for transfers between devices, shards(): lax.all_to_all(joined, 'seq', split_axis=3, concat_axis=1, tiled=True)  105 us
    reshape x2, local copies, waits for them, and re-layouts, shards(): img_flat = full_img.reshape(local_prompts, img_len, 3 * local_heads * HD)  29.7 us
    all_to_all x1, waiting for transfers between devices, shards(): lax.all_to_all(head_rows, 'seq', split_axis=1, concat_axis=2, tiled=True)  25.5 us
    dot_general x1, matrix products, shards(): jnp.dot(attended, lax.all_gather(proj_weight, ('cfg', 'req', 'seq'), axis...  10.3 us
    all_to_all x1, blocking collectives, shards(): lax.all_to_all(jnp.broadcast_to(stats[None], (seq, stats.shape[0])), 'seq...  10.2 us
    unnamed x14, local copies, waits for them, and re-layouts  9.89 us
    all_to_all x1, starting transfers between devices, shards(): lax.all_to_all(text_rows, 'seq', split_axis=3, concat_axis=1, tiled=True)  7.88 us
  transfers between devices with their start and end apart: 5, of which 3 were waited for; matrix products, arithmetic and copies ran while one was open for 16% of the time, Pallas kernels for 32%

profile of v1, /device:TPU:8, one launch (start us, length us, event | category | flops | bytes accessed | tf_op | source)
XLA Modules:
  0.0 369.7 jit_solution(3661564294341832901)
XLA Ops:
  7.2 0.0 copy-start
  7.2 0.0 all-gather.2.cloned.1.call-start
  7.2 0.7 all-gather.2.cloned.1.call-update
  7.9 1.1 copy.43
  9.1 1.4 copy.33
  10.4 7.9 %all-to-all-start.1 = ((bf16[2,32,2,16,128]{4,2,1,0,3:T(2,128)(2,1)}), bf16[2,32,2,16,128]{4,2,1,0,3:T(2,128)(2,1)S(1)}, u32[]{:S(2)}, u32[]{:S(2)}) async-start(bf16[2,32,2,16,128]{4,2,1,0,3:T(2,128)(2,1)} %copy.33), calls=%async_computation.1 | async-start | bytes 1048576 | tf_op jit(solution)/shard_map/all_to_all | solution.py:111
  18.3 8.7 %copy.30 = bf16[1,2,256,6144]{2,3,1,0:T(8,128)(2,1)} copy(bf16[1,2,256,6144]{3,2,1,0:T(8,128)(2,1)} %param.10) | data formatting | bytes 12582912 | tf_op args[0]
  27.0 6.2 %copy.31 = bf16[2,256,3,16,128]{1,4,2,0,3:T(8,128)(2,1)} copy(bf16[2,256,3,16,128]{1,4,3,2,0:T(8,128)(2,1)} %bitcast.50) | data formatting | bytes 12582912 | tf_op jit(solution)/shard_map/reshape;squeeze | solution.py:108
  33.2 0.0 all-to-all-done.1
  33.2 7.3 %all-to-all-start = ((bf16[2,256,3,16,128]{1,4,2,0,3:T(8,128)(2,1)}), bf16[2,256,3,16,128]{1,4,2,0,3:T(8,128)(2,1)}, u32[]{:S(2)}, u32[]{:S(2)}) async-start(bf16[2,256,3,16,128]{1,4,2,0,3:T(8,128)(2,1)} %copy.31), calls=%async_computation | async-start | bytes 12582912 | tf_op jit(solution)/shard_map/all_to_all | solution.py:110
  40.5 0.4 copy.34
  41.0 1.1 reshape.67.kt_ref.vt_ref
  42.1 105.1 %all-to-all-done = bf16[2,256,3,16,128]{1,4,2,0,3:T(8,128)(2,1)} async-done(((bf16[2,256,3,16,128]{1,4,2,0,3:T(8,128)(2,1)}), bf16[2,256,3,16,128]{1,4,2,0,3:T(8,128)(2,1)}, u32[]{:S(2)}, u32[]{:S(2)}) %all-to-all-start) | async-done | bytes 6291488 | tf_op jit(solution)/shard_map/all_to_all | solution.py:110
  147.2 13.1 %copy.41 = bf16[2,16,256,3,1,128]{5,3,2,1,0,4:T(4,128)(2,1)} copy(bf16[2,16,256,3,1,128]{2,5,3,0,1,4:T(8,128)(2,1)} %bitcast.5) | data formatting | bytes 12582912 | tf_op jit(solution)/shard_map/reshape | solution.py:115
  160.3 16.6 %reshape.73.q_ref.ki_ref.vi_ref = bf16[2,4096,384]{2,1,0:T(8,128)(2,1)} reshape(bf16[2,16,256,3,1,128]{5,3,2,1,0,4:T(4,128)(2,1)} %copy.41) | data formatting | bytes 12582912 | tf_op jit(solution)/shard_map/reshape | solution.py:115
  176.9 118.0 %shard_map.121 = (bf16[2,4096,128]{2,1,0:T(8,128)(2,1)}, f32[2,8,8,128]{3,2,1,0:T(8,128)}) custom-call(s32[2]{0:T(128)} %tl_ref.1, bf16[2,4096,384]{2,1,0:T(8,128)(2,1)} %reshape.73.q_ref.ki_ref.vi_ref, bf16[2,512,256]{2,1,0:T(8,128)(2,1)} %reshape.67.kt_ref.vt_ref, bf16[2,512,256]{2,1,0:T(8,128)(2,1)} %reshape.67.kt_ref.vt_ref, ...), custom_call_target="tpu_custom_call" | custom-call | flops 19327352832 | bytes 8912896 | tf_op jit(solution)/shard_map/pallas_call | solution.py:76
  294.9 0.0 copy-start.1
  294.9 5.8 %copy.38 = bf16[2,4096,1,128]{3,0,2,1:T(2,128)(2,1)} copy(bf16[2,4096,1,128]{3,1,0,2:T(8,128)(2,1)} %bitcast.53) | data formatting | bytes 4194304 | tf_op jit(solution)/shard_map/reshape | solution.py:118
  300.7 4.7 %all-to-all-start.2 = ((bf16[2,4096,1,128]{3,0,2,1:T(2,128)(2,1)}), bf16[2,4096,1,128]{3,0,2,1:T(2,128)(2,1)S(1)}, u32[]{:S(2)}, u32[]{:S(2)}) async-start(bf16[2,4096,1,128]{3,0,2,1:T(2,128)(2,1)} %copy.38), calls=%async_computation.2 | async-start | bytes 4194304 | tf_op jit(solution)/shard_map/all_to_all | solution.py:119
  305.4 0.0 copy-done.1
  305.5 25.5 %all-to-all-done.2 = bf16[2,4096,1,128]{3,0,2,1:T(2,128)(2,1)S(1)} async-done(((bf16[2,4096,1,128]{3,0,2,1:T(2,128)(2,1)}), bf16[2,4096,1,128]{3,0,2,1:T(2,128)(2,1)S(1)}, u32[]{:S(2)}, u32[]{:S(2)}) %all-to-all-start.2) | async-done | bytes 2097184 | tf_op jit(solution)/shard_map/all_to_all | solution.py:119
  331.0 2.7 copy.45
  333.6 2.8 dot_general.8
  336.5 0.0 all-gather.2.cloned.1.call-done
  336.5 10.3 %fusion.7 = (f32[2,256]{1,0:T(2,128)S(1)}, f32[2,256,3072]{2,1,0:T(8,128)S(1)}) fusion(bf16[2,256,2048]{2,1,0:T(8,128)(2,1)S(1)} %dot_general.8, bf16[2048,3072]{1,0:T(8,128)(2,1)} %all-gather.2.cloned.1.call-done, f32[2,3072]{1,0:T(2,128)S(1)} %get-tuple-element.13, bf16[1,2,256,3072]{3,2,1,0:T(8,128)(2,1)} %param.16), kind=kOutput, calls=%fused_computation.23 | convolution fusion | flops 6448741888 | bytes 24143872 | tf_op jit(solution)/shard_map/dot_general | solution.py:121
  346.8 0.8 multiply_reduce_fusion
  347.6 0.0 copy-done
  347.6 0.0 copy-start.5
  347.6 0.0 copy-start.2
  347.6 0.0 copy-start.3
  347.6 0.0 copy-start.4
  347.6 1.6 fusion.4
  349.2 0.1 collective-permute-start
  349.3 0.0 copy-done.5
  349.4 0.0 copy-done.2
  349.4 0.1 reduce_max.18
  349.5 1.1 collective-permute-done
  350.6 0.0 copy-done.3
  350.6 0.0 copy-done.4
  350.6 0.8 multiply_reduce_fusion.1
  351.4 0.1 pad_maximum_fusion
  351.5 10.2 %all_to_all.54 = f32[16,1,4]{2,1,0:T(1,128)S(1)} all-to-all(f32[16,1,4]{2,1,0:T(1,128)S(1)} %broadcast_in_dim.2), channel_id=1, replica_groups=mesh['cfg'=2,'req'=4,'seq'=16] {'seq'}, dimensions={0} | all-to-all | bytes 512 | tf_op jit(solution)/shard_map/all_to_all | solution.py:148
  361.6 0.1 copy.40
  361.7 0.6 slice_reduce_fusion
  362.4 0.5 sqrt_bitcast_fusion
  (6 shorter events, 0.1 us)
Async XLA Ops:
  7.2 340.4 %copy-start = (bf16[3072,64]{0,1:T(8,128)(2,1)S(1)}, bf16[3072,64]{0,1:T(8,128)(2,1)}, u32[]{:S(2)}) copy-start(bf16[3072,64]{0,1:T(8,128)(2,1)} %param.19) | copy-start | bytes 1179652
  7.2 329.3 %all-gather.2.cloned.1.call-start = ((), (), s32[]{:S(2)}) async-start(), calls=%async_computation.4 | async-start | bytes 12681216 | tf_op jit(solution)/shard_map/all_gather | solution.py:123
  10.4 22.8 %all-to-all-start.1 = ((bf16[2,32,2,16,128]{4,2,1,0,3:T(2,128)(2,1)}), bf16[2,32,2,16,128]{4,2,1,0,3:T(2,128)(2,1)S(1)}, u32[]{:S(2)}, u32[]{:S(2)}) async-start(bf16[2,32,2,16,128]{4,2,1,0,3:T(2,128)(2,1)} %copy.33), calls=%async_computation.1 | async-start | bytes 1048576 | tf_op jit(solution)/shard_map/all_to_all | solution.py:111
  33.2 114.0 %all-to-all-start = ((bf16[2,256,3,16,128]{1,4,2,0,3:T(8,128)(2,1)}), bf16[2,256,3,16,128]{1,4,2,0,3:T(8,128)(2,1)}, u32[]{:S(2)}, u32[]{:S(2)}) async-start(bf16[2,256,3,16,128]{1,4,2,0,3:T(8,128)(2,1)} %copy.31), calls=%async_computation | async-start | bytes 12582912 | tf_op jit(solution)/shard_map/all_to_all | solution.py:110
  294.9 10.6 %copy-start.1 = (f32[1,2,3,3072]{3,1,2,0:T(2,128)S(1)}, f32[1,2,3,3072]{3,1,2,0:T(2,128)}, u32[]{:S(2)}) copy-start(f32[1,2,3,3072]{3,1,2,0:T(2,128)} %param.15) | copy-start | bytes 221188
  300.7 30.3 %all-to-all-start.2 = ((bf16[2,4096,1,128]{3,0,2,1:T(2,128)(2,1)}), bf16[2,4096,1,128]{3,0,2,1:T(2,128)(2,1)S(1)}, u32[]{:S(2)}, u32[]{:S(2)}) async-start(bf16[2,4096,1,128]{3,0,2,1:T(2,128)(2,1)} %copy.38), calls=%async_computation.2 | async-start | bytes 4194304 | tf_op jit(solution)/shard_map/all_to_all | solution.py:119
  347.6 1.8 copy-start.5
  347.6 1.8 copy-start.2
  347.6 3.0 copy-start.3
  347.6 3.0 copy-start.4
  349.2 1.3 collective-permute-start
Sparse Core Ops, SparseCore 0:
  11.1 142.1 all-gather.1

commit v2 on v1

--- a/solution.py
+++ b/solution.py
@@ -30,10 +30,14 @@
 
 def attn_kernel(tl_ref, q_ref, kt_ref, vt_ref, ki_ref, vi_ref, o_ref, m_ref):
     p = pl.program_id(0)
-    q = q_ref[...]
+    q = q_ref[...].reshape(-1, HD)
+    kt = kt_ref[...].reshape(-1, HD)
+    vt = vt_ref[...].reshape(-1, HD)
+    ki = ki_ref[...].reshape(-1, HD)
+    vi = vi_ref[...].reshape(-1, HD)
     dims = (((1,), (1,)), ((), ()))
-    st = lax.dot_general(q, kt_ref[...], dims, preferred_element_type=jnp.float32) * HD ** (-0.5)
-    si = lax.dot_general(q, ki_ref[...], dims, preferred_element_type=jnp.float32) * HD ** (-0.5)
+    st = lax.dot_general(q, kt, dims, preferred_element_type=jnp.float32) * HD ** (-0.5)
+    si = lax.dot_general(q, ki, dims, preferred_element_type=jnp.float32) * HD ** (-0.5)
     col = lax.broadcasted_iota(jnp.int32, st.shape, 1)
     st = jnp.where(col < tl_ref[p], st, -jnp.inf)
     m = jnp.maximum(jnp.max(st, axis=1, keepdims=True), jnp.max(si, axis=1, keepdims=True))
@@ -42,34 +46,36 @@
     inv = 1.0 / (jnp.sum(et, axis=1, keepdims=True) + jnp.sum(ei, axis=1, keepdims=True))
     pt = (et * inv).astype(jnp.bfloat16)
     pi = (ei * inv).astype(jnp.bfloat16)
-    o = jnp.dot(pt, vt_ref[...], preferred_element_type=jnp.float32)
-    o = o + jnp.dot(pi, vi_ref[...], preferred_element_type=jnp.float32)
-    o_ref[...] = o.astype(o_ref.dtype)
+    o = jnp.dot(pt, vt, preferred_element_type=jnp.float32)
+    o = o + jnp.dot(pi, vi, preferred_element_type=jnp.float32)
+    o_ref[...] = o.astype(o_ref.dtype).reshape(o_ref.shape)
     m_ref[...] = jnp.full(m_ref.shape, jnp.max(m), jnp.float32)
 
 
 def attention(text_len, img, txt):
-    prompts, img_len, _ = img.shape
-    txt_len = txt.shape[1]
-    nq = img_len // BQ
+    src, prompts, _, rows, _ = img.shape
+    trows = txt.shape[3]
+    img_len = src * rows
+    txt_len = src * trows
+    per = BQ // rows
+    nq = src // per
     grid_spec = pltpu.PrefetchScalarGridSpec(
         num_scalar_prefetch=1,
         grid=(prompts, nq),
         in_specs=[
-            pl.BlockSpec((None, BQ, HD), lambda p, i, tl: (p, i, 0)),
-            pl.BlockSpec((None, txt_len, HD), lambda p, i, tl: (p, 0, 0)),
-            pl.BlockSpec((None, txt_len, HD), lambda p, i, tl: (p, 0, 1)),
-            pl.BlockSpec((None, img_len, HD), lambda p, i, tl: (p, 0, 1)),
-            pl.BlockSpec((None, img_len, HD), lambda p, i, tl: (p, 0, 2)),
+            pl.BlockSpec((per, None, None, rows, HD), lambda p, i, tl: (i, p, 0, 0, 0)),
+            pl.BlockSpec((src, None, None, trows, HD), lambda p, i, tl: (0, p, 0, 0, 0)),
+            pl.BlockSpec((src, None, None, trows, HD), lambda p, i, tl: (0, p, 1, 0, 0)),
+            pl.BlockSpec((src, None, None, rows, HD), lambda p, i, tl: (0, p, 1, 0, 0)),
+            pl.BlockSpec((src, None, None, rows, HD), lambda p, i, tl: (0, p, 2, 0, 0)),
         ],
         out_specs=[
-            pl.BlockSpec((None, BQ, HD), lambda p, i, tl: (p, i, 0)),
+            pl.BlockSpec((per, None, rows, HD), lambda p, i, tl: (i, p, 0, 0)),
             pl.BlockSpec((None, None, 8, 128), lambda p, i, tl: (p, i, 0, 0)),
         ],
     )
-    flops = 4 * prompts * img_len * (img_len + txt_len) * HD
     cost = pl.CostEstimate(
-        flops=flops,
+        flops=4 * prompts * img_len * (img_len + txt_len) * HD,
         transcendentals=prompts * img_len * (img_len + txt_len),
         bytes_accessed=img.size * 2 + txt.size * 2 + prompts * img_len * HD * 2,
     )
@@ -77,7 +83,7 @@
         attn_kernel,
         grid_spec=grid_spec,
         out_shape=[
-            jax.ShapeDtypeStruct((prompts, img_len, HD), jnp.bfloat16),
+            jax.ShapeDtypeStruct((src, prompts, rows, HD), jnp.bfloat16),
             jax.ShapeDtypeStruct((prompts, nq, 8, 128), jnp.float32),
         ],
         compiler_params=pltpu.CompilerParams(
@@ -105,25 +111,22 @@
     img_dev = img_qkv.shape[2]
     txt_dev = txt_kv.shape[2]
     seq = lax.axis_size("seq")
-    joined = img_qkv[0].reshape(local_prompts, img_dev, 3, HEADS, HD)
-    text_rows = txt_kv[0].reshape(local_prompts, txt_dev, 2, HEADS, HD)
-    full_img = lax.all_to_all(joined, "seq", split_axis=3, concat_axis=1, tiled=True)
-    full_txt = lax.all_to_all(text_rows, "seq", split_axis=3, concat_axis=1, tiled=True)
-    img_len = full_img.shape[1]
-    txt_len = full_txt.shape[1]
-    local_heads = full_img.shape[3]
-    img_flat = full_img.reshape(local_prompts, img_len, 3 * local_heads * HD)
-    txt_flat = full_txt.reshape(local_prompts, txt_len, 2 * local_heads * HD)
-    head_rows, local_max = attention(text_len, img_flat, txt_flat)
-    head_rows = head_rows.reshape(local_prompts, img_len, local_heads, HD)
-    token_rows = lax.all_to_all(head_rows, "seq", split_axis=1, concat_axis=2, tiled=True)
-    attended = token_rows.reshape(local_prompts * img_dev, HEADS * HD)
-    projected = jnp.dot(
-        attended,
-        lax.all_gather(proj_weight, ("cfg", "req", "seq"), axis=0, tiled=True),
+    joined = img_qkv[0].reshape(local_prompts, img_dev, 3, seq, HEADS // seq * HD)
+    joined = joined.transpose(3, 0, 2, 1, 4)
+    text_rows = txt_kv[0].reshape(local_prompts, txt_dev, 2, seq, HEADS // seq * HD)
+    text_rows = text_rows.transpose(3, 0, 2, 1, 4)
+    full_img = lax.all_to_all(joined, "seq", 0, 0, tiled=True)
+    full_txt = lax.all_to_all(text_rows, "seq", 0, 0, tiled=True)
+    img_len = img_dev * seq
+    head_rows, local_max = attention(text_len, full_img, full_txt)
+    token_rows = lax.all_to_all(head_rows, "seq", 0, 0, tiled=True)
+    weight = lax.all_gather(proj_weight, ("cfg", "req", "seq"), axis=0, tiled=True)
+    projected = jnp.einsum(
+        "hptd,hdo->pto",
+        token_rows,
+        weight.reshape(seq, HEADS // seq * HD, weight.shape[1]),
         preferred_element_type=jnp.float32,
     )
-    projected = projected.reshape(local_prompts, img_dev, projected.shape[1])
     mod_rows = modulation[0]
     hidden = img_hidden[0].astype(jnp.float32) + mod_rows[:, 0][:, None, :] * projected
     average = jnp.mean(hidden, axis=2, keepdims=True)

time: 371 us -> 320 us (0.86)
  waiting for transfers between devices: 132 us -> 29.3 us
  blocking collectives: 10.2 us -> 111 us
  local copies, waits for them, and re-layouts: 60.2 us -> 19.7 us
  starting transfers between devices: 20 us -> 11.7 us
    all_to_all x3 -> x2, waiting for transfers between devices: 131 us -> 27.5 us  [the longest x1 27.5 us: shards(): token_rows = lax.all_to_all(head_rows, 'seq', 0, 0, tiled=True)]
    all_to_all x0 -> x1, blocking collectives: none -> 101 us  [shards(): full_img = lax.all_to_all(joined, 'seq', 0, 0, tiled=True)]
    reshape x4 -> x0, local copies, waits for them, and re-layouts: 36.7 us -> none  [the longest x2 29.7 us: shards(): img_flat = full_img.reshape(local_prompts, img_len, 3 * local_heads * HD)]
    all_to_all x3 -> x2, starting transfers between devices: 19.9 us -> 11.6 us  [the longest x1 7.88 us: shards(): full_txt = lax.all_to_all(text_rows, 'seq', 0, 0, tiled=True)]
    unnamed x14 -> x16, local copies, waits for them, and re-layouts: 9.89 us -> 9.88 us
  transfers between devices with their start and end apart: 5 -> 4, of which waited for: 3 -> 2; matrix products, arithmetic and copies ran while one was open for 16% -> 6% of each run, Pallas kernels for 32% -> 37%
where the time goes in v2:
time: 320 us; the launch traced here: 319 us
  Pallas kernels  119 us (37%)
  blocking collectives  111 us (35%)
  waiting for transfers between devices  29.3 us (9%)
  local copies, waits for them, and re-layouts  19.7 us (6%)
  between operations  14.2 us (4%)
  starting transfers between devices  11.7 us (4%)
  matrix products  11.5 us (4%)
    pallas_call x1, Pallas kernels, attention(): pl.pallas_call(attn_kernel, grid_spec=grid_spec, out_shape=[jax.ShapeDtyp...  119 us
    all_to_all x1, blocking collectives, shards(): full_img = lax.all_to_all(joined, 'seq', 0, 0, tiled=True)  101 us
    all_to_all x1, waiting for transfers between devices, shards(): token_rows = lax.all_to_all(head_rows, 'seq', 0, 0, tiled=True)  27.5 us
    all_to_all x1, blocking collectives, shards(): lax.all_to_all(jnp.broadcast_to(stats[None], (seq, stats.shape[0])), 'seq...  10.1 us
    dot_general x1, matrix products, shards(): jnp.einsum('hptd,hdo->pto', token_rows, weight.reshape(seq, HEADS // seq...  9.92 us
    unnamed x16, local copies, waits for them, and re-layouts  9.88 us
    another operation x1, local copies, waits for them, and re-layouts, shards(): img_qkv[0].reshape(local_prompts, img_dev, 3, seq, HEADS // seq * HD)  8.65 us
    all_to_all x1, starting transfers between devices, shards(): full_txt = lax.all_to_all(text_rows, 'seq', 0, 0, tiled=True)  7.88 us
  transfers between devices with their start and end apart: 4, of which 2 were waited for; matrix products, arithmetic and copies ran while one was open for 6% of the time, Pallas kernels for 37%

profile of v2, /device:TPU:8, one launch (start us, length us, event | category | flops | bytes accessed | tf_op | source)
XLA Modules:
  0.0 319.2 jit_solution(2101936347889273590)
XLA Ops:
  7.2 0.0 copy-start
  7.2 0.0 all-gather.2.cloned.1.call-start
  7.2 0.7 all-gather.2.cloned.1.call-update
  7.9 1.1 copy.23
  9.1 1.1 copy.25
  10.1 7.9 %all-to-all-start.1 = ((bf16[16,2,2,32,128]{4,3,2,1,0:T(8,128)(2,1)}), bf16[16,2,2,32,128]{4,3,2,1,0:T(8,128)(2,1)S(1)}, u32[]{:S(2)}, u32[]{:S(2)}) async-start(bf16[16,2,2,32,128]{4,3,2,1,0:T(8,128)(2,1)} %bitcast.37), calls=%async_computation.1 | async-start | bytes 1048576 | tf_op jit(solution)/shard_map/all_to_all | solution.py:119
  18.0 8.7 %copy.18 = bf16[1,2,256,6144]{2,3,1,0:T(8,128)(2,1)} copy(bf16[1,2,256,6144]{3,2,1,0:T(8,128)(2,1)} %param.10) | data formatting | bytes 12582912 | tf_op args[0]
  26.7 8.6 %copy.19 = bf16[2,256,3,16,128]{4,1,2,0,3:T(8,128)(2,1)} copy(bf16[2,256,3,16,128]{1,4,3,2,0:T(8,128)(2,1)} %bitcast.39) | data formatting | bytes 12582912 | tf_op jit(solution)/shard_map/reshape;squeeze | solution.py:114
  35.4 0.0 all-to-all-done.1.kt_ref.vt_ref
  35.4 0.0 copy-start.1
  35.4 101.2 %all_to_all.24.q_ref.ki_ref.vi_ref = bf16[16,2,3,256,128]{4,3,2,1,0:T(8,128)(2,1)} all-to-all(bf16[16,2,3,256,128]{4,3,2,1,0:T(8,128)(2,1)} %bitcast.38), channel_id=1, replica_groups=mesh['cfg'=2,'req'=4,'seq'=16] {'seq'}, dimensions={0} | all-to-all | bytes 12582912 | tf_op jit(solution)/shard_map/all_to_all | solution.py:118
  136.6 0.0 copy-done.1
  136.6 0.0 copy-start.2
  136.6 118.6 %shard_map.121 = (bf16[16,2,256,128]{3,2,1,0:T(8,128)(2,1)}, f32[2,8,8,128]{3,2,1,0:T(8,128)}) custom-call(s32[2]{0:T(128)} %tl_ref.1, bf16[16,2,3,256,128]{4,3,2,1,0:T(8,128)(2,1)} %all_to_all.24.q_ref.ki_ref.vi_ref, bf16[16,2,2,32,128]{4,3,2,1,0:T(8,128)(2,1)} %copy-done.1, bf16[16,2,2,32,128]{4,3,2,1,0:T(8,128)(2,1)} %copy-done.1, ...), custom_call_target="tpu_custom_call" | custom-call | flops 19327352832 | bytes 8912896 | tf_op jit(solution)/shard_map/pallas_call | solution.py:82
  255.2 3.7 %all-to-all-start.2 = ((bf16[16,2,256,128]{3,2,1,0:T(8,128)(2,1)}), bf16[16,2,256,128]{3,2,1,0:T(8,128)(2,1)S(1)}, u32[]{:S(2)}, u32[]{:S(2)}) async-start(bf16[16,2,256,128]{3,2,1,0:T(8,128)(2,1)} %get-tuple-element.5), calls=%async_computation.2 | async-start | bytes 4194304 | tf_op jit(solution)/shard_map/all_to_all | solution.py:122
  258.9 0.0 copy-done.2
  258.9 27.5 %all-to-all-done.2 = bf16[16,2,256,128]{3,2,1,0:T(8,128)(2,1)S(1)} async-done(((bf16[16,2,256,128]{3,2,1,0:T(8,128)(2,1)}), bf16[16,2,256,128]{3,2,1,0:T(8,128)(2,1)S(1)}, u32[]{:S(2)}, u32[]{:S(2)}) %all-to-all-start.2) | async-done | bytes 2097184 | tf_op jit(solution)/shard_map/all_to_all | solution.py:122
  286.4 0.0 all-gather.2.cloned.1.call-done
  286.4 9.9 %fusion.3 = (f32[2,256]{1,0:T(2,128)S(1)}, f32[2,256,3072]{2,1,0:T(8,128)S(1)}) fusion(bf16[16,2,256,128]{3,2,1,0:T(8,128)(2,1)S(1)} %all-to-all-done.2, bf16[16,128,3072,1]{2,1,3,0:T(8,128)(2,1)} %bitcast.45, f32[2,3072]{1,0:T(2,128)S(1)} %get-tuple-element.13, bf16[1,2,256,3072]{3,2,1,0:T(8,128)(2,1)} %param.16), kind=kOutput, calls=%fused_computation.22 | convolution fusion | flops 6448741888 | bytes 24143872 | tf_op jit(solution)/shard_map/hptd,hdo->pto/dot_general | solution.py:124
  296.4 0.8 multiply_reduce_fusion
  297.1 0.0 copy-done
  297.2 0.0 copy-start.6
  297.2 0.0 copy-start.3
  297.2 0.0 copy-start.4
  297.2 0.0 copy-start.5
  297.2 1.6 fusion
  298.8 0.1 collective-permute-start
  298.9 0.0 copy-done.6
  298.9 0.0 copy-done.3
  299.0 0.1 reduce_max.18
  299.1 1.1 collective-permute-done
  300.1 0.0 copy-done.4
  300.2 0.0 copy-done.5
  300.2 0.8 multiply_reduce_fusion.1
  301.0 0.1 pad_maximum_fusion
  301.0 10.1 %all_to_all.25 = f32[16,1,4]{2,1,0:T(1,128)S(1)} all-to-all(f32[16,1,4]{2,1,0:T(1,128)S(1)} %broadcast_in_dim.2), channel_id=1, replica_groups=mesh['cfg'=2,'req'=4,'seq'=16] {'seq'}, dimensions={0} | all-to-all | bytes 512 | tf_op jit(solution)/shard_map/all_to_all | solution.py:151
  311.2 0.1 copy.21
  311.2 0.6 slice_reduce_fusion
  311.9 0.5 sqrt_bitcast_fusion
  (6 shorter events, 0.1 us)
Async XLA Ops:
  7.2 290.0 %copy-start = (bf16[3072,64]{0,1:T(8,128)(2,1)S(1)}, bf16[3072,64]{0,1:T(8,128)(2,1)}, u32[]{:S(2)}) copy-start(bf16[3072,64]{0,1:T(8,128)(2,1)} %param.19) | copy-start | bytes 1179652
  7.2 279.3 %all-gather.2.cloned.1.call-start = ((), (), s32[]{:S(2)}) async-start(), calls=%async_computation.4 | async-start | bytes 12681216 | tf_op jit(solution)/shard_map/all_gather | solution.py:123
  10.1 25.2 %all-to-all-start.1 = ((bf16[16,2,2,32,128]{4,3,2,1,0:T(8,128)(2,1)}), bf16[16,2,2,32,128]{4,3,2,1,0:T(8,128)(2,1)S(1)}, u32[]{:S(2)}, u32[]{:S(2)}) async-start(bf16[16,2,2,32,128]{4,3,2,1,0:T(8,128)(2,1)} %bitcast.37), calls=%async_computation.1 | async-start | bytes 1048576 | tf_op jit(solution)/shard_map/all_to_all | solution.py:119
  35.4 101.2 %copy-start.1 = (bf16[16,2,2,32,128]{4,3,2,1,0:T(8,128)(2,1)}, bf16[16,2,2,32,128]{4,3,2,1,0:T(8,128)(2,1)S(1)}, u32[]{:S(2)}) copy-start(bf16[16,2,2,32,128]{4,3,2,1,0:T(8,128)(2,1)S(1)} %all-to-all-done.1.kt_ref.vt_ref) | copy-start | bytes 1572868
  136.6 122.3 %copy-start.2 = (f32[1,2,3,3072]{3,1,2,0:T(2,128)S(1)}, f32[1,2,3,3072]{3,1,2,0:T(2,128)}, u32[]{:S(2)}) copy-start(f32[1,2,3,3072]{3,1,2,0:T(2,128)} %param.15) | copy-start | bytes 221188
  255.2 31.3 %all-to-all-start.2 = ((bf16[16,2,256,128]{3,2,1,0:T(8,128)(2,1)}), bf16[16,2,256,128]{3,2,1,0:T(8,128)(2,1)S(1)}, u32[]{:S(2)}, u32[]{:S(2)}) async-start(bf16[16,2,256,128]{3,2,1,0:T(8,128)(2,1)} %get-tuple-element.5), calls=%async_computation.2 | async-start | bytes 4194304 | tf_op jit(solution)/shard_map/all_to_all | solution.py:122
  297.2 1.8 copy-start.6
  297.2 1.8 copy-start.3
  297.2 3.0 copy-start.4
  297.2 3.0 copy-start.5
  298.8 1.3 collective-permute-start
Sparse Core Ops, SparseCore 0:
  11.1 124.4 all-gather.1

commit v3 on v2

--- a/solution.py
+++ b/solution.py
@@ -111,15 +111,21 @@
     img_dev = img_qkv.shape[2]
     txt_dev = txt_kv.shape[2]
     seq = lax.axis_size("seq")
-    joined = img_qkv[0].reshape(local_prompts, img_dev, 3, seq, HEADS // seq * HD)
-    joined = joined.transpose(3, 0, 2, 1, 4)
-    text_rows = txt_kv[0].reshape(local_prompts, txt_dev, 2, seq, HEADS // seq * HD)
-    text_rows = text_rows.transpose(3, 0, 2, 1, 4)
-    full_img = lax.all_to_all(joined, "seq", 0, 0, tiled=True)
-    full_txt = lax.all_to_all(text_rows, "seq", 0, 0, tiled=True)
     img_len = img_dev * seq
-    head_rows, local_max = attention(text_len, full_img, full_txt)
-    token_rows = lax.all_to_all(head_rows, "seq", 0, 0, tiled=True)
+    outs = []
+    maxes = []
+    for p in range(local_prompts):
+        joined = img_qkv[0, p].reshape(1, img_dev, 3, seq, HEADS // seq * HD)
+        joined = joined.transpose(3, 0, 2, 1, 4)
+        text_rows = txt_kv[0, p].reshape(1, txt_dev, 2, seq, HEADS // seq * HD)
+        text_rows = text_rows.transpose(3, 0, 2, 1, 4)
+        full_img = lax.all_to_all(joined, "seq", 0, 0, tiled=True)
+        full_txt = lax.all_to_all(text_rows, "seq", 0, 0, tiled=True)
+        head_rows, top = attention(text_len[p : p + 1], full_img, full_txt)
+        outs.append(lax.all_to_all(head_rows, "seq", 0, 0, tiled=True))
+        maxes.append(top)
+    token_rows = jnp.concatenate(outs, axis=1)
+    local_max = jnp.concatenate(maxes)
     weight = lax.all_gather(proj_weight, ("cfg", "req", "seq"), axis=0, tiled=True)
     projected = jnp.einsum(
         "hptd,hdo->pto",

time: 320 us -> 294 us (0.919)
  blocking collectives: 111 us -> 10.4 us
  waiting for transfers between devices: 29.3 us -> 66.5 us
  starting transfers between devices: 11.7 us -> 40.1 us
    all_to_all x1 -> x0, blocking collectives: 101 us -> none  [shards(): full_img = lax.all_to_all(joined, 'seq', 0, 0, tiled=True)]
    all_to_all x1 -> x4, waiting for transfers between devices: 27.5 us -> 58 us  [the longest x2 45.5 us: shards(): full_img = lax.all_to_all(joined, 'seq', 0, 0, tiled=True)]
    all_to_all x1 -> x4, starting transfers between devices: 3.72 us -> 27.9 us  [the longest x2 14.6 us: shards(): outs.append(lax.all_to_all(head_rows, 'seq', 0, 0, tiled=True))]
    all_to_all x1 -> x2, waiting for transfers between devices: 0.01 us -> 7.83 us  [shards(): full_txt = lax.all_to_all(text_rows, 'seq', 0, 0, tiled=True)]
    slice x0 -> x2, local copies, waits for them, and re-layouts: none -> 6.78 us  [the longest x1 6.2 us: shards(): joined = img_qkv[0, p].reshape(1, img_dev, 3, seq, HEADS // seq * HD)]
    all_to_all x1 -> x2, starting transfers between devices: 7.88 us -> 12.1 us  [shards(): full_txt = lax.all_to_all(text_rows, 'seq', 0, 0, tiled=True)]
    pallas_call x1 -> x2, Pallas kernels: 119 us -> 122 us  [attention(): pl.pallas_call(attn_kernel, grid_spec=grid_spec, out_shape=[jax.ShapeDtyp...]
    another operation x2 -> x4, local copies, waits for them, and re-layouts: 9.71 us -> 7.23 us  [the longest x2 5.61 us: shards(): joined = img_qkv[0, p].reshape(1, img_dev, 3, seq, HEADS // seq * HD)]
  transfers between devices with their start and end apart: 4 -> 8, of which waited for: 2 -> 3; matrix products, arithmetic and copies ran while one was open for 6% -> 8% of each run, Pallas kernels for 37% -> 42%
where the time goes in v3:
time: 294 us; the launch traced here: 293 us
  Pallas kernels  122 us (41%)
  waiting for transfers between devices  66.5 us (23%)
  starting transfers between devices  40.1 us (14%)
  local copies, waits for them, and re-layouts  21.7 us (7%)
  between operations  14.3 us (5%)
  matrix products  11.8 us (4%)
  blocking collectives  10.4 us (4%)
  other arithmetic  6.11 us (2%)
    pallas_call x2, Pallas kernels, attention(): pl.pallas_call(attn_kernel, grid_spec=grid_spec, out_shape=[jax.ShapeDtyp...  122 us
    all_to_all x2, waiting for transfers between devices, shards(): full_img = lax.all_to_all(joined, 'seq', 0, 0, tiled=True)  45.5 us
    all_to_all x2, starting transfers between devices, shards(): outs.append(lax.all_to_all(head_rows, 'seq', 0, 0, tiled=True))  14.6 us
    all_to_all x2, starting transfers between devices, shards(): full_img = lax.all_to_all(joined, 'seq', 0, 0, tiled=True)  13.3 us
    all_to_all x2, waiting for transfers between devices, shards(): outs.append(lax.all_to_all(head_rows, 'seq', 0, 0, tiled=True))  12.5 us
    all_to_all x2, starting transfers between devices, shards(): full_txt = lax.all_to_all(text_rows, 'seq', 0, 0, tiled=True)  12.1 us
    all_to_all x1, blocking collectives, shards(): lax.all_to_all(jnp.broadcast_to(stats[None], (seq, stats.shape[0])), 'seq...  10.4 us
    dot_general x1, matrix products, shards(): jnp.einsum('hptd,hdo->pto', token_rows, weight.reshape(seq, HEADS // seq...  10.2 us
  transfers between devices with their start and end apart: 8, of which 3 were waited for; matrix products, arithmetic and copies ran while one was open for 8% of the time, Pallas kernels for 42%

profile of v3, /device:TPU:8, one launch (start us, length us, event | category | flops | bytes accessed | tf_op | source)
XLA Modules:
  0.0 292.7 jit_solution(13401902750173061222)
XLA Ops:
  7.2 0.0 copy-start
  7.2 0.0 all-gather.2.cloned.1.call-start
  7.2 0.7 all-gather.2.cloned.1.call-update
  7.9 1.1 slice_bitcast_fusion.1
  9.0 0.8 copy.36
  9.8 7.9 %all-to-all-start.1 = ((bf16[16,1,2,32,128]{4,3,2,1,0:T(8,128)(2,1)}), bf16[16,1,2,32,128]{4,3,2,1,0:T(8,128)(2,1)S(1)}, u32[]{:S(2)}, u32[]{:S(2)}) async-start(bf16[16,1,2,32,128]{4,3,2,1,0:T(8,128)(2,1)} %bitcast.50), calls=%async_computation.1 | async-start | bytes 524288 | tf_op jit(solution)/shard_map/all_to_all | solution.py:123
  17.8 0.8 copy.35
  18.6 7.8 %all-to-all-done.1.kt_ref.vt_ref = bf16[16,1,2,32,128]{4,3,2,1,0:T(8,128)(2,1)S(1)} async-done(((bf16[16,1,2,32,128]{4,3,2,1,0:T(8,128)(2,1)}), bf16[16,1,2,32,128]{4,3,2,1,0:T(8,128)(2,1)S(1)}, u32[]{:S(2)}, u32[]{:S(2)}) %all-to-all-start.1) | async-done | bytes 262176 | tf_op jit(solution)/shard_map/all_to_all | solution.py:123
  26.4 0.0 copy-start.2
  26.4 4.2 %all-to-all-start.4 = ((bf16[16,1,2,32,128]{4,3,2,1,0:T(8,128)(2,1)}), bf16[16,1,2,32,128]{4,3,2,1,0:T(8,128)(2,1)}, u32[]{:S(2)}, u32[]{:S(2)}) async-start(bf16[16,1,2,32,128]{4,3,2,1,0:T(8,128)(2,1)} %bitcast.49), calls=%async_computation.4 | async-start | bytes 524288 | tf_op jit(solution)/shard_map/all_to_all | solution.py:123
  30.6 6.2 %fusion.7 = (bf16[1,1,256,6144]{3,2,1,0:T(8,128)(2,1)}, bf16[1,1,256,6144]{3,2,1,0:T(8,128)(2,1)}) fusion(bf16[1,2,256,6144]{3,2,1,0:T(8,128)(2,1)} %param.10), kind=kLoop, calls=%fused_computation.29 | loop fusion | bytes 12582912 | tf_op jit(solution)/shard_map/slice | solution.py:118
  36.8 0.0 copy-done.2
  36.8 3.2 %copy.29 = bf16[1,1,256,6144]{2,3,1,0:T(8,128)(2,1)S(1)} copy(bf16[1,1,256,6144]{3,2,1,0:T(8,128)(2,1)} %get-tuple-element.13) | data formatting | bytes 6291456
  40.0 2.8 copy.22
  42.8 0.0 all-to-all-done.4.kt_ref.vt_ref
  42.8 7.1 %all-to-all-start = ((bf16[16,1,3,256,128]{4,3,2,1,0:T(8,128)(2,1)}), bf16[16,1,3,256,128]{4,3,2,1,0:T(8,128)(2,1)}, u32[]{:S(2)}, u32[]{:S(2)}) async-start(bf16[16,1,3,256,128]{4,3,2,1,0:T(8,128)(2,1)} %bitcast.4), calls=%async_computation | async-start | bytes 6291456 | tf_op jit(solution)/shard_map/all_to_all | solution.py:122
  49.9 3.2 %copy.30 = bf16[1,1,256,6144]{2,3,1,0:T(8,128)(2,1)S(1)} copy(bf16[1,1,256,6144]{3,2,1,0:T(8,128)(2,1)} %get-tuple-element.14) | data formatting | bytes 6291456
  53.1 0.0 copy-start.6
  53.1 2.8 copy.25
  56.0 45.5 %all-to-all-done.q_ref.ki_ref.vi_ref = bf16[16,1,3,256,128]{4,3,2,1,0:T(8,128)(2,1)} async-done(((bf16[16,1,3,256,128]{4,3,2,1,0:T(8,128)(2,1)}), bf16[16,1,3,256,128]{4,3,2,1,0:T(8,128)(2,1)}, u32[]{:S(2)}, u32[]{:S(2)}) %all-to-all-start) | async-done | bytes 3145760 | tf_op jit(solution)/shard_map/all_to_all | solution.py:122
  101.4 6.2 %all-to-all-start.3 = ((bf16[16,1,3,256,128]{4,3,2,1,0:T(8,128)(2,1)}), bf16[16,1,3,256,128]{4,3,2,1,0:T(8,128)(2,1)S(1)}, u32[]{:S(2)}, u32[]{:S(2)}) async-start(bf16[16,1,3,256,128]{4,3,2,1,0:T(8,128)(2,1)} %bitcast.7), calls=%async_computation.3 | async-start | bytes 6291456 | tf_op jit(solution)/shard_map/all_to_all | solution.py:122
  107.7 0.0 copy-done.6
  107.7 0.6 fusion.8
  108.2 60.8 %shard_map.121 = (bf16[16,1,256,128]{3,2,1,0:T(8,128)(2,1)}, f32[1,8,8,128]{3,2,1,0:T(8,128)}) custom-call(s32[1]{0:T(128)} %get-tuple-element.22.tl_ref, bf16[16,1,3,256,128]{4,3,2,1,0:T(8,128)(2,1)} %all-to-all-done.q_ref.ki_ref.vi_ref, bf16[16,1,2,32,128]{4,3,2,1,0:T(8,128)(2,1)} %copy-done.2, bf16[16,1,2,32,128]{4,3,2,1,0:T(8,128)(2,1)} %copy-done.2, ...), custom_call_target="tpu_custom_call" | custom-call | flops 9663676416 | bytes 4456448 | tf_op jit(solution)/shard_map/pallas_call | solution.py:82
  169.1 0.0 all-to-all-done.3.q_ref.ki_ref.vi_ref
  169.1 0.0 copy-start.1
  169.1 7.4 %all-to-all-start.2 = ((bf16[16,1,256,128]{3,2,1,0:T(8,128)(2,1)}), bf16[16,1,256,128]{3,2,1,0:T(8,128)(2,1)}, u32[]{:S(2)}, u32[]{:S(2)}) async-start(bf16[16,1,256,128]{3,2,1,0:T(8,128)(2,1)} %get-tuple-element.7), calls=%async_computation.2 | async-start | bytes 2097152 | tf_op jit(solution)/shard_map/all_to_all | solution.py:125
  176.5 0.0 copy-done.1
  176.5 60.8 %shard_map.122 = (bf16[16,1,256,128]{3,2,1,0:T(8,128)(2,1)}, f32[1,8,8,128]{3,2,1,0:T(8,128)}) custom-call(s32[1]{0:T(128)} %get-tuple-element.23.tl_ref, bf16[16,1,3,256,128]{4,3,2,1,0:T(8,128)(2,1)} %copy-done.1, bf16[16,1,2,32,128]{4,3,2,1,0:T(8,128)(2,1)} %all-to-all-done.4.kt_ref.vt_ref, bf16[16,1,2,32,128]{4,3,2,1,0:T(8,128)(2,1)} %all-to-all-done.4.kt_ref.vt_ref, ...), custom_call_target="tpu_custom_call" | custom-call | flops 9663676416 | bytes 4456448 | tf_op jit(solution)/shard_map/pallas_call | solution.py:82
  237.4 0.0 all-to-all-done.2
  237.4 7.2 %all-to-all-start.5 = ((bf16[16,1,256,128]{3,2,1,0:T(8,128)(2,1)}), bf16[16,1,256,128]{3,2,1,0:T(8,128)(2,1)S(1)}, u32[]{:S(2)}, u32[]{:S(2)}) async-start(bf16[16,1,256,128]{3,2,1,0:T(8,128)(2,1)} %get-tuple-element.8), calls=%async_computation.5 | async-start | bytes 2097152 | tf_op jit(solution)/shard_map/all_to_all | solution.py:125
  244.5 0.8 fusion.5
  245.3 12.5 %all-to-all-done.5 = bf16[16,1,256,128]{3,2,1,0:T(8,128)(2,1)S(1)} async-done(((bf16[16,1,256,128]{3,2,1,0:T(8,128)(2,1)}), bf16[16,1,256,128]{3,2,1,0:T(8,128)(2,1)S(1)}, u32[]{:S(2)}, u32[]{:S(2)}) %all-to-all-start.5) | async-done | bytes 1048608 | tf_op jit(solution)/shard_map/all_to_all | solution.py:125
  257.9 0.0 all-gather.2.cloned.1.call-done
  257.9 10.2 %fusion.9 = (f32[2,256]{1,0:T(2,128)S(1)}, f32[2,256,3072]{2,1,0:T(8,128)S(1)}) fusion(bf16[16,128,3072,1]{2,1,3,0:T(8,128)(2,1)} %bitcast.58, bf16[16,1,256,128]{3,2,1,0:T(8,128)(2,1)S(1)} %all-to-all-done.5, bf16[16,1,256,128]{3,2,1,0:T(8,128)(2,1)} %all-to-all-done.2, f32[2,3072]{1,0:T(2,128)S(1)} %get-tuple-element.21, bf16[1,2,256,3072]{3,2,1,0:T(8,128)(2,1)} %param.16), kind=kOutput, calls=%fused_computation.31 | convolution fusion | flops 6449790464 | bytes 24143872 | tf_op jit(solution)/shard_map/hptd,hdo->pto/dot_general | solution.py:130
  268.1 0.8 multiply_reduce_fusion
  268.9 0.0 copy-done
  268.9 0.0 copy-start.8
  268.9 0.0 copy-start.4
  269.0 0.0 copy-start.5
  269.0 0.0 copy-start.3
  269.0 0.0 copy-start.7
  269.0 1.6 fusion
  270.6 0.1 collective-permute-start
  270.7 0.0 copy-done.8
  270.7 0.0 copy-done.4
  270.7 0.6 reduce_max.31
  271.3 0.0 copy-done.5
  271.3 0.6 reduce_max.33
  272.0 0.0 collective-permute-done
  272.0 0.0 copy-done.3
  272.0 0.0 copy-done.7
  272.0 0.8 multiply_reduce_fusion.1
  272.8 1.4 pad_maximum_fusion
  274.1 10.4 %all_to_all.39 = f32[16,1,4]{2,1,0:T(1,128)S(1)} all-to-all(f32[16,1,4]{2,1,0:T(1,128)S(1)} %broadcast_in_dim.2), channel_id=1, replica_groups=mesh['cfg'=2,'req'=4,'seq'=16] {'seq'}, dimensions={0} | all-to-all | bytes 512 | tf_op jit(solution)/shard_map/all_to_all | solution.py:157
  284.6 0.1 copy.27
  284.7 0.6 slice_reduce_fusion
  285.3 0.5 sqrt_bitcast_fusion
  (7 shorter events, 0.1 us)
Async XLA Ops:
  7.2 261.8 %copy-start = (bf16[3072,64]{0,1:T(8,128)(2,1)S(1)}, bf16[3072,64]{0,1:T(8,128)(2,1)}, u32[]{:S(2)}) copy-start(bf16[3072,64]{0,1:T(8,128)(2,1)} %param.19) | copy-start | bytes 1179652
  7.2 250.7 %all-gather.2.cloned.1.call-start = ((), (), s32[]{:S(2)}) async-start(), calls=%async_computation.7 | async-start | bytes 12681216 | tf_op jit(solution)/shard_map/all_gather | solution.py:129
  9.8 16.6 %all-to-all-start.1 = ((bf16[16,1,2,32,128]{4,3,2,1,0:T(8,128)(2,1)}), bf16[16,1,2,32,128]{4,3,2,1,0:T(8,128)(2,1)S(1)}, u32[]{:S(2)}, u32[]{:S(2)}) async-start(bf16[16,1,2,32,128]{4,3,2,1,0:T(8,128)(2,1)} %bitcast.50), calls=%async_computation.1 | async-start | bytes 524288 | tf_op jit(solution)/shard_map/all_to_all | solution.py:123
  26.4 10.4 %copy-start.2 = (bf16[16,1,2,32,128]{4,3,2,1,0:T(8,128)(2,1)}, bf16[16,1,2,32,128]{4,3,2,1,0:T(8,128)(2,1)S(1)}, u32[]{:S(2)}) copy-start(bf16[16,1,2,32,128]{4,3,2,1,0:T(8,128)(2,1)S(1)} %all-to-all-done.1.kt_ref.vt_ref) | copy-start | bytes 786436
  26.4 16.4 %all-to-all-start.4 = ((bf16[16,1,2,32,128]{4,3,2,1,0:T(8,128)(2,1)}), bf16[16,1,2,32,128]{4,3,2,1,0:T(8,128)(2,1)}, u32[]{:S(2)}, u32[]{:S(2)}) async-start(bf16[16,1,2,32,128]{4,3,2,1,0:T(8,128)(2,1)} %bitcast.49), calls=%async_computation.4 | async-start | bytes 524288 | tf_op jit(solution)/shard_map/all_to_all | solution.py:123
  42.8 58.6 %all-to-all-start = ((bf16[16,1,3,256,128]{4,3,2,1,0:T(8,128)(2,1)}), bf16[16,1,3,256,128]{4,3,2,1,0:T(8,128)(2,1)}, u32[]{:S(2)}, u32[]{:S(2)}) async-start(bf16[16,1,3,256,128]{4,3,2,1,0:T(8,128)(2,1)} %bitcast.4), calls=%async_computation | async-start | bytes 6291456 | tf_op jit(solution)/shard_map/all_to_all | solution.py:122
  53.1 54.5 %copy-start.6 = (s32[2]{0:T(128)S(1)}, s32[2]{0:T(128)}, u32[]{:S(2)}) copy-start(s32[2]{0:T(128)} %param.12) | copy-start | bytes 28
  101.4 67.6 %all-to-all-start.3 = ((bf16[16,1,3,256,128]{4,3,2,1,0:T(8,128)(2,1)}), bf16[16,1,3,256,128]{4,3,2,1,0:T(8,128)(2,1)S(1)}, u32[]{:S(2)}, u32[]{:S(2)}) async-start(bf16[16,1,3,256,128]{4,3,2,1,0:T(8,128)(2,1)} %bitcast.7), calls=%async_computation.3 | async-start | bytes 6291456 | tf_op jit(solution)/shard_map/all_to_all | solution.py:122
  169.1 7.4 %copy-start.1 = (bf16[16,1,3,256,128]{4,3,2,1,0:T(8,128)(2,1)}, bf16[16,1,3,256,128]{4,3,2,1,0:T(8,128)(2,1)S(1)}, u32[]{:S(2)}) copy-start(bf16[16,1,3,256,128]{4,3,2,1,0:T(8,128)(2,1)S(1)} %all-to-all-done.3.q_ref.ki_ref.vi_ref) | copy-start | bytes 9437188
  169.1 68.3 %all-to-all-start.2 = ((bf16[16,1,256,128]{3,2,1,0:T(8,128)(2,1)}), bf16[16,1,256,128]{3,2,1,0:T(8,128)(2,1)}, u32[]{:S(2)}, u32[]{:S(2)}) async-start(bf16[16,1,256,128]{3,2,1,0:T(8,128)(2,1)} %get-tuple-element.7), calls=%async_computation.2 | async-start | bytes 2097152 | tf_op jit(solution)/shard_map/all_to_all | solution.py:125
  237.4 20.5 %all-to-all-start.5 = ((bf16[16,1,256,128]{3,2,1,0:T(8,128)(2,1)}), bf16[16,1,256,128]{3,2,1,0:T(8,128)(2,1)S(1)}, u32[]{:S(2)}, u32[]{:S(2)}) async-start(bf16[16,1,256,128]{3,2,1,0:T(8,128)(2,1)} %get-tuple-element.8), calls=%async_computation.5 | async-start | bytes 2097152 | tf_op jit(solution)/shard_map/all_to_all | solution.py:125
  268.9 1.8 copy-start.8
  268.9 1.8 copy-start.4
  269.0 2.4 copy-start.5
  269.0 3.0 %copy-start.3 = (f32[2,256,32]{1,2,0:T(8,128)S(1)}, f32[2,256,32]{1,2,0:T(8,128)}, u32[]{:S(2)}) copy-start(f32[2,256,32]{1,2,0:T(8,128)} %param.17) | copy-start | bytes 196612
  269.0 3.0 %copy-start.7 = (f32[2]{0:T(128)S(1)}, f32[2]{0:T(128)}, u32[]{:S(2)}) copy-start(f32[2]{0:T(128)} %param.14) | copy-start | bytes 28
  270.6 1.4 collective-permute-start
Sparse Core Ops, SparseCore 0:
  11.1 132.0 all-gather.1

commit v4 on v3

--- a/solution.py
+++ b/solution.py
@@ -11,7 +11,7 @@
 HEADS = 16
 HD = 128
 STEPS = 4
-BQ = 512
+BQ = 256
 
 
 time_shift = 1.15

time: 294 us -> 266 us (0.905)
  Pallas kernels: 122 us -> 93.7 us
    pallas_call x2, Pallas kernels: 122 us -> 93.7 us  [attention(): pl.pallas_call(attn_kernel, grid_spec=grid_spec, out_shape=[jax.ShapeDtyp...]
  transfers between devices with their start and end apart: 8 -> 8, of which waited for: 3 -> 3; matrix products, arithmetic and copies ran while one was open for 8% -> 9% of each run, Pallas kernels for 42% -> 35%
where the time goes in v4:
time: 266 us; the launch traced here: 265 us
  Pallas kernels  93.7 us (35%)
  waiting for transfers between devices  66.5 us (25%)
  starting transfers between devices  40.1 us (15%)
  local copies, waits for them, and re-layouts  21.7 us (8%)
  between operations  14.3 us (5%)
  matrix products  11.8 us (4%)
  blocking collectives  10.4 us (4%)
  other arithmetic  6.13 us (2%)
    pallas_call x2, Pallas kernels, attention(): pl.pallas_call(attn_kernel, grid_spec=grid_spec, out_shape=[jax.ShapeDtyp...  93.7 us
    all_to_all x2, waiting for transfers between devices, shards(): full_img = lax.all_to_all(joined, 'seq', 0, 0, tiled=True)  45.5 us
    all_to_all x2, starting transfers between devices, shards(): outs.append(lax.all_to_all(head_rows, 'seq', 0, 0, tiled=True))  14.6 us
    all_to_all x2, starting transfers between devices, shards(): full_img = lax.all_to_all(joined, 'seq', 0, 0, tiled=True)  13.3 us
    all_to_all x2, waiting for transfers between devices, shards(): outs.append(lax.all_to_all(head_rows, 'seq', 0, 0, tiled=True))  12.5 us
    all_to_all x2, starting transfers between devices, shards(): full_txt = lax.all_to_all(text_rows, 'seq', 0, 0, tiled=True)  12.1 us
    all_to_all x1, blocking collectives, shards(): lax.all_to_all(jnp.broadcast_to(stats[None], (seq, stats.shape[0])), 'seq...  10.4 us
    dot_general x1, matrix products, shards(): jnp.einsum('hptd,hdo->pto', token_rows, weight.reshape(seq, HEADS // seq...  10.2 us
  transfers between devices with their start and end apart: 8, of which 3 were waited for; matrix products, arithmetic and copies ran while one was open for 9% of the time, Pallas kernels for 35%

profile of v4, /device:TPU:8, one launch (start us, length us, event | category | flops | bytes accessed | tf_op | source)
XLA Modules:
  0.0 264.7 jit_solution(17458199663561561326)
XLA Ops:
  7.2 0.0 copy-start
  7.2 0.0 all-gather.2.cloned.1.call-start
  7.2 0.7 all-gather.2.cloned.1.call-update
  7.9 1.1 slice_bitcast_fusion.1
  9.0 0.8 copy.36
  9.8 7.9 %all-to-all-start.1 = ((bf16[16,1,2,32,128]{4,3,2,1,0:T(8,128)(2,1)}), bf16[16,1,2,32,128]{4,3,2,1,0:T(8,128)(2,1)S(1)}, u32[]{:S(2)}, u32[]{:S(2)}) async-start(bf16[16,1,2,32,128]{4,3,2,1,0:T(8,128)(2,1)} %bitcast.50), calls=%async_computation.1 | async-start | bytes 524288 | tf_op jit(solution)/shard_map/all_to_all | solution.py:123
  17.8 0.8 copy.35
  18.6 7.8 %all-to-all-done.1.kt_ref.vt_ref = bf16[16,1,2,32,128]{4,3,2,1,0:T(8,128)(2,1)S(1)} async-done(((bf16[16,1,2,32,128]{4,3,2,1,0:T(8,128)(2,1)}), bf16[16,1,2,32,128]{4,3,2,1,0:T(8,128)(2,1)S(1)}, u32[]{:S(2)}, u32[]{:S(2)}) %all-to-all-start.1) | async-done | bytes 262176 | tf_op jit(solution)/shard_map/all_to_all | solution.py:123
  26.4 0.0 copy-start.2
  26.4 4.2 %all-to-all-start.4 = ((bf16[16,1,2,32,128]{4,3,2,1,0:T(8,128)(2,1)}), bf16[16,1,2,32,128]{4,3,2,1,0:T(8,128)(2,1)}, u32[]{:S(2)}, u32[]{:S(2)}) async-start(bf16[16,1,2,32,128]{4,3,2,1,0:T(8,128)(2,1)} %bitcast.49), calls=%async_computation.4 | async-start | bytes 524288 | tf_op jit(solution)/shard_map/all_to_all | solution.py:123
  30.6 6.2 %fusion.7 = (bf16[1,1,256,6144]{3,2,1,0:T(8,128)(2,1)}, bf16[1,1,256,6144]{3,2,1,0:T(8,128)(2,1)}) fusion(bf16[1,2,256,6144]{3,2,1,0:T(8,128)(2,1)} %param.10), kind=kLoop, calls=%fused_computation.29 | loop fusion | bytes 12582912 | tf_op jit(solution)/shard_map/slice | solution.py:118
  36.8 0.0 copy-done.2
  36.8 3.2 %copy.29 = bf16[1,1,256,6144]{2,3,1,0:T(8,128)(2,1)S(1)} copy(bf16[1,1,256,6144]{3,2,1,0:T(8,128)(2,1)} %get-tuple-element.13) | data formatting | bytes 6291456
  40.0 2.8 %copy.22 = bf16[1,256,3,16,128]{4,1,2,0,3:T(8,128)(2,1)} copy(bf16[1,256,3,16,128]{1,4,3,2,0:T(8,128)(2,1)S(1)} %bitcast.51) | data formatting | bytes 6291456 | tf_op jit(solution)/shard_map/reshape;squeeze | solution.py:118
  42.8 0.0 all-to-all-done.4.kt_ref.vt_ref
  42.8 7.1 %all-to-all-start = ((bf16[16,1,3,256,128]{4,3,2,1,0:T(8,128)(2,1)}), bf16[16,1,3,256,128]{4,3,2,1,0:T(8,128)(2,1)}, u32[]{:S(2)}, u32[]{:S(2)}) async-start(bf16[16,1,3,256,128]{4,3,2,1,0:T(8,128)(2,1)} %bitcast.4), calls=%async_computation | async-start | bytes 6291456 | tf_op jit(solution)/shard_map/all_to_all | solution.py:122
  49.9 3.2 %copy.30 = bf16[1,1,256,6144]{2,3,1,0:T(8,128)(2,1)S(1)} copy(bf16[1,1,256,6144]{3,2,1,0:T(8,128)(2,1)} %get-tuple-element.14) | data formatting | bytes 6291456
  53.1 0.0 copy-start.6
  53.1 2.8 %copy.25 = bf16[1,256,3,16,128]{4,1,2,0,3:T(8,128)(2,1)} copy(bf16[1,256,3,16,128]{1,4,3,2,0:T(8,128)(2,1)S(1)} %bitcast.52) | data formatting | bytes 6291456 | tf_op jit(solution)/shard_map/reshape;squeeze | solution.py:118
  56.0 45.5 %all-to-all-done.q_ref.ki_ref.vi_ref = bf16[16,1,3,256,128]{4,3,2,1,0:T(8,128)(2,1)} async-done(((bf16[16,1,3,256,128]{4,3,2,1,0:T(8,128)(2,1)}), bf16[16,1,3,256,128]{4,3,2,1,0:T(8,128)(2,1)}, u32[]{:S(2)}, u32[]{:S(2)}) %all-to-all-start) | async-done | bytes 3145760 | tf_op jit(solution)/shard_map/all_to_all | solution.py:122
  101.4 6.2 %all-to-all-start.3 = ((bf16[16,1,3,256,128]{4,3,2,1,0:T(8,128)(2,1)}), bf16[16,1,3,256,128]{4,3,2,1,0:T(8,128)(2,1)S(1)}, u32[]{:S(2)}, u32[]{:S(2)}) async-start(bf16[16,1,3,256,128]{4,3,2,1,0:T(8,128)(2,1)} %bitcast.7), calls=%async_computation.3 | async-start | bytes 6291456 | tf_op jit(solution)/shard_map/all_to_all | solution.py:122
  107.7 0.0 copy-done.6
  107.7 0.6 fusion.8
  108.2 46.9 %shard_map.121 = (bf16[16,1,256,128]{3,2,1,0:T(8,128)(2,1)}, f32[1,16,8,128]{3,2,1,0:T(8,128)}) custom-call(s32[1]{0:T(128)} %get-tuple-element.22.tl_ref, bf16[16,1,3,256,128]{4,3,2,1,0:T(8,128)(2,1)} %all-to-all-done.q_ref.ki_ref.vi_ref, bf16[16,1,2,32,128]{4,3,2,1,0:T(8,128)(2,1)} %copy-done.2, bf16[16,1,2,32,128]{4,3,2,1,0:T(8,128)(2,1)} %copy-done.2, ...), custom_call_target="tpu_custom_call" | custom-call | flops 9663676416 | bytes 4456448 | tf_op jit(solution)/shard_map/pallas_call | solution.py:82
  155.1 0.0 all-to-all-done.3.q_ref.ki_ref.vi_ref
  155.1 0.0 copy-start.1
  155.2 7.3 %all-to-all-start.2 = ((bf16[16,1,256,128]{3,2,1,0:T(8,128)(2,1)}), bf16[16,1,256,128]{3,2,1,0:T(8,128)(2,1)}, u32[]{:S(2)}, u32[]{:S(2)}) async-start(bf16[16,1,256,128]{3,2,1,0:T(8,128)(2,1)} %get-tuple-element.7), calls=%async_computation.2 | async-start | bytes 2097152 | tf_op jit(solution)/shard_map/all_to_all | solution.py:125
  162.4 0.0 copy-done.1
  162.4 46.8 %shard_map.122 = (bf16[16,1,256,128]{3,2,1,0:T(8,128)(2,1)}, f32[1,16,8,128]{3,2,1,0:T(8,128)}) custom-call(s32[1]{0:T(128)} %get-tuple-element.23.tl_ref, bf16[16,1,3,256,128]{4,3,2,1,0:T(8,128)(2,1)} %copy-done.1, bf16[16,1,2,32,128]{4,3,2,1,0:T(8,128)(2,1)} %all-to-all-done.4.kt_ref.vt_ref, bf16[16,1,2,32,128]{4,3,2,1,0:T(8,128)(2,1)} %all-to-all-done.4.kt_ref.vt_ref, ...), custom_call_target="tpu_custom_call" | custom-call | flops 9663676416 | bytes 4456448 | tf_op jit(solution)/shard_map/pallas_call | solution.py:82
  209.2 0.0 all-to-all-done.2
  209.2 7.3 %all-to-all-start.5 = ((bf16[16,1,256,128]{3,2,1,0:T(8,128)(2,1)}), bf16[16,1,256,128]{3,2,1,0:T(8,128)(2,1)S(1)}, u32[]{:S(2)}, u32[]{:S(2)}) async-start(bf16[16,1,256,128]{3,2,1,0:T(8,128)(2,1)} %get-tuple-element.8), calls=%async_computation.5 | async-start | bytes 2097152 | tf_op jit(solution)/shard_map/all_to_all | solution.py:125
  216.6 0.8 fusion.5
  217.3 12.5 %all-to-all-done.5 = bf16[16,1,256,128]{3,2,1,0:T(8,128)(2,1)S(1)} async-done(((bf16[16,1,256,128]{3,2,1,0:T(8,128)(2,1)}), bf16[16,1,256,128]{3,2,1,0:T(8,128)(2,1)S(1)}, u32[]{:S(2)}, u32[]{:S(2)}) %all-to-all-start.5) | async-done | bytes 1048608 | tf_op jit(solution)/shard_map/all_to_all | solution.py:125
  229.9 0.0 all-gather.2.cloned.1.call-done
  229.9 10.2 %fusion.9 = (f32[2,256]{1,0:T(2,128)S(1)}, f32[2,256,3072]{2,1,0:T(8,128)S(1)}) fusion(bf16[16,128,3072,1]{2,1,3,0:T(8,128)(2,1)} %bitcast.58, bf16[16,1,256,128]{3,2,1,0:T(8,128)(2,1)S(1)} %all-to-all-done.5, bf16[16,1,256,128]{3,2,1,0:T(8,128)(2,1)} %all-to-all-done.2, f32[2,3072]{1,0:T(2,128)S(1)} %get-tuple-element.21, bf16[1,2,256,3072]{3,2,1,0:T(8,128)(2,1)} %param.16), kind=kOutput, calls=%fused_computation.31 | convolution fusion | flops 6449790464 | bytes 24143872 | tf_op jit(solution)/shard_map/hptd,hdo->pto/dot_general | solution.py:130
  240.1 0.8 multiply_reduce_fusion
  240.9 0.0 copy-done
  240.9 0.0 copy-start.8
  240.9 0.0 copy-start.3
  241.0 0.0 copy-start.4
  241.0 0.0 copy-start.5
  241.0 0.0 copy-start.7
  241.0 1.6 fusion
  242.6 0.1 collective-permute-start
  242.7 0.0 copy-done.8
  242.7 0.0 copy-done.3
  242.7 0.6 reduce_max.31
  243.4 0.0 copy-done.4
  243.4 0.6 reduce_max.33
  244.0 0.0 collective-permute-done
  244.0 0.0 copy-done.5
  244.0 0.0 copy-done.7
  244.0 0.8 multiply_reduce_fusion.1
  244.8 1.4 pad_maximum_fusion
  246.2 10.4 %all_to_all.39 = f32[16,1,4]{2,1,0:T(1,128)S(1)} all-to-all(f32[16,1,4]{2,1,0:T(1,128)S(1)} %broadcast_in_dim.2), channel_id=1, replica_groups=mesh['cfg'=2,'req'=4,'seq'=16] {'seq'}, dimensions={0} | all-to-all | bytes 512 | tf_op jit(solution)/shard_map/all_to_all | solution.py:157
  256.6 0.1 copy.27
  256.7 0.6 slice_reduce_fusion
  257.3 0.5 sqrt_bitcast_fusion
  (7 shorter events, 0.1 us)
Async XLA Ops:
  7.2 233.8 %copy-start = (bf16[3072,64]{0,1:T(8,128)(2,1)S(1)}, bf16[3072,64]{0,1:T(8,128)(2,1)}, u32[]{:S(2)}) copy-start(bf16[3072,64]{0,1:T(8,128)(2,1)} %param.19) | copy-start | bytes 1179652
  7.2 222.7 %all-gather.2.cloned.1.call-start = ((), (), s32[]{:S(2)}) async-start(), calls=%async_computation.7 | async-start | bytes 12681216 | tf_op jit(solution)/shard_map/all_gather | solution.py:129
  9.8 16.6 %all-to-all-start.1 = ((bf16[16,1,2,32,128]{4,3,2,1,0:T(8,128)(2,1)}), bf16[16,1,2,32,128]{4,3,2,1,0:T(8,128)(2,1)S(1)}, u32[]{:S(2)}, u32[]{:S(2)}) async-start(bf16[16,1,2,32,128]{4,3,2,1,0:T(8,128)(2,1)} %bitcast.50), calls=%async_computation.1 | async-start | bytes 524288 | tf_op jit(solution)/shard_map/all_to_all | solution.py:123
  26.4 10.4 %copy-start.2 = (bf16[16,1,2,32,128]{4,3,2,1,0:T(8,128)(2,1)}, bf16[16,1,2,32,128]{4,3,2,1,0:T(8,128)(2,1)S(1)}, u32[]{:S(2)}) copy-start(bf16[16,1,2,32,128]{4,3,2,1,0:T(8,128)(2,1)S(1)} %all-to-all-done.1.kt_ref.vt_ref) | copy-start | bytes 786436
  26.4 16.4 %all-to-all-start.4 = ((bf16[16,1,2,32,128]{4,3,2,1,0:T(8,128)(2,1)}), bf16[16,1,2,32,128]{4,3,2,1,0:T(8,128)(2,1)}, u32[]{:S(2)}, u32[]{:S(2)}) async-start(bf16[16,1,2,32,128]{4,3,2,1,0:T(8,128)(2,1)} %bitcast.49), calls=%async_computation.4 | async-start | bytes 524288 | tf_op jit(solution)/shard_map/all_to_all | solution.py:123
  42.8 58.6 %all-to-all-start = ((bf16[16,1,3,256,128]{4,3,2,1,0:T(8,128)(2,1)}), bf16[16,1,3,256,128]{4,3,2,1,0:T(8,128)(2,1)}, u32[]{:S(2)}, u32[]{:S(2)}) async-start(bf16[16,1,3,256,128]{4,3,2,1,0:T(8,128)(2,1)} %bitcast.4), calls=%async_computation | async-start | bytes 6291456 | tf_op jit(solution)/shard_map/all_to_all | solution.py:122
  53.1 54.5 %copy-start.6 = (s32[2]{0:T(128)S(1)}, s32[2]{0:T(128)}, u32[]{:S(2)}) copy-start(s32[2]{0:T(128)} %param.12) | copy-start | bytes 28
  101.4 53.7 %all-to-all-start.3 = ((bf16[16,1,3,256,128]{4,3,2,1,0:T(8,128)(2,1)}), bf16[16,1,3,256,128]{4,3,2,1,0:T(8,128)(2,1)S(1)}, u32[]{:S(2)}, u32[]{:S(2)}) async-start(bf16[16,1,3,256,128]{4,3,2,1,0:T(8,128)(2,1)} %bitcast.7), calls=%async_computation.3 | async-start | bytes 6291456 | tf_op jit(solution)/shard_map/all_to_all | solution.py:122
  155.1 7.3 %copy-start.1 = (bf16[16,1,3,256,128]{4,3,2,1,0:T(8,128)(2,1)}, bf16[16,1,3,256,128]{4,3,2,1,0:T(8,128)(2,1)S(1)}, u32[]{:S(2)}) copy-start(bf16[16,1,3,256,128]{4,3,2,1,0:T(8,128)(2,1)S(1)} %all-to-all-done.3.q_ref.ki_ref.vi_ref) | copy-start | bytes 9437188
  155.2 54.1 %all-to-all-start.2 = ((bf16[16,1,256,128]{3,2,1,0:T(8,128)(2,1)}), bf16[16,1,256,128]{3,2,1,0:T(8,128)(2,1)}, u32[]{:S(2)}, u32[]{:S(2)}) async-start(bf16[16,1,256,128]{3,2,1,0:T(8,128)(2,1)} %get-tuple-element.7), calls=%async_computation.2 | async-start | bytes 2097152 | tf_op jit(solution)/shard_map/all_to_all | solution.py:125
  209.2 20.7 %all-to-all-start.5 = ((bf16[16,1,256,128]{3,2,1,0:T(8,128)(2,1)}), bf16[16,1,256,128]{3,2,1,0:T(8,128)(2,1)S(1)}, u32[]{:S(2)}, u32[]{:S(2)}) async-start(bf16[16,1,256,128]{3,2,1,0:T(8,128)(2,1)} %get-tuple-element.8), calls=%async_computation.5 | async-start | bytes 2097152 | tf_op jit(solution)/shard_map/all_to_all | solution.py:125
  240.9 1.8 copy-start.8
  240.9 1.8 copy-start.3
  241.0 2.4 copy-start.4
  241.0 3.0 %copy-start.5 = (f32[2,256,32]{1,2,0:T(8,128)S(1)}, f32[2,256,32]{1,2,0:T(8,128)}, u32[]{:S(2)}) copy-start(f32[2,256,32]{1,2,0:T(8,128)} %param.17) | copy-start | bytes 196612
  241.0 3.0 %copy-start.7 = (f32[2]{0:T(128)S(1)}, f32[2]{0:T(128)}, u32[]{:S(2)}) copy-start(f32[2]{0:T(128)} %param.14) | copy-start | bytes 28
  242.6 1.4 collective-permute-start
Sparse Core Ops, SparseCore 0:
  11.1 132.0 all-gather.1

commit v5 on v4

--- a/solution.py
+++ b/solution.py
@@ -11,7 +11,8 @@
 HEADS = 16
 HD = 128
 STEPS = 4
-BQ = 256
+BQ = 1024
+CK = 512
 
 
 time_shift = 1.15
@@ -30,24 +31,30 @@
 
 def attn_kernel(tl_ref, q_ref, kt_ref, vt_ref, ki_ref, vi_ref, o_ref, m_ref):
     p = pl.program_id(0)
+    dims = (((1,), (1,)), ((), ()))
     q = q_ref[...].reshape(-1, HD)
-    kt = kt_ref[...].reshape(-1, HD)
-    vt = vt_ref[...].reshape(-1, HD)
-    ki = ki_ref[...].reshape(-1, HD)
-    vi = vi_ref[...].reshape(-1, HD)
-    dims = (((1,), (1,)), ((), ()))
-    st = lax.dot_general(q, kt, dims, preferred_element_type=jnp.float32) * HD ** (-0.5)
-    si = lax.dot_general(q, ki, dims, preferred_element_type=jnp.float32) * HD ** (-0.5)
+    st = lax.dot_general(q, kt_ref[...].reshape(-1, HD), dims, preferred_element_type=jnp.float32)
+    st = st * HD ** (-0.5)
     col = lax.broadcasted_iota(jnp.int32, st.shape, 1)
     st = jnp.where(col < tl_ref[p], st, -jnp.inf)
-    m = jnp.maximum(jnp.max(st, axis=1, keepdims=True), jnp.max(si, axis=1, keepdims=True))
-    et = jnp.exp(st - m)
-    ei = jnp.exp(si - m)
-    inv = 1.0 / (jnp.sum(et, axis=1, keepdims=True) + jnp.sum(ei, axis=1, keepdims=True))
-    pt = (et * inv).astype(jnp.bfloat16)
-    pi = (ei * inv).astype(jnp.bfloat16)
-    o = jnp.dot(pt, vt, preferred_element_type=jnp.float32)
-    o = o + jnp.dot(pi, vi, preferred_element_type=jnp.float32)
+    m = jnp.max(st, axis=1, keepdims=True)
+    e = jnp.exp(st - m)
+    l = jnp.sum(e, axis=1, keepdims=True)
+    acc = jnp.dot(
+        e.astype(jnp.bfloat16), vt_ref[...].reshape(-1, HD), preferred_element_type=jnp.float32
+    )
+    per = CK // ki_ref.shape[1]
+    for c in range(ki_ref.shape[0] // per):
+        k = ki_ref[c * per : (c + 1) * per].reshape(-1, HD)
+        v = vi_ref[c * per : (c + 1) * per].reshape(-1, HD)
+        s = lax.dot_general(q, k, dims, preferred_element_type=jnp.float32) * HD ** (-0.5)
+        m_new = jnp.maximum(m, jnp.max(s, axis=1, keepdims=True))
+        alpha = jnp.exp(m - m_new)
+        e = jnp.exp(s - m_new)
+        l = alpha * l + jnp.sum(e, axis=1, keepdims=True)
+        acc = alpha * acc + jnp.dot(e.astype(jnp.bfloat16), v, preferred_element_type=jnp.float32)
+        m = m_new
+    o = acc * (1.0 / l)
     o_ref[...] = o.astype(o_ref.dtype).reshape(o_ref.shape)
     m_ref[...] = jnp.full(m_ref.shape, jnp.max(m), jnp.float32)
 

time: 266 us -> 252 us (0.947)
  Pallas kernels: 93.7 us -> 68.3 us
  waiting for transfers between devices: 66.5 us -> 80.4 us
  starting transfers between devices: 40.1 us -> 37 us
    pallas_call x2, Pallas kernels: 93.7 us -> 68.3 us  [attention(): pl.pallas_call(attn_kernel, grid_spec=grid_spec, out_shape=[jax.ShapeDtyp...]
    all_to_all x2, waiting for transfers between devices: 45.5 us -> 57.1 us  [shards(): full_img = lax.all_to_all(joined, 'seq', 0, 0, tiled=True)]
    all_to_all x2, starting transfers between devices: 14.6 us -> 11.4 us  [shards(): outs.append(lax.all_to_all(head_rows, 'seq', 0, 0, tiled=True))]
  transfers between devices with their start and end apart: 8 -> 8, of which waited for: 3 -> 4; matrix products, arithmetic and copies ran while one was open for 9% -> 9% of each run, Pallas kernels for 35% -> 27%
where the time goes in v5:
time: 252 us; the launch traced here: 250 us
  waiting for transfers between devices  80.4 us (32%)
  Pallas kernels  68.3 us (27%)
  starting transfers between devices  37 us (15%)
  local copies, waits for them, and re-layouts  21.7 us (9%)
  between operations  14.3 us (6%)
  matrix products  11.8 us (5%)
  blocking collectives  10.6 us (4%)
  other arithmetic  6.11 us (2%)
    pallas_call x2, Pallas kernels, attention(): pl.pallas_call(attn_kernel, grid_spec=grid_spec, out_shape=[jax.ShapeDtyp...  68.3 us
    all_to_all x2, waiting for transfers between devices, shards(): full_img = lax.all_to_all(joined, 'seq', 0, 0, tiled=True)  57.1 us
    all_to_all x2, waiting for transfers between devices, shards(): outs.append(lax.all_to_all(head_rows, 'seq', 0, 0, tiled=True))  14.8 us
    all_to_all x2, starting transfers between devices, shards(): full_img = lax.all_to_all(joined, 'seq', 0, 0, tiled=True)  13.3 us
    all_to_all x2, starting transfers between devices, shards(): full_txt = lax.all_to_all(text_rows, 'seq', 0, 0, tiled=True)  12.1 us
    all_to_all x2, starting transfers between devices, shards(): outs.append(lax.all_to_all(head_rows, 'seq', 0, 0, tiled=True))  11.4 us
    all_to_all x1, blocking collectives, shards(): lax.all_to_all(jnp.broadcast_to(stats[None], (seq, stats.shape[0])), 'seq...  10.6 us
    dot_general x1, matrix products, shards(): jnp.einsum('hptd,hdo->pto', token_rows, weight.reshape(seq, HEADS // seq...  10.2 us
  transfers between devices with their start and end apart: 8, of which 4 were waited for; matrix products, arithmetic and copies ran while one was open for 9% of the time, Pallas kernels for 27%

profile of v5, /device:TPU:8, one launch (start us, length us, event | category | flops | bytes accessed | tf_op | source)
XLA Modules:
  0.0 250.2 jit_solution(665151088768316125)
XLA Ops:
  7.2 0.0 copy-start
  7.2 0.0 all-gather.2.cloned.1.call-start
  7.2 0.7 all-gather.2.cloned.1.call-update
  7.9 1.1 slice_bitcast_fusion.1
  9.0 0.8 copy.36
  9.8 7.9 %all-to-all-start.1 = ((bf16[16,1,2,32,128]{4,3,2,1,0:T(8,128)(2,1)}), bf16[16,1,2,32,128]{4,3,2,1,0:T(8,128)(2,1)S(1)}, u32[]{:S(2)}, u32[]{:S(2)}) async-start(bf16[16,1,2,32,128]{4,3,2,1,0:T(8,128)(2,1)} %bitcast.50), calls=%async_computation.1 | async-start | bytes 524288 | tf_op jit(solution)/shard_map/all_to_all | solution.py:130
  17.8 0.8 copy.35
  18.6 7.8 %all-to-all-done.1.kt_ref.vt_ref = bf16[16,1,2,32,128]{4,3,2,1,0:T(8,128)(2,1)S(1)} async-done(((bf16[16,1,2,32,128]{4,3,2,1,0:T(8,128)(2,1)}), bf16[16,1,2,32,128]{4,3,2,1,0:T(8,128)(2,1)S(1)}, u32[]{:S(2)}, u32[]{:S(2)}) %all-to-all-start.1) | async-done | bytes 262176 | tf_op jit(solution)/shard_map/all_to_all | solution.py:130
  26.4 0.0 copy-start.2
  26.4 4.2 %all-to-all-start.4 = ((bf16[16,1,2,32,128]{4,3,2,1,0:T(8,128)(2,1)}), bf16[16,1,2,32,128]{4,3,2,1,0:T(8,128)(2,1)}, u32[]{:S(2)}, u32[]{:S(2)}) async-start(bf16[16,1,2,32,128]{4,3,2,1,0:T(8,128)(2,1)} %bitcast.49), calls=%async_computation.4 | async-start | bytes 524288 | tf_op jit(solution)/shard_map/all_to_all | solution.py:130
  30.6 6.2 %fusion.7 = (bf16[1,1,256,6144]{3,2,1,0:T(8,128)(2,1)}, bf16[1,1,256,6144]{3,2,1,0:T(8,128)(2,1)}) fusion(bf16[1,2,256,6144]{3,2,1,0:T(8,128)(2,1)} %param.10), kind=kLoop, calls=%fused_computation.29 | loop fusion | bytes 12582912 | tf_op jit(solution)/shard_map/slice | solution.py:125
  36.8 0.0 copy-done.2
  36.8 3.2 %copy.29 = bf16[1,1,256,6144]{2,3,1,0:T(8,128)(2,1)S(1)} copy(bf16[1,1,256,6144]{3,2,1,0:T(8,128)(2,1)} %get-tuple-element.13) | data formatting | bytes 6291456
  40.0 2.8 %copy.22 = bf16[1,256,3,16,128]{4,1,2,0,3:T(8,128)(2,1)} copy(bf16[1,256,3,16,128]{1,4,3,2,0:T(8,128)(2,1)S(1)} %bitcast.51) | data formatting | bytes 6291456 | tf_op jit(solution)/shard_map/reshape;squeeze | solution.py:125
  42.8 0.0 all-to-all-done.4.kt_ref.vt_ref
  42.8 7.1 %all-to-all-start = ((bf16[16,1,3,256,128]{4,3,2,1,0:T(8,128)(2,1)}), bf16[16,1,3,256,128]{4,3,2,1,0:T(8,128)(2,1)}, u32[]{:S(2)}, u32[]{:S(2)}) async-start(bf16[16,1,3,256,128]{4,3,2,1,0:T(8,128)(2,1)} %bitcast.4), calls=%async_computation | async-start | bytes 6291456 | tf_op jit(solution)/shard_map/all_to_all | solution.py:129
  49.9 3.2 %copy.30 = bf16[1,1,256,6144]{2,3,1,0:T(8,128)(2,1)S(1)} copy(bf16[1,1,256,6144]{3,2,1,0:T(8,128)(2,1)} %get-tuple-element.14) | data formatting | bytes 6291456
  53.1 0.0 copy-start.6
  53.1 2.8 %copy.25 = bf16[1,256,3,16,128]{4,1,2,0,3:T(8,128)(2,1)} copy(bf16[1,256,3,16,128]{1,4,3,2,0:T(8,128)(2,1)S(1)} %bitcast.52) | data formatting | bytes 6291456 | tf_op jit(solution)/shard_map/reshape;squeeze | solution.py:125
  56.0 45.5 %all-to-all-done.q_ref.ki_ref.vi_ref = bf16[16,1,3,256,128]{4,3,2,1,0:T(8,128)(2,1)} async-done(((bf16[16,1,3,256,128]{4,3,2,1,0:T(8,128)(2,1)}), bf16[16,1,3,256,128]{4,3,2,1,0:T(8,128)(2,1)}, u32[]{:S(2)}, u32[]{:S(2)}) %all-to-all-start) | async-done | bytes 3145760 | tf_op jit(solution)/shard_map/all_to_all | solution.py:129
  101.4 6.2 %all-to-all-start.3 = ((bf16[16,1,3,256,128]{4,3,2,1,0:T(8,128)(2,1)}), bf16[16,1,3,256,128]{4,3,2,1,0:T(8,128)(2,1)S(1)}, u32[]{:S(2)}, u32[]{:S(2)}) async-start(bf16[16,1,3,256,128]{4,3,2,1,0:T(8,128)(2,1)} %bitcast.7), calls=%async_computation.3 | async-start | bytes 6291456 | tf_op jit(solution)/shard_map/all_to_all | solution.py:129
  107.7 0.0 copy-done.6
  107.7 0.6 fusion.8
  108.2 34.2 %shard_map.121 = (bf16[16,1,256,128]{3,2,1,0:T(8,128)(2,1)}, f32[1,4,8,128]{3,2,1,0:T(8,128)}) custom-call(s32[1]{0:T(128)} %get-tuple-element.22.tl_ref, bf16[16,1,3,256,128]{4,3,2,1,0:T(8,128)(2,1)} %all-to-all-done.q_ref.ki_ref.vi_ref, bf16[16,1,2,32,128]{4,3,2,1,0:T(8,128)(2,1)} %copy-done.2, bf16[16,1,2,32,128]{4,3,2,1,0:T(8,128)(2,1)} %copy-done.2, ...), custom_call_target="tpu_custom_call" | custom-call | flops 9663676416 | bytes 4456448 | tf_op jit(solution)/shard_map/pallas_call | solution.py:89
  142.4 11.6 %all-to-all-done.3.q_ref.ki_ref.vi_ref = bf16[16,1,3,256,128]{4,3,2,1,0:T(8,128)(2,1)S(1)} async-done(((bf16[16,1,3,256,128]{4,3,2,1,0:T(8,128)(2,1)}), bf16[16,1,3,256,128]{4,3,2,1,0:T(8,128)(2,1)S(1)}, u32[]{:S(2)}, u32[]{:S(2)}) %all-to-all-start.3) | async-done | bytes 3145760 | tf_op jit(solution)/shard_map/all_to_all | solution.py:129
  154.0 0.0 copy-start.1
  154.0 4.5 %all-to-all-start.2 = ((bf16[16,1,256,128]{3,2,1,0:T(8,128)(2,1)}), bf16[16,1,256,128]{3,2,1,0:T(8,128)(2,1)}, u32[]{:S(2)}, u32[]{:S(2)}) async-start(bf16[16,1,256,128]{3,2,1,0:T(8,128)(2,1)} %get-tuple-element.7), calls=%async_computation.2 | async-start | bytes 2097152 | tf_op jit(solution)/shard_map/all_to_all | solution.py:132
  158.6 0.0 copy-done.1
  158.6 34.1 %shard_map.122 = (bf16[16,1,256,128]{3,2,1,0:T(8,128)(2,1)}, f32[1,4,8,128]{3,2,1,0:T(8,128)}) custom-call(s32[1]{0:T(128)} %get-tuple-element.23.tl_ref, bf16[16,1,3,256,128]{4,3,2,1,0:T(8,128)(2,1)} %copy-done.1, bf16[16,1,2,32,128]{4,3,2,1,0:T(8,128)(2,1)} %all-to-all-done.4.kt_ref.vt_ref, bf16[16,1,2,32,128]{4,3,2,1,0:T(8,128)(2,1)} %all-to-all-done.4.kt_ref.vt_ref, ...), custom_call_target="tpu_custom_call" | custom-call | flops 9663676416 | bytes 4456448 | tf_op jit(solution)/shard_map/pallas_call | solution.py:89
  192.7 0.0 all-to-all-done.2
  192.7 6.9 %all-to-all-start.5 = ((bf16[16,1,256,128]{3,2,1,0:T(8,128)(2,1)}), bf16[16,1,256,128]{3,2,1,0:T(8,128)(2,1)S(1)}, u32[]{:S(2)}, u32[]{:S(2)}) async-start(bf16[16,1,256,128]{3,2,1,0:T(8,128)(2,1)} %get-tuple-element.8), calls=%async_computation.5 | async-start | bytes 2097152 | tf_op jit(solution)/shard_map/all_to_all | solution.py:132
  199.7 0.8 fusion.5
  200.5 14.8 %all-to-all-done.5 = bf16[16,1,256,128]{3,2,1,0:T(8,128)(2,1)S(1)} async-done(((bf16[16,1,256,128]{3,2,1,0:T(8,128)(2,1)}), bf16[16,1,256,128]{3,2,1,0:T(8,128)(2,1)S(1)}, u32[]{:S(2)}, u32[]{:S(2)}) %all-to-all-start.5) | async-done | bytes 1048608 | tf_op jit(solution)/shard_map/all_to_all | solution.py:132
  215.2 0.0 all-gather.2.cloned.1.call-done
  215.2 10.2 %fusion.9 = (f32[2,256]{1,0:T(2,128)S(1)}, f32[2,256,3072]{2,1,0:T(8,128)S(1)}) fusion(bf16[16,128,3072,1]{2,1,3,0:T(8,128)(2,1)} %bitcast.58, bf16[16,1,256,128]{3,2,1,0:T(8,128)(2,1)S(1)} %all-to-all-done.5, bf16[16,1,256,128]{3,2,1,0:T(8,128)(2,1)} %all-to-all-done.2, f32[2,3072]{1,0:T(2,128)S(1)} %get-tuple-element.21, bf16[1,2,256,3072]{3,2,1,0:T(8,128)(2,1)} %param.16), kind=kOutput, calls=%fused_computation.31 | convolution fusion | flops 6449790464 | bytes 24143872 | tf_op jit(solution)/shard_map/hptd,hdo->pto/dot_general | solution.py:137
  225.5 0.8 multiply_reduce_fusion
  226.3 0.0 copy-done
  226.3 0.0 copy-start.8
  226.3 0.0 copy-start.4
  226.3 0.0 copy-start.5
  226.3 0.0 copy-start.3
  226.3 0.0 copy-start.7
  226.3 1.6 fusion
  227.9 0.1 collective-permute-start
  228.0 0.0 copy-done.8
  228.1 0.0 copy-done.4
  228.1 0.6 reduce_max.31
  228.7 0.0 copy-done.5
  228.7 0.6 reduce_max.33
  229.3 0.0 collective-permute-done
  229.3 0.0 copy-done.3
  229.3 0.0 copy-done.7
  229.3 0.8 multiply_reduce_fusion.1
  230.1 1.4 pad_maximum_fusion
  231.5 10.6 %all_to_all.39 = f32[16,1,4]{2,1,0:T(1,128)S(1)} all-to-all(f32[16,1,4]{2,1,0:T(1,128)S(1)} %broadcast_in_dim.2), channel_id=1, replica_groups=mesh['cfg'=2,'req'=4,'seq'=16] {'seq'}, dimensions={0} | all-to-all | bytes 512 | tf_op jit(solution)/shard_map/all_to_all | solution.py:164
  242.1 0.1 copy.27
  242.2 0.6 slice_reduce_fusion
  242.8 0.5 sqrt_bitcast_fusion
  (7 shorter events, 0.1 us)
Async XLA Ops:
  7.2 219.1 %copy-start = (bf16[3072,64]{0,1:T(8,128)(2,1)S(1)}, bf16[3072,64]{0,1:T(8,128)(2,1)}, u32[]{:S(2)}) copy-start(bf16[3072,64]{0,1:T(8,128)(2,1)} %param.19) | copy-start | bytes 1179652
  7.2 208.0 %all-gather.2.cloned.1.call-start = ((), (), s32[]{:S(2)}) async-start(), calls=%async_computation.7 | async-start | bytes 12681216 | tf_op jit(solution)/shard_map/all_gather | solution.py:136
  9.8 16.6 %all-to-all-start.1 = ((bf16[16,1,2,32,128]{4,3,2,1,0:T(8,128)(2,1)}), bf16[16,1,2,32,128]{4,3,2,1,0:T(8,128)(2,1)S(1)}, u32[]{:S(2)}, u32[]{:S(2)}) async-start(bf16[16,1,2,32,128]{4,3,2,1,0:T(8,128)(2,1)} %bitcast.50), calls=%async_computation.1 | async-start | bytes 524288 | tf_op jit(solution)/shard_map/all_to_all | solution.py:130
  26.4 10.4 %copy-start.2 = (bf16[16,1,2,32,128]{4,3,2,1,0:T(8,128)(2,1)}, bf16[16,1,2,32,128]{4,3,2,1,0:T(8,128)(2,1)S(1)}, u32[]{:S(2)}) copy-start(bf16[16,1,2,32,128]{4,3,2,1,0:T(8,128)(2,1)S(1)} %all-to-all-done.1.kt_ref.vt_ref) | copy-start | bytes 786436
  26.4 16.4 %all-to-all-start.4 = ((bf16[16,1,2,32,128]{4,3,2,1,0:T(8,128)(2,1)}), bf16[16,1,2,32,128]{4,3,2,1,0:T(8,128)(2,1)}, u32[]{:S(2)}, u32[]{:S(2)}) async-start(bf16[16,1,2,32,128]{4,3,2,1,0:T(8,128)(2,1)} %bitcast.49), calls=%async_computation.4 | async-start | bytes 524288 | tf_op jit(solution)/shard_map/all_to_all | solution.py:130
  42.8 58.6 %all-to-all-start = ((bf16[16,1,3,256,128]{4,3,2,1,0:T(8,128)(2,1)}), bf16[16,1,3,256,128]{4,3,2,1,0:T(8,128)(2,1)}, u32[]{:S(2)}, u32[]{:S(2)}) async-start(bf16[16,1,3,256,128]{4,3,2,1,0:T(8,128)(2,1)} %bitcast.4), calls=%async_computation | async-start | bytes 6291456 | tf_op jit(solution)/shard_map/all_to_all | solution.py:129
  53.1 54.5 %copy-start.6 = (s32[2]{0:T(128)S(1)}, s32[2]{0:T(128)}, u32[]{:S(2)}) copy-start(s32[2]{0:T(128)} %param.12) | copy-start | bytes 28
  101.4 52.6 %all-to-all-start.3 = ((bf16[16,1,3,256,128]{4,3,2,1,0:T(8,128)(2,1)}), bf16[16,1,3,256,128]{4,3,2,1,0:T(8,128)(2,1)S(1)}, u32[]{:S(2)}, u32[]{:S(2)}) async-start(bf16[16,1,3,256,128]{4,3,2,1,0:T(8,128)(2,1)} %bitcast.7), calls=%async_computation.3 | async-start | bytes 6291456 | tf_op jit(solution)/shard_map/all_to_all | solution.py:129
  154.0 4.5 %copy-start.1 = (bf16[16,1,3,256,128]{4,3,2,1,0:T(8,128)(2,1)}, bf16[16,1,3,256,128]{4,3,2,1,0:T(8,128)(2,1)S(1)}, u32[]{:S(2)}) copy-start(bf16[16,1,3,256,128]{4,3,2,1,0:T(8,128)(2,1)S(1)} %all-to-all-done.3.q_ref.ki_ref.vi_ref) | copy-start | bytes 9437188
  154.0 38.7 %all-to-all-start.2 = ((bf16[16,1,256,128]{3,2,1,0:T(8,128)(2,1)}), bf16[16,1,256,128]{3,2,1,0:T(8,128)(2,1)}, u32[]{:S(2)}, u32[]{:S(2)}) async-start(bf16[16,1,256,128]{3,2,1,0:T(8,128)(2,1)} %get-tuple-element.7), calls=%async_computation.2 | async-start | bytes 2097152 | tf_op jit(solution)/shard_map/all_to_all | solution.py:132
  192.7 22.5 %all-to-all-start.5 = ((bf16[16,1,256,128]{3,2,1,0:T(8,128)(2,1)}), bf16[16,1,256,128]{3,2,1,0:T(8,128)(2,1)S(1)}, u32[]{:S(2)}, u32[]{:S(2)}) async-start(bf16[16,1,256,128]{3,2,1,0:T(8,128)(2,1)} %get-tuple-element.8), calls=%async_computation.5 | async-start | bytes 2097152 | tf_op jit(solution)/shard_map/all_to_all | solution.py:132
  226.3 1.8 copy-start.8
  226.3 1.8 copy-start.4
  226.3 2.4 copy-start.5
  226.3 3.0 %copy-start.3 = (f32[2,256,32]{1,2,0:T(8,128)S(1)}, f32[2,256,32]{1,2,0:T(8,128)}, u32[]{:S(2)}) copy-start(f32[2,256,32]{1,2,0:T(8,128)} %param.17) | copy-start | bytes 196612
  226.3 3.0 %copy-start.7 = (f32[2]{0:T(128)S(1)}, f32[2]{0:T(128)}, u32[]{:S(2)}) copy-start(f32[2]{0:T(128)} %param.14) | copy-start | bytes 28
  227.9 1.3 collective-permute-start
Sparse Core Ops, SparseCore 0:
  11.1 132.0 all-gather.1

commit v6 on v5

--- a/solution.py
+++ b/solution.py
@@ -30,13 +30,12 @@
 
 
 def attn_kernel(tl_ref, q_ref, kt_ref, vt_ref, ki_ref, vi_ref, o_ref, m_ref):
-    p = pl.program_id(0)
     dims = (((1,), (1,)), ((), ()))
     q = q_ref[...].reshape(-1, HD)
     st = lax.dot_general(q, kt_ref[...].reshape(-1, HD), dims, preferred_element_type=jnp.float32)
     st = st * HD ** (-0.5)
     col = lax.broadcasted_iota(jnp.int32, st.shape, 1)
-    st = jnp.where(col < tl_ref[p], st, -jnp.inf)
+    st = jnp.where(col < tl_ref[0], st, -jnp.inf)
     m = jnp.max(st, axis=1, keepdims=True)
     e = jnp.exp(st - m)
     l = jnp.sum(e, axis=1, keepdims=True)
@@ -59,47 +58,46 @@
     m_ref[...] = jnp.full(m_ref.shape, jnp.max(m), jnp.float32)
 
 
-def attention(text_len, img, txt):
-    src, prompts, _, rows, _ = img.shape
-    trows = txt.shape[3]
+def attention(text_len, buf, rows, trows):
+    src = buf.shape[0]
     img_len = src * rows
     txt_len = src * trows
     per = BQ // rows
     nq = src // per
     grid_spec = pltpu.PrefetchScalarGridSpec(
         num_scalar_prefetch=1,
-        grid=(prompts, nq),
+        grid=(1, nq),
         in_specs=[
-            pl.BlockSpec((per, None, None, rows, HD), lambda p, i, tl: (i, p, 0, 0, 0)),
-            pl.BlockSpec((src, None, None, trows, HD), lambda p, i, tl: (0, p, 0, 0, 0)),
-            pl.BlockSpec((src, None, None, trows, HD), lambda p, i, tl: (0, p, 1, 0, 0)),
-            pl.BlockSpec((src, None, None, rows, HD), lambda p, i, tl: (0, p, 1, 0, 0)),
-            pl.BlockSpec((src, None, None, rows, HD), lambda p, i, tl: (0, p, 2, 0, 0)),
+            pl.BlockSpec((per, rows, HD), lambda p, i, tl: (i, 0, 0)),
+            pl.BlockSpec((src, trows, HD), lambda p, i, tl: (0, 3 * rows // trows, 0)),
+            pl.BlockSpec((src, trows, HD), lambda p, i, tl: (0, 3 * rows // trows + 1, 0)),
+            pl.BlockSpec((src, rows, HD), lambda p, i, tl: (0, 1, 0)),
+            pl.BlockSpec((src, rows, HD), lambda p, i, tl: (0, 2, 0)),
         ],
         out_specs=[
-            pl.BlockSpec((per, None, rows, HD), lambda p, i, tl: (i, p, 0, 0)),
-            pl.BlockSpec((None, None, 8, 128), lambda p, i, tl: (p, i, 0, 0)),
+            pl.BlockSpec((per, rows, HD), lambda p, i, tl: (i, 0, 0)),
+            pl.BlockSpec((None, 8, 128), lambda p, i, tl: (i, 0, 0)),
         ],
     )
     cost = pl.CostEstimate(
-        flops=4 * prompts * img_len * (img_len + txt_len) * HD,
-        transcendentals=prompts * img_len * (img_len + txt_len),
-        bytes_accessed=img.size * 2 + txt.size * 2 + prompts * img_len * HD * 2,
+        flops=4 * img_len * (img_len + txt_len) * HD,
+        transcendentals=img_len * (img_len + txt_len),
+        bytes_accessed=buf.size * 2 + img_len * HD * 2,
     )
     out, top = pl.pallas_call(
         attn_kernel,
         grid_spec=grid_spec,
         out_shape=[
-            jax.ShapeDtypeStruct((src, prompts, rows, HD), jnp.bfloat16),
-            jax.ShapeDtypeStruct((prompts, nq, 8, 128), jnp.float32),
+            jax.ShapeDtypeStruct((src, rows, HD), jnp.bfloat16),
+            jax.ShapeDtypeStruct((nq, 8, 128), jnp.float32),
         ],
         compiler_params=pltpu.CompilerParams(
             dimension_semantics=("arbitrary", "arbitrary"),
             vmem_limit_bytes=60 * 1024 * 1024,
         ),
         cost_estimate=cost,
-    )(text_len, img, txt, txt, img, img)
-    return out, jnp.max(top, axis=(1, 2, 3))
+    )(text_len, buf, buf, buf, buf, buf)
+    return out, jnp.max(top)[None]
 
 
 def shards(
@@ -122,14 +120,15 @@
     outs = []
     maxes = []
     for p in range(local_prompts):
-        joined = img_qkv[0, p].reshape(1, img_dev, 3, seq, HEADS // seq * HD)
-        joined = joined.transpose(3, 0, 2, 1, 4)
-        text_rows = txt_kv[0, p].reshape(1, txt_dev, 2, seq, HEADS // seq * HD)
-        text_rows = text_rows.transpose(3, 0, 2, 1, 4)
-        full_img = lax.all_to_all(joined, "seq", 0, 0, tiled=True)
-        full_txt = lax.all_to_all(text_rows, "seq", 0, 0, tiled=True)
-        head_rows, top = attention(text_len[p : p + 1], full_img, full_txt)
-        outs.append(lax.all_to_all(head_rows, "seq", 0, 0, tiled=True))
+        joined = img_qkv[0, p].reshape(img_dev, 3, seq, HEADS // seq * HD)
+        joined = joined.transpose(2, 1, 0, 3).reshape(seq, 3 * img_dev, HD)
+        text_rows = txt_kv[0, p].reshape(txt_dev, 2, seq, HEADS // seq * HD)
+        text_rows = text_rows.transpose(2, 1, 0, 3).reshape(seq, 2 * txt_dev, HD)
+        buf = lax.all_to_all(
+            jnp.concatenate([joined, text_rows], axis=1), "seq", 0, 0, tiled=True
+        )
+        head_rows, top = attention(text_len[p : p + 1], buf, img_dev, txt_dev)
+        outs.append(lax.all_to_all(head_rows, "seq", 0, 0, tiled=True)[:, None])
         maxes.append(top)
     token_rows = jnp.concatenate(outs, axis=1)
     local_max = jnp.concatenate(maxes)

time: 252 us -> 239 us (0.948)
  local copies, waits for them, and re-layouts: 21.7 us -> 8.1 us
  starting transfers between devices: 37 us -> 30.9 us
  waiting for transfers between devices: 80.4 us -> 85.3 us
  other arithmetic: 6.11 us -> 9.37 us
    slice x2 -> x1, local copies, waits for them, and re-layouts: 6.78 us -> 0.58 us  [shards(): head_rows, top = attention(text_len[p:p + 1], buf, img_dev, txt_dev)]
    all_to_all x6 -> x4, starting transfers between devices: 36.9 us -> 30.8 us  [the longest x2 18.2 us: shards(): outs.append(lax.all_to_all(head_rows, 'seq', 0, 0, tiled=True)[:, None])]
    another operation x4, local copies, waits for them, and re-layouts: 7.23 us -> 1.83 us  [the longest x2 1.62 us: shards(): joined = img_qkv[0, p].reshape(img_dev, 3, seq, HEADS // seq * HD)]
    all_to_all x6 -> x4, waiting for transfers between devices: 79.7 us -> 84.6 us  [the longest x2 70.7 us: shards(): lax.all_to_all(jnp.concatenate([joined, text_rows], axis=1), 'seq', 0, 0,...]
    concatenate x0 -> x2, other arithmetic: none -> 4.04 us  [shards(): jnp.concatenate([joined, text_rows], axis=1)]
    unnamed x23 -> x26, local copies, waits for them, and re-layouts: 7.54 us -> 5.58 us
  transfers between devices with their start and end apart: 8 -> 6, of which waited for: 4 -> 3; matrix products, arithmetic and copies ran while one was open for 9% -> 6% of each run, Pallas kernels for 27% -> 29%
where the time goes in v6:
time: 239 us; the launch traced here: 238 us
  waiting for transfers between devices  85.3 us (36%)
  Pallas kernels  68.4 us (29%)
  starting transfers between devices  30.9 us (13%)
  between operations  14.3 us (6%)
  matrix products  11.5 us (5%)
  blocking collectives  10.4 us (4%)
  other arithmetic  9.37 us (4%)
  local copies, waits for them, and re-layouts  8.1 us (3%)
    all_to_all x2, waiting for transfers between devices, shards(): lax.all_to_all(jnp.concatenate([joined, text_rows], axis=1), 'seq', 0, 0,...  70.7 us
    pallas_call x2, Pallas kernels, attention(): pl.pallas_call(attn_kernel, grid_spec=grid_spec, out_shape=[jax.ShapeDtyp...  68.4 us
    all_to_all x2, starting transfers between devices, shards(): outs.append(lax.all_to_all(head_rows, 'seq', 0, 0, tiled=True)[:, None])  18.2 us
    all_to_all x2, waiting for transfers between devices, shards(): outs.append(lax.all_to_all(head_rows, 'seq', 0, 0, tiled=True)[:, None])  13.9 us
    all_to_all x2, starting transfers between devices, shards(): lax.all_to_all(jnp.concatenate([joined, text_rows], axis=1), 'seq', 0, 0,...  12.6 us
    all_to_all x1, blocking collectives, shards(): lax.all_to_all(jnp.broadcast_to(stats[None], (seq, stats.shape[0])), 'seq...  10.4 us
    dot_general x1, matrix products, shards(): jnp.einsum('hptd,hdo->pto', token_rows, weight.reshape(seq, HEADS // seq...  9.93 us
    unnamed x26, local copies, waits for them, and re-layouts  5.58 us
  transfers between devices with their start and end apart: 6, of which 3 were waited for; matrix products, arithmetic and copies ran while one was open for 6% of the time, Pallas kernels for 29%

profile of v6, /device:TPU:8, one launch (start us, length us, event | category | flops | bytes accessed | tf_op | source)
XLA Modules:
  0.0 238.3 jit_solution(3976213300495397216)
XLA Ops:
  7.2 0.0 copy-start
  7.2 0.0 all-gather.2.cloned.1.call-start
  7.2 0.7 all-gather.2.cloned.1.call-update
  7.9 3.3 %slice_bitcast_fusion.1 = (bf16[32,8,48,128]{3,1,2,0:T(8,128)(2,1)S(1)}, bf16[32,8,48,128]{3,1,2,0:T(8,128)(2,1)S(1)}) fusion(bf16[1,2,256,6144]{3,2,1,0:T(8,128)(2,1)} %param.10), kind=kLoop, calls=%fused_computation.7 | loop fusion | bytes 12582912
  11.2 0.0 copy-start.2
  11.2 0.7 copy.25
  11.9 0.8 copy.19
  12.7 0.0 copy-done.2
  12.7 0.7 slice_bitcast_fusion.3
  13.5 0.1 copy.20
  13.6 2.0 pad_maximum_fusion.1
  15.6 7.9 %all-to-all-start.2 = ((bf16[16,832,128]{2,1,0:T(8,128)(2,1)}), bf16[16,832,128]{2,1,0:T(8,128)(2,1)}, u32[]{:S(2)}, u32[]{:S(2)}) async-start(bf16[16,832,128]{2,1,0:T(8,128)(2,1)} %pad_maximum_fusion.1), calls=%async_computation.2 | async-start | bytes 6815744 | tf_op jit(solution)/shard_map/all_to_all | solution.py:127
  23.6 0.0 copy-start.1
  23.6 0.7 copy.23
  24.3 0.8 copy.17
  25.1 0.0 copy-done.1
  25.2 0.1 copy.18
  25.3 0.0 copy-start.7
  25.3 2.0 pad_maximum_fusion
  27.3 49.0 %all-to-all-done.2.q_ref.kt_ref.vt_ref.ki_ref.vi_ref = bf16[16,832,128]{2,1,0:T(8,128)(2,1)} async-done(((bf16[16,832,128]{2,1,0:T(8,128)(2,1)}), bf16[16,832,128]{2,1,0:T(8,128)(2,1)}, u32[]{:S(2)}, u32[]{:S(2)}) %all-to-all-start.2) | async-done | bytes 3407904 | tf_op jit(solution)/shard_map/all_to_all | solution.py:127
  76.3 4.7 %all-to-all-start = ((bf16[16,832,128]{2,1,0:T(8,128)(2,1)}), bf16[16,832,128]{2,1,0:T(8,128)(2,1)}, u32[]{:S(2)}, u32[]{:S(2)}) async-start(bf16[16,832,128]{2,1,0:T(8,128)(2,1)} %pad_maximum_fusion), calls=%async_computation | async-start | bytes 6815744 | tf_op jit(solution)/shard_map/all_to_all | solution.py:127
  81.0 0.0 copy-done.7
  81.0 0.6 fusion.7
  81.6 34.2 %shard_map.122 = (bf16[16,256,128]{2,1,0:T(8,128)(2,1)}, f32[4,8,128]{2,1,0:T(8,128)}) custom-call(s32[1]{0:T(128)} %get-tuple-element.23.tl_ref, bf16[16,832,128]{2,1,0:T(8,128)(2,1)} %all-to-all-done.2.q_ref.kt_ref.vt_ref.ki_ref.vi_ref, bf16[16,832,128]{2,1,0:T(8,128)(2,1)} %all-to-all-done.2.q_ref.kt_ref.vt_ref.ki_ref.vi_ref, ...), custom_call_target="tpu_custom_call" | custom-call | flops 9663676416 | bytes 4456448 | tf_op jit(solution)/shard_map/pallas_call | solution.py:87
  115.9 21.7 %all-to-all-done.q_ref.kt_ref.vt_ref.ki_ref.vi_ref = bf16[16,832,128]{2,1,0:T(8,128)(2,1)} async-done(((bf16[16,832,128]{2,1,0:T(8,128)(2,1)}), bf16[16,832,128]{2,1,0:T(8,128)(2,1)}, u32[]{:S(2)}, u32[]{:S(2)}) %all-to-all-start) | async-done | bytes 3407904 | tf_op jit(solution)/shard_map/all_to_all | solution.py:127
  137.6 10.9 %all-to-all-start.3 = ((bf16[16,256,128]{2,1,0:T(8,128)(2,1)}), bf16[16,256,128]{2,1,0:T(8,128)(2,1)S(1)}, u32[]{:S(2)}, u32[]{:S(2)}) async-start(bf16[16,256,128]{2,1,0:T(8,128)(2,1)} %get-tuple-element.8), calls=%async_computation.3 | async-start | bytes 2097152 | tf_op jit(solution)/shard_map/all_to_all | solution.py:131
  148.6 0.0 copy-start.3
  148.6 34.2 %shard_map.121 = (bf16[16,256,128]{2,1,0:T(8,128)(2,1)}, f32[4,8,128]{2,1,0:T(8,128)}) custom-call(s32[1]{0:T(128)} %get-tuple-element.22.tl_ref, bf16[16,832,128]{2,1,0:T(8,128)(2,1)} %all-to-all-done.q_ref.kt_ref.vt_ref.ki_ref.vi_ref, bf16[16,832,128]{2,1,0:T(8,128)(2,1)} %all-to-all-done.q_ref.kt_ref.vt_ref.ki_ref.vi_ref, ...), custom_call_target="tpu_custom_call" | custom-call | flops 9663676416 | bytes 4456448 | tf_op jit(solution)/shard_map/pallas_call | solution.py:87
  182.8 0.0 all-to-all-done.3
  182.8 7.2 %all-to-all-start.1 = ((bf16[16,256,128]{2,1,0:T(8,128)(2,1)}), bf16[16,256,128]{2,1,0:T(8,128)(2,1)S(1)}, u32[]{:S(2)}, u32[]{:S(2)}) async-start(bf16[16,256,128]{2,1,0:T(8,128)(2,1)} %get-tuple-element.7), calls=%async_computation.1 | async-start | bytes 2097152 | tf_op jit(solution)/shard_map/all_to_all | solution.py:131
  190.0 0.0 copy-done.3
  190.0 13.9 %all-to-all-done.1 = bf16[16,256,128]{2,1,0:T(8,128)(2,1)S(1)} async-done(((bf16[16,256,128]{2,1,0:T(8,128)(2,1)}), bf16[16,256,128]{2,1,0:T(8,128)(2,1)S(1)}, u32[]{:S(2)}, u32[]{:S(2)}) %all-to-all-start.1) | async-done | bytes 1048608 | tf_op jit(solution)/shard_map/all_to_all | solution.py:131
  203.9 0.0 all-gather.2.cloned.1.call-done
  203.9 9.9 %fusion.8 = (f32[2,256]{1,0:T(2,128)S(1)}, f32[2,256,3072]{2,1,0:T(8,128)S(1)}) fusion(bf16[16,128,3072,1]{2,1,0,3:T(8,128)(2,1)} %bitcast.79, bf16[16,1,256,128]{3,2,0,1:T(8,128)(2,1)S(1)} %bitcast.70, bf16[16,1,256,128]{3,2,0,1:T(8,128)(2,1)S(1)} %bitcast.71, f32[2,3072]{1,0:T(2,128)S(1)} %get-tuple-element.21, bf16[1,2,256,3072]{3,2,1,0:T(8,128)(2,1)} %param.16), kind=kOutput, calls=%fused_computation.32 | convolution fusion | flops 6449790464 | bytes 24143872 | tf_op jit(solution)/shard_map/hptd,hdo->pto/dot_general | solution.py:136
  213.9 0.8 multiply_reduce_fusion
  214.6 0.0 copy-done
  214.7 0.0 copy-start.9
  214.7 0.0 copy-start.6
  214.7 0.0 copy-start.5
  214.7 0.0 copy-start.4
  214.7 0.0 copy-start.8
  214.7 1.6 fusion
  216.3 0.1 collective-permute-start
  216.4 0.0 copy-done.9
  216.5 0.0 copy-done.6
  216.5 0.6 reduce_max.27
  217.1 0.0 copy-done.5
  217.1 0.6 reduce_max.28
  217.7 0.0 collective-permute-done
  217.7 0.0 copy-done.4
  217.7 0.0 copy-done.8
  217.7 0.8 multiply_reduce_fusion.1
  218.5 1.4 pad_maximum_fusion.2
  219.9 10.4 %all_to_all.29 = f32[16,1,4]{2,1,0:T(1,128)S(1)} all-to-all(f32[16,1,4]{2,1,0:T(1,128)S(1)} %broadcast_in_dim.26), channel_id=1, replica_groups=mesh['cfg'=2,'req'=4,'seq'=16] {'seq'}, dimensions={0} | all-to-all | bytes 512 | tf_op jit(solution)/shard_map/all_to_all | solution.py:163
  230.2 0.1 copy.21
  230.3 0.6 slice_reduce_fusion
  231.0 0.5 sqrt_bitcast_fusion
  (8 shorter events, 0.2 us)
Async XLA Ops:
  7.2 207.5 %copy-start = (bf16[3072,64]{0,1:T(8,128)(2,1)S(1)}, bf16[3072,64]{0,1:T(8,128)(2,1)}, u32[]{:S(2)}) copy-start(bf16[3072,64]{0,1:T(8,128)(2,1)} %param.19) | copy-start | bytes 1179652
  7.2 196.7 %all-gather.2.cloned.1.call-start = ((), (), s32[]{:S(2)}) async-start(), calls=%async_computation.5 | async-start | bytes 12681216 | tf_op jit(solution)/shard_map/all_gather | solution.py:135
  11.2 1.6 copy-start.2
  15.6 60.7 %all-to-all-start.2 = ((bf16[16,832,128]{2,1,0:T(8,128)(2,1)}), bf16[16,832,128]{2,1,0:T(8,128)(2,1)}, u32[]{:S(2)}, u32[]{:S(2)}) async-start(bf16[16,832,128]{2,1,0:T(8,128)(2,1)} %pad_maximum_fusion.1), calls=%async_computation.2 | async-start | bytes 6815744 | tf_op jit(solution)/shard_map/all_to_all | solution.py:127
  23.6 1.6 copy-start.1
  25.3 55.7 %copy-start.7 = (s32[2]{0:T(128)S(1)}, s32[2]{0:T(128)}, u32[]{:S(2)}) copy-start(s32[2]{0:T(128)} %param.12) | copy-start | bytes 28
  76.3 61.3 %all-to-all-start = ((bf16[16,832,128]{2,1,0:T(8,128)(2,1)}), bf16[16,832,128]{2,1,0:T(8,128)(2,1)}, u32[]{:S(2)}, u32[]{:S(2)}) async-start(bf16[16,832,128]{2,1,0:T(8,128)(2,1)} %pad_maximum_fusion), calls=%async_computation | async-start | bytes 6815744 | tf_op jit(solution)/shard_map/all_to_all | solution.py:127
  137.6 45.2 %all-to-all-start.3 = ((bf16[16,256,128]{2,1,0:T(8,128)(2,1)}), bf16[16,256,128]{2,1,0:T(8,128)(2,1)S(1)}, u32[]{:S(2)}, u32[]{:S(2)}) async-start(bf16[16,256,128]{2,1,0:T(8,128)(2,1)} %get-tuple-element.8), calls=%async_computation.3 | async-start | bytes 2097152 | tf_op jit(solution)/shard_map/all_to_all | solution.py:131
  148.6 41.4 %copy-start.3 = (f32[1,2,3,3072]{3,1,2,0:T(2,128)S(1)}, f32[1,2,3,3072]{3,1,2,0:T(2,128)}, u32[]{:S(2)}) copy-start(f32[1,2,3,3072]{3,1,2,0:T(2,128)} %param.15) | copy-start | bytes 221188
  182.8 21.2 %all-to-all-start.1 = ((bf16[16,256,128]{2,1,0:T(8,128)(2,1)}), bf16[16,256,128]{2,1,0:T(8,128)(2,1)S(1)}, u32[]{:S(2)}, u32[]{:S(2)}) async-start(bf16[16,256,128]{2,1,0:T(8,128)(2,1)} %get-tuple-element.7), calls=%async_computation.1 | async-start | bytes 2097152 | tf_op jit(solution)/shard_map/all_to_all | solution.py:131
  214.7 1.8 copy-start.9
  214.7 1.8 copy-start.6
  214.7 2.4 %copy-start.5 = (f32[4,8,128]{2,1,0:T(8,128)S(1)}, f32[4,8,128]{2,1,0:T(8,128)}, u32[]{:S(2)}) copy-start(f32[4,8,128]{2,1,0:T(8,128)} %get-tuple-element.10) | copy-start | bytes 49156
  214.7 3.0 %copy-start.4 = (f32[2,256,32]{1,2,0:T(8,128)S(1)}, f32[2,256,32]{1,2,0:T(8,128)}, u32[]{:S(2)}) copy-start(f32[2,256,32]{1,2,0:T(8,128)} %param.17) | copy-start | bytes 196612
  214.7 3.0 %copy-start.8 = (f32[2]{0:T(128)S(1)}, f32[2]{0:T(128)}, u32[]{:S(2)}) copy-start(f32[2]{0:T(128)} %param.14) | copy-start | bytes 28
  216.3 1.3 collective-permute-start
Sparse Core Ops, SparseCore 0:
  11.1 136.1 all-gather.1

commit v7 on v6

--- a/solution.py
+++ b/solution.py
@@ -132,7 +132,12 @@
         maxes.append(top)
     token_rows = jnp.concatenate(outs, axis=1)
     local_max = jnp.concatenate(maxes)
-    weight = lax.all_gather(proj_weight, ("cfg", "req", "seq"), axis=0, tiled=True)
+    weight_half = lax.all_gather(proj_weight, ("req", "seq"), axis=0, tiled=True)
+    other_half = swapped(weight_half, "cfg", 0)
+    first = lax.axis_index("cfg") == 0
+    weight = jnp.concatenate(
+        [jnp.where(first, weight_half, other_half), jnp.where(first, other_half, weight_half)], axis=0
+    )
     projected = jnp.einsum(
         "hptd,hdo->pto",
         token_rows,

time: 239 us -> 286 us (1.20)
  waiting for transfers between devices: 85.3 us -> 116 us
  other arithmetic: 9.37 us -> 30.2 us
  starting transfers between devices: 30.9 us -> 25.1 us
    all_gather x1, waiting for transfers between devices: 0.01 us -> 90.8 us  [shards(): lax.all_gather(proj_weight, ('req', 'seq'), axis=0, tiled=True)]
    all_to_all x2, waiting for transfers between devices: 70.7 us -> 18.5 us  [shards(): lax.all_to_all(jnp.concatenate([joined, text_rows], axis=1), 'seq', 0, 0,...]
    concatenate x0 -> x1, other arithmetic: none -> 10.5 us  [shards(): jnp.concatenate([jnp.where(first, weight_half, other_half), jnp.where(fir...]
    select_n x0 -> x1, other arithmetic: none -> 10.3 us  [shards(): jnp.where(first, weight_half, other_half)]
    all_to_all x2, waiting for transfers between devices: 13.9 us -> 5.87 us  [shards(): outs.append(lax.all_to_all(head_rows, 'seq', 0, 0, tiled=True)[:, None])]
    all_to_all x2, starting transfers between devices: 18.2 us -> 11.6 us  [shards(): outs.append(lax.all_to_all(head_rows, 'seq', 0, 0, tiled=True)[:, None])]
  transfers between devices with their start and end apart: 6 -> 7, of which waited for: 3 -> 3; matrix products, arithmetic and copies ran while one was open for 6% -> 12% of each run, Pallas kernels for 29% -> 24%
where the time goes in v7:
time: 286 us; the launch traced here: 284 us
  waiting for transfers between devices  116 us (41%)
  Pallas kernels  68.3 us (24%)
  other arithmetic  30.2 us (11%)
  starting transfers between devices  25.1 us (9%)
  between operations  14.3 us (5%)
  matrix products  11.6 us (4%)
  blocking collectives  10.5 us (4%)
  local copies, waits for them, and re-layouts  8.09 us (3%)
    all_gather x1, waiting for transfers between devices, shards(): lax.all_gather(proj_weight, ('req', 'seq'), axis=0, tiled=True)  90.8 us
    pallas_call x2, Pallas kernels, attention(): pl.pallas_call(attn_kernel, grid_spec=grid_spec, out_shape=[jax.ShapeDtyp...  68.3 us
    all_to_all x2, waiting for transfers between devices, shards(): lax.all_to_all(jnp.concatenate([joined, text_rows], axis=1), 'seq', 0, 0,...  18.5 us
    all_to_all x2, starting transfers between devices, shards(): lax.all_to_all(jnp.concatenate([joined, text_rows], axis=1), 'seq', 0, 0,...  13.4 us
    all_to_all x2, starting transfers between devices, shards(): outs.append(lax.all_to_all(head_rows, 'seq', 0, 0, tiled=True)[:, None])  11.6 us
    all_to_all x1, blocking collectives, shards(): lax.all_to_all(jnp.broadcast_to(stats[None], (seq, stats.shape[0])), 'seq...  10.5 us
    concatenate x1, other arithmetic, shards(): jnp.concatenate([jnp.where(first, weight_half, other_half), jnp.where(fir...  10.5 us
    select_n x1, other arithmetic, shards(): jnp.where(first, weight_half, other_half)  10.3 us
  transfers between devices with their start and end apart: 7, of which 3 were waited for; matrix products, arithmetic and copies ran while one was open for 12% of the time, Pallas kernels for 24%

profile of v7, /device:TPU:8, one launch (start us, length us, event | category | flops | bytes accessed | tf_op | source)
XLA Modules:
  0.0 283.9 jit_solution(4744817205809567303)
XLA Ops:
  7.2 0.0 copy-start
  7.2 0.0 all-gather.2.cloned.1.call-start
  7.2 0.7 all-gather.2.cloned.1.call-update
  7.9 3.3 %slice_bitcast_fusion.1 = (bf16[32,8,48,128]{3,1,2,0:T(8,128)(2,1)S(1)}, bf16[32,8,48,128]{3,1,2,0:T(8,128)(2,1)S(1)}) fusion(bf16[1,2,256,6144]{3,2,1,0:T(8,128)(2,1)} %param.10), kind=kLoop, calls=%fused_computation.10 | loop fusion | bytes 12582912
  11.2 0.0 copy-start.2
  11.2 0.7 copy.25
  11.9 0.8 copy.19
  12.7 0.0 copy-done.2
  12.7 0.7 slice_bitcast_fusion.3
  13.5 0.1 copy.20
  13.6 2.0 pad_maximum_fusion.2
  15.6 7.9 %all-to-all-start.2 = ((bf16[16,832,128]{2,1,0:T(8,128)(2,1)}), bf16[16,832,128]{2,1,0:T(8,128)(2,1)}, u32[]{:S(2)}, u32[]{:S(2)}) async-start(bf16[16,832,128]{2,1,0:T(8,128)(2,1)} %pad_maximum_fusion.2), calls=%async_computation.2 | async-start | bytes 6815744 | tf_op jit(solution)/shard_map/all_to_all | solution.py:127
  23.6 90.8 %all-gather.2.cloned.1.call-done = bf16[1024,3072]{1,0:T(8,128)(2,1)} async-done(((bf16[16,3072]{1,0:T(8,128)(2,1)}), bf16[1024,3072]{1,0:T(8,128)(2,1)}) %all-gather.2.cloned.1.call-update) | async-done | bytes 6291472 | tf_op jit(solution)/shard_map/all_gather | solution.py:135
  114.3 0.0 collective-permute-start
  114.3 0.0 copy-start.1
  114.3 0.7 copy.23
  115.1 0.8 copy.17
  115.9 0.0 copy-done.1
  116.0 0.1 copy.18
  116.1 0.0 copy-start.7
  116.1 0.0 copy-start.3
  116.1 2.0 pad_maximum_fusion.1
  118.1 0.0 all-to-all-done.2.q_ref.kt_ref.vt_ref.ki_ref.vi_ref
  118.1 5.5 %all-to-all-start = ((bf16[16,832,128]{2,1,0:T(8,128)(2,1)}), bf16[16,832,128]{2,1,0:T(8,128)(2,1)}, u32[]{:S(2)}, u32[]{:S(2)}) async-start(bf16[16,832,128]{2,1,0:T(8,128)(2,1)} %pad_maximum_fusion.1), calls=%async_computation | async-start | bytes 6815744 | tf_op jit(solution)/shard_map/all_to_all | solution.py:127
  123.7 0.0 copy-done.7
  123.7 0.6 fusion.7
  124.3 0.0 copy-done.3
  124.3 34.2 %shard_map.122 = (bf16[16,256,128]{2,1,0:T(8,128)(2,1)}, f32[4,8,128]{2,1,0:T(8,128)}) custom-call(s32[1]{0:T(128)} %get-tuple-element.25.tl_ref, bf16[16,832,128]{2,1,0:T(8,128)(2,1)} %all-to-all-done.2.q_ref.kt_ref.vt_ref.ki_ref.vi_ref, bf16[16,832,128]{2,1,0:T(8,128)(2,1)} %all-to-all-done.2.q_ref.kt_ref.vt_ref.ki_ref.vi_ref, ...), custom_call_target="tpu_custom_call" | custom-call | flops 9663676416 | bytes 4456448 | tf_op jit(solution)/shard_map/pallas_call | solution.py:87
  158.5 18.5 %all-to-all-done.q_ref.kt_ref.vt_ref.ki_ref.vi_ref = bf16[16,832,128]{2,1,0:T(8,128)(2,1)} async-done(((bf16[16,832,128]{2,1,0:T(8,128)(2,1)}), bf16[16,832,128]{2,1,0:T(8,128)(2,1)}, u32[]{:S(2)}, u32[]{:S(2)}) %all-to-all-start) | async-done | bytes 3407904 | tf_op jit(solution)/shard_map/all_to_all | solution.py:127
  176.9 4.4 %all-to-all-start.3 = ((bf16[16,256,128]{2,1,0:T(8,128)(2,1)}), bf16[16,256,128]{2,1,0:T(8,128)(2,1)S(1)}, u32[]{:S(2)}, u32[]{:S(2)}) async-start(bf16[16,256,128]{2,1,0:T(8,128)(2,1)} %get-tuple-element.8), calls=%async_computation.3 | async-start | bytes 2097152 | tf_op jit(solution)/shard_map/all_to_all | solution.py:131
  181.3 34.2 %shard_map.121 = (bf16[16,256,128]{2,1,0:T(8,128)(2,1)}, f32[4,8,128]{2,1,0:T(8,128)}) custom-call(s32[1]{0:T(128)} %get-tuple-element.24.tl_ref, bf16[16,832,128]{2,1,0:T(8,128)(2,1)} %all-to-all-done.q_ref.kt_ref.vt_ref.ki_ref.vi_ref, bf16[16,832,128]{2,1,0:T(8,128)(2,1)} %all-to-all-done.q_ref.kt_ref.vt_ref.ki_ref.vi_ref, ...), custom_call_target="tpu_custom_call" | custom-call | flops 9663676416 | bytes 4456448 | tf_op jit(solution)/shard_map/pallas_call | solution.py:87
  215.4 0.0 collective-permute-done
  215.5 10.3 %broadcast_select_fusion.1 = (bf16[1024,3072]{1,0:T(8,128)(2,1)}, bf16[1024,3072]{1,0:T(8,128)(2,1)}) fusion(bf16[1024,3072]{1,0:T(8,128)(2,1)} %all-gather.2.cloned.1.call-done, bf16[1024,3072]{1,0:T(8,128)(2,1)} %collective-permute-done, pred[]{:T(512)S(6)} %eq.4), kind=kLoop, calls=%fused_computation.6 | loop fusion | flops 6291456 | bytes 25165824 | tf_op jit(solution)/shard_map/jit(_where)/select_n | solution.py:139
  225.7 0.0 all-to-all-done.3
  225.7 7.2 %all-to-all-start.1 = ((bf16[16,256,128]{2,1,0:T(8,128)(2,1)}), bf16[16,256,128]{2,1,0:T(8,128)(2,1)S(1)}, u32[]{:S(2)}, u32[]{:S(2)}) async-start(bf16[16,256,128]{2,1,0:T(8,128)(2,1)} %get-tuple-element.7), calls=%async_computation.1 | async-start | bytes 2097152 | tf_op jit(solution)/shard_map/all_to_all | solution.py:131
  233.0 10.5 %pad_maximum_fusion = bf16[2048,3072]{1,0:T(8,128)(2,1)} fusion(bf16[1024,3072]{1,0:T(8,128)(2,1)} %get-tuple-element.14, bf16[1024,3072]{1,0:T(8,128)(2,1)} %get-tuple-element.13), kind=kLoop, calls=%fused_computation | loop fusion | flops 25165824 | bytes 25165824 | tf_op jit(solution)/shard_map/concatenate | solution.py:138
  243.5 5.9 %all-to-all-done.1 = bf16[16,256,128]{2,1,0:T(8,128)(2,1)S(1)} async-done(((bf16[16,256,128]{2,1,0:T(8,128)(2,1)}), bf16[16,256,128]{2,1,0:T(8,128)(2,1)S(1)}, u32[]{:S(2)}, u32[]{:S(2)}) %all-to-all-start.1) | async-done | bytes 1048608 | tf_op jit(solution)/shard_map/all_to_all | solution.py:131
  249.3 10.0 %fusion.8 = (f32[2,256]{1,0:T(2,128)S(1)}, f32[2,256,3072]{2,1,0:T(8,128)S(1)}) fusion(bf16[16,128,3072,1]{2,1,0,3:T(8,128)(2,1)} %bitcast.66, bf16[16,1,256,128]{3,2,0,1:T(8,128)(2,1)S(1)} %bitcast.71, bf16[16,1,256,128]{3,2,0,1:T(8,128)(2,1)S(1)} %bitcast.72, f32[2,3072]{1,0:T(2,128)S(1)} %get-tuple-element.23, bf16[1,2,256,3072]{3,2,1,0:T(8,128)(2,1)} %param.16), kind=kOutput, calls=%fused_computation.35 | convolution fusion | flops 6449790464 | bytes 24143872 | tf_op jit(solution)/shard_map/hptd,hdo->pto/dot_general | solution.py:141
  259.3 0.8 multiply_reduce_fusion
  260.1 0.0 copy-done
  260.1 0.0 copy-start.9
  260.1 0.0 copy-start.6
  260.1 0.0 copy-start.5
  260.1 0.0 copy-start.4
  260.1 0.0 copy-start.8
  260.2 1.6 fusion
  261.8 0.1 collective-permute-start.1
  261.9 0.0 copy-done.9
  261.9 0.0 copy-done.6
  261.9 0.6 reduce_max.27
  262.5 0.0 copy-done.5
  262.5 0.6 reduce_max.28
  263.1 0.0 collective-permute-done.1
  263.1 0.0 copy-done.4
  263.1 0.0 copy-done.8
  263.1 0.8 multiply_reduce_fusion.1
  263.9 1.4 pad_maximum_fusion.3
  265.3 10.5 %all_to_all.29 = f32[16,1,4]{2,1,0:T(1,128)S(1)} all-to-all(f32[16,1,4]{2,1,0:T(1,128)S(1)} %broadcast_in_dim.26), channel_id=1, replica_groups=mesh['cfg'=2,'req'=4,'seq'=16] {'seq'}, dimensions={0} | all-to-all | bytes 512 | tf_op jit(solution)/shard_map/all_to_all | solution.py:168
  275.8 0.1 copy.21
  275.9 0.6 slice_reduce_fusion
  276.5 0.5 sqrt_bitcast_fusion
  (8 shorter events, 0.2 us)
Async XLA Ops:
  7.2 252.9 %copy-start = (bf16[3072,64]{0,1:T(8,128)(2,1)S(1)}, bf16[3072,64]{0,1:T(8,128)(2,1)}, u32[]{:S(2)}) copy-start(bf16[3072,64]{0,1:T(8,128)(2,1)} %param.19) | copy-start | bytes 1179652
  7.2 107.2 %all-gather.2.cloned.1.call-start = ((), (), s32[]{:S(2)}) async-start(), calls=%async_computation.5 | async-start | bytes 6389760 | tf_op jit(solution)/shard_map/all_gather | solution.py:135
  11.2 1.6 copy-start.2
  15.6 102.5 %all-to-all-start.2 = ((bf16[16,832,128]{2,1,0:T(8,128)(2,1)}), bf16[16,832,128]{2,1,0:T(8,128)(2,1)}, u32[]{:S(2)}, u32[]{:S(2)}) async-start(bf16[16,832,128]{2,1,0:T(8,128)(2,1)} %pad_maximum_fusion.2), calls=%async_computation.2 | async-start | bytes 6815744 | tf_op jit(solution)/shard_map/all_to_all | solution.py:127
  114.3 101.1 %collective-permute-start = (bf16[1024,3072]{1,0:T(8,128)(2,1)}, bf16[1024,3072]{1,0:T(8,128)(2,1)}, u32[]{:S(2)}, u32[]{:S(2)}) collective-permute-start(bf16[1024,3072]{1,0:T(8,128)(2,1)} %all-gather.2.cloned.1.call-done), channel_id=1, source_target_pairs={{0,64},{64,0},{1,65},{65,1},{2,66},{66,2},{3,67},{67,3},{4,68},{68... | collective-permute-start | bytes 18874376 | tf_op jit(solution)/shard_map/ppermute | solution.py:23
  114.3 1.5 copy-start.1
  116.1 7.6 %copy-start.7 = (s32[2]{0:T(128)S(1)}, s32[2]{0:T(128)}, u32[]{:S(2)}) copy-start(s32[2]{0:T(128)} %param.12) | copy-start | bytes 28
  116.1 8.2 %copy-start.3 = (f32[1,2,3,3072]{3,1,2,0:T(2,128)S(1)}, f32[1,2,3,3072]{3,1,2,0:T(2,128)}, u32[]{:S(2)}) copy-start(f32[1,2,3,3072]{3,1,2,0:T(2,128)} %param.15) | copy-start | bytes 221188
  118.1 58.8 %all-to-all-start = ((bf16[16,832,128]{2,1,0:T(8,128)(2,1)}), bf16[16,832,128]{2,1,0:T(8,128)(2,1)}, u32[]{:S(2)}, u32[]{:S(2)}) async-start(bf16[16,832,128]{2,1,0:T(8,128)(2,1)} %pad_maximum_fusion.1), calls=%async_computation | async-start | bytes 6815744 | tf_op jit(solution)/shard_map/all_to_all | solution.py:127
  176.9 48.8 %all-to-all-start.3 = ((bf16[16,256,128]{2,1,0:T(8,128)(2,1)}), bf16[16,256,128]{2,1,0:T(8,128)(2,1)S(1)}, u32[]{:S(2)}, u32[]{:S(2)}) async-start(bf16[16,256,128]{2,1,0:T(8,128)(2,1)} %get-tuple-element.8), calls=%async_computation.3 | async-start | bytes 2097152 | tf_op jit(solution)/shard_map/all_to_all | solution.py:131
  225.7 23.6 %all-to-all-start.1 = ((bf16[16,256,128]{2,1,0:T(8,128)(2,1)}), bf16[16,256,128]{2,1,0:T(8,128)(2,1)S(1)}, u32[]{:S(2)}, u32[]{:S(2)}) async-start(bf16[16,256,128]{2,1,0:T(8,128)(2,1)} %get-tuple-element.7), calls=%async_computation.1 | async-start | bytes 2097152 | tf_op jit(solution)/shard_map/all_to_all | solution.py:131
  260.1 1.8 copy-start.9
  260.1 1.8 copy-start.6
  260.1 2.4 copy-start.5
  260.1 3.0 %copy-start.4 = (f32[2,256,32]{1,2,0:T(8,128)S(1)}, f32[2,256,32]{1,2,0:T(8,128)}, u32[]{:S(2)}) copy-start(f32[2,256,32]{1,2,0:T(8,128)} %param.17) | copy-start | bytes 196612
  260.1 3.0 %copy-start.8 = (f32[2]{0:T(128)S(1)}, f32[2]{0:T(128)}, u32[]{:S(2)}) copy-start(f32[2]{0:T(128)} %param.14) | copy-start | bytes 28
  261.8 1.3 collective-permute-start.1
Sparse Core Ops, SparseCore 0:
  10.8 103.4 all-gather.1

commit v8 on v6

--- a/solution.py
+++ b/solution.py
@@ -130,25 +130,25 @@
         head_rows, top = attention(text_len[p : p + 1], buf, img_dev, txt_dev)
         outs.append(lax.all_to_all(head_rows, "seq", 0, 0, tiled=True)[:, None])
         maxes.append(top)
-    token_rows = jnp.concatenate(outs, axis=1)
     local_max = jnp.concatenate(maxes)
     weight = lax.all_gather(proj_weight, ("cfg", "req", "seq"), axis=0, tiled=True)
-    projected = jnp.einsum(
-        "hptd,hdo->pto",
-        token_rows,
-        weight.reshape(seq, HEADS // seq * HD, weight.shape[1]),
-        preferred_element_type=jnp.float32,
-    )
+    weight = weight.reshape(seq, HEADS // seq * HD, weight.shape[1])
     mod_rows = modulation[0]
-    hidden = img_hidden[0].astype(jnp.float32) + mod_rows[:, 0][:, None, :] * projected
-    average = jnp.mean(hidden, axis=2, keepdims=True)
-    centred = hidden - average
-    variance = jnp.mean(centred * centred, axis=2, keepdims=True)
-    normed = (
-        centred / jnp.sqrt(variance + norm_eps) * (1.0 + mod_rows[:, 1][:, None, :])
-        + mod_rows[:, 2][:, None, :]
-    ).astype(jnp.bfloat16)
-    velocity = jnp.einsum("ptd,dc->ptc", normed, final_weight, preferred_element_type=jnp.float32)
+    velocities = []
+    for p in range(local_prompts):
+        projected = jnp.einsum(
+            "htd,hdo->to", outs[p][:, 0], weight, preferred_element_type=jnp.float32
+        )
+        hidden = img_hidden[0, p].astype(jnp.float32) + mod_rows[p, 0][None, :] * projected
+        average = jnp.mean(hidden, axis=1, keepdims=True)
+        centred = hidden - average
+        variance = jnp.mean(centred * centred, axis=1, keepdims=True)
+        normed = (
+            centred / jnp.sqrt(variance + norm_eps) * (1.0 + mod_rows[p, 1][None, :])
+            + mod_rows[p, 2][None, :]
+        ).astype(jnp.bfloat16)
+        velocities.append(jnp.dot(normed, final_weight, preferred_element_type=jnp.float32))
+    velocity = jnp.stack(velocities)
     half_chan = latents.shape[2]
     copy_pos = lax.axis_index("cfg")
     own_part = lax.dynamic_slice_in_dim(velocity, copy_pos * half_chan, half_chan, 2)

time: 239 us -> 239 us (level)
  blocking collectives: 10.4 us -> 0 us
  matrix products: 11.5 us -> 15.9 us
  starting transfers between devices: 30.9 us -> 34.4 us
    all_to_all x1 -> x0, blocking collectives: 10.4 us -> none  [shards(): lax.all_to_all(jnp.broadcast_to(stats[None], (seq, stats.shape[0])), 'seq...]
    all_to_all x2, waiting for transfers between devices: 13.9 us -> 5.71 us  [shards(): outs.append(lax.all_to_all(head_rows, 'seq', 0, 0, tiled=True)[:, None])]
    all_to_all x0 -> x1, waiting for transfers between devices: none -> 6.81 us  [shards(): lax.all_to_all(jnp.broadcast_to(stats[None], (seq, stats.shape[0])), 'seq...]
    dot_general x2 -> x4, matrix products: 11.5 us -> 15.9 us  [the longest x2 14.4 us: shards(): jnp.einsum('htd,hdo->to', outs[p][:, 0], weight, preferred_element_type=j...]
    all_to_all x0 -> x1, starting transfers between devices: none -> 3.42 us  [shards(): lax.all_to_all(jnp.broadcast_to(stats[None], (seq, stats.shape[0])), 'seq...]
    unnamed x26 -> x38, local copies, waits for them, and re-layouts: 5.58 us -> 6.14 us
  transfers between devices with their start and end apart: 6 -> 7, of which waited for: 3 -> 4; matrix products, arithmetic and copies ran while one was open for 6% -> 10% of each run, Pallas kernels for 29% -> 29%
where the time goes in v8:
time: 239 us; the launch traced here: 238 us
  waiting for transfers between devices  83.9 us (35%)
  Pallas kernels  68.4 us (29%)
  starting transfers between devices  34.4 us (14%)
  matrix products  15.9 us (7%)
  between operations  14.4 us (6%)
  other arithmetic  11.6 us (5%)
  local copies, waits for them, and re-layouts  9.24 us (4%)
    all_to_all x2, waiting for transfers between devices, shards(): lax.all_to_all(jnp.concatenate([joined, text_rows], axis=1), 'seq', 0, 0,...  70.7 us
    pallas_call x2, Pallas kernels, attention(): pl.pallas_call(attn_kernel, grid_spec=grid_spec, out_shape=[jax.ShapeDtyp...  68.4 us
    all_to_all x2, starting transfers between devices, shards(): outs.append(lax.all_to_all(head_rows, 'seq', 0, 0, tiled=True)[:, None])  18.2 us
    dot_general x2, matrix products, shards(): jnp.einsum('htd,hdo->to', outs[p][:, 0], weight, preferred_element_type=j...  14.4 us
    all_to_all x2, starting transfers between devices, shards(): lax.all_to_all(jnp.concatenate([joined, text_rows], axis=1), 'seq', 0, 0,...  12.6 us
    all_to_all x1, waiting for transfers between devices, shards(): lax.all_to_all(jnp.broadcast_to(stats[None], (seq, stats.shape[0])), 'seq...  6.81 us
    unnamed x38, local copies, waits for them, and re-layouts  6.14 us
    all_to_all x2, waiting for transfers between devices, shards(): outs.append(lax.all_to_all(head_rows, 'seq', 0, 0, tiled=True)[:, None])  5.71 us
  transfers between devices with their start and end apart: 7, of which 4 were waited for; matrix products, arithmetic and copies ran while one was open for 10% of the time, Pallas kernels for 29%

profile of v8, /device:TPU:8, one launch (start us, length us, event | category | flops | bytes accessed | tf_op | source)
XLA Modules:
  0.0 237.9 jit_solution(8848434995560859754)
XLA Ops:
  7.2 0.0 copy-start
  7.2 0.0 all-gather.2.cloned.1.call-start
  7.2 0.7 all-gather.2.cloned.1.call-update
  7.9 3.3 %slice_bitcast_fusion = (bf16[32,8,48,128]{3,1,2,0:T(8,128)(2,1)S(1)}, bf16[32,8,48,128]{3,1,2,0:T(8,128)(2,1)S(1)}) fusion(bf16[1,2,256,6144]{3,2,1,0:T(8,128)(2,1)} %param.10), kind=kLoop, calls=%fused_computation.10 | loop fusion | bytes 12582912
  11.2 0.7 copy.24
  11.9 0.0 copy-start.3
  11.9 0.8 copy.19
  12.7 0.2 copy-done.3
  12.9 0.7 slice_bitcast_fusion.2
  13.7 0.1 copy.20
  13.8 2.0 pad_maximum_fusion.1
  15.8 7.9 %all-to-all-start.2 = ((bf16[16,832,128]{2,1,0:T(8,128)(2,1)}), bf16[16,832,128]{2,1,0:T(8,128)(2,1)}, u32[]{:S(2)}, u32[]{:S(2)}) async-start(bf16[16,832,128]{2,1,0:T(8,128)(2,1)} %pad_maximum_fusion.1), calls=%async_computation.2 | async-start | bytes 6815744 | tf_op jit(solution)/shard_map/all_to_all | solution.py:127
  23.8 0.7 copy.22
  24.5 0.0 copy-start.2
  24.5 0.8 copy.17
  25.3 0.1 copy-done.2
  25.5 0.1 copy.18
  25.6 2.0 pad_maximum_fusion
  27.6 48.9 %all-to-all-done.2.q_ref.kt_ref.vt_ref.ki_ref.vi_ref = bf16[16,832,128]{2,1,0:T(8,128)(2,1)} async-done(((bf16[16,832,128]{2,1,0:T(8,128)(2,1)}), bf16[16,832,128]{2,1,0:T(8,128)(2,1)}, u32[]{:S(2)}, u32[]{:S(2)}) %all-to-all-start.2) | async-done | bytes 3407904 | tf_op jit(solution)/shard_map/all_to_all | solution.py:127
  76.6 4.7 %all-to-all-start = ((bf16[16,832,128]{2,1,0:T(8,128)(2,1)}), bf16[16,832,128]{2,1,0:T(8,128)(2,1)}, u32[]{:S(2)}, u32[]{:S(2)}) async-start(bf16[16,832,128]{2,1,0:T(8,128)(2,1)} %pad_maximum_fusion), calls=%async_computation | async-start | bytes 6815744 | tf_op jit(solution)/shard_map/all_to_all | solution.py:127
  81.3 0.0 copy-done.12
  81.3 0.6 fusion.10
  81.9 34.3 %shard_map.122 = (bf16[16,256,128]{2,1,0:T(8,128)(2,1)}, f32[4,8,128]{2,1,0:T(8,128)}) custom-call(s32[1]{0:T(128)} %get-tuple-element.25.tl_ref, bf16[16,832,128]{2,1,0:T(8,128)(2,1)} %all-to-all-done.2.q_ref.kt_ref.vt_ref.ki_ref.vi_ref, bf16[16,832,128]{2,1,0:T(8,128)(2,1)} %all-to-all-done.2.q_ref.kt_ref.vt_ref.ki_ref.vi_ref, ...), custom_call_target="tpu_custom_call" | custom-call | flops 9663676416 | bytes 4456448 | tf_op jit(solution)/shard_map/pallas_call | solution.py:87
  116.2 21.8 %all-to-all-done.q_ref.kt_ref.vt_ref.ki_ref.vi_ref = bf16[16,832,128]{2,1,0:T(8,128)(2,1)} async-done(((bf16[16,832,128]{2,1,0:T(8,128)(2,1)}), bf16[16,832,128]{2,1,0:T(8,128)(2,1)}, u32[]{:S(2)}, u32[]{:S(2)}) %all-to-all-start) | async-done | bytes 3407904 | tf_op jit(solution)/shard_map/all_to_all | solution.py:127
  137.9 10.9 %all-to-all-start.3 = ((bf16[16,256,128]{2,1,0:T(8,128)(2,1)}), bf16[16,256,128]{2,1,0:T(8,128)(2,1)S(1)}, u32[]{:S(2)}, u32[]{:S(2)}) async-start(bf16[16,256,128]{2,1,0:T(8,128)(2,1)} %get-tuple-element.8), calls=%async_computation.3 | async-start | bytes 2097152 | tf_op jit(solution)/shard_map/all_to_all | solution.py:131
  148.9 0.0 copy-done.5
  148.9 0.7 slice_add_fusion
  149.6 34.1 %shard_map.121 = (bf16[16,256,128]{2,1,0:T(8,128)(2,1)}, f32[4,8,128]{2,1,0:T(8,128)}) custom-call(s32[1]{0:T(128)} %get-tuple-element.26.tl_ref, bf16[16,832,128]{2,1,0:T(8,128)(2,1)} %all-to-all-done.q_ref.kt_ref.vt_ref.ki_ref.vi_ref, bf16[16,832,128]{2,1,0:T(8,128)(2,1)} %all-to-all-done.q_ref.kt_ref.vt_ref.ki_ref.vi_ref, ...), custom_call_target="tpu_custom_call" | custom-call | flops 9663676416 | bytes 4456448 | tf_op jit(solution)/shard_map/pallas_call | solution.py:87
  183.7 0.0 all-to-all-done.3
  183.7 0.0 copy-start.1
  183.7 7.3 %all-to-all-start.1 = ((bf16[16,256,128]{2,1,0:T(8,128)(2,1)}), bf16[16,256,128]{2,1,0:T(8,128)(2,1)}, u32[]{:S(2)}, u32[]{:S(2)}) async-start(bf16[16,256,128]{2,1,0:T(8,128)(2,1)} %get-tuple-element.7), calls=%async_computation.1 | async-start | bytes 2097152 | tf_op jit(solution)/shard_map/all_to_all | solution.py:131
  191.0 0.0 all-gather.2.cloned.1.call-done
  191.0 0.0 copy-done.1
  191.0 7.2 %fusion.12 = (f32[256]{0:T(256)S(1)}, f32[256,3072]{1,0:T(8,128)S(1)}) fusion(bf16[16,256,128]{2,1,0:T(8,128)(2,1)} %copy-done.1, bf16[16,128,3072]{2,1,0:T(8,128)(2,1)} %bitcast.95, f32[3072]{0:T(1024)} %bitcast.92, bf16[1,2,256,3072]{3,2,1,0:T(8,128)(2,1)} %param.16), kind=kOutput, calls=%fused_computation.42 | convolution fusion | flops 3224370944 | bytes 18363392 | tf_op jit(solution)/shard_map/htd,hdo->to/dot_general | solution.py:139
  198.3 0.5 multiply_reduce_fusion
  198.7 0.6 add_sqrt_fusion
  199.3 5.7 %all-to-all-done.1 = bf16[16,256,128]{2,1,0:T(8,128)(2,1)} async-done(((bf16[16,256,128]{2,1,0:T(8,128)(2,1)}), bf16[16,256,128]{2,1,0:T(8,128)(2,1)}, u32[]{:S(2)}, u32[]{:S(2)}) %all-to-all-start.1) | async-done | bytes 1048608 | tf_op jit(solution)/shard_map/all_to_all | solution.py:131
  205.1 7.2 %fusion.11 = (f32[256]{0:T(256)S(1)}, f32[256,3072]{1,0:T(8,128)S(1)}) fusion(bf16[16,256,128]{2,1,0:T(8,128)(2,1)} %all-to-all-done.1, bf16[16,128,3072]{2,1,0:T(8,128)(2,1)} %bitcast.96, f32[3072]{0:T(1024)} %bitcast.91, bf16[1,2,256,3072]{3,2,1,0:T(8,128)(2,1)} %param.16), kind=kOutput, calls=%fused_computation.41 | convolution fusion | flops 3224370944 | bytes 18363392 | tf_op jit(solution)/shard_map/htd,hdo->to/dot_general | solution.py:139
  212.2 0.0 copy-start.10
  212.3 0.5 multiply_reduce_fusion.1
  212.8 0.2 copy-done.10
  213.0 0.0 copy-done.11
  213.0 0.7 fusion.6
  213.7 0.0 copy-start.4
  213.8 0.0 copy-start.15
  213.8 0.0 copy-start.14
  213.8 0.0 copy-start.6
  213.8 0.8 fusion.7
  214.6 0.0 copy-done.4
  214.6 0.1 collective-permute-start
  214.8 0.6 reduce_max.27
  215.4 0.0 copy-done.7
  215.4 0.6 reduce_max.28
  216.0 0.0 collective-permute-done
  216.0 0.9 multiply_reduce_fusion.2
  216.9 1.4 pad_maximum_fusion.2
  218.3 0.6 broadcast_in_dim.8
  218.9 3.4 %all-to-all-start.4 = ((f32[16,1,4]{2,1,0:T(1,128)}), f32[16,1,4]{2,1,0:T(1,128)S(1)}, u32[]{:S(2)}, u32[]{:S(2)}) async-start(f32[16,1,4]{2,1,0:T(1,128)} %broadcast_in_dim.8), calls=%async_computation.4 | async-start | bytes 16384 | tf_op jit(solution)/shard_map/all_to_all | solution.py:163
  222.3 0.0 copy-done.6
  222.3 0.7 multiply_add_fusion
  223.0 6.8 %all-to-all-done.4 = f32[16,1,4]{2,1,0:T(1,128)S(1)} async-done(((f32[16,1,4]{2,1,0:T(1,128)}), f32[16,1,4]{2,1,0:T(1,128)S(1)}, u32[]{:S(2)}, u32[]{:S(2)}) %all-to-all-start.4) | async-done | bytes 288 | tf_op jit(solution)/shard_map/all_to_all | solution.py:163
  229.8 0.1 copy.21
  229.9 0.6 slice_reduce_fusion
  230.5 0.5 sqrt_bitcast_fusion
  (20 shorter events, 0.2 us)
Async XLA Ops:
  7.2 205.6 %copy-start = (bf16[3072,64]{0,1:T(8,128)(2,1)S(1)}, bf16[3072,64]{0,1:T(8,128)(2,1)}, u32[]{:S(2)}) copy-start(bf16[3072,64]{0,1:T(8,128)(2,1)} %param.19) | copy-start | bytes 1179652
  7.2 183.8 %all-gather.2.cloned.1.call-start = ((), (), s32[]{:S(2)}) async-start(), calls=%async_computation.5 | async-start | bytes 12681216 | tf_op jit(solution)/shard_map/all_gather | solution.py:134
  11.9 1.0 copy-start.3
  15.8 60.7 %all-to-all-start.2 = ((bf16[16,832,128]{2,1,0:T(8,128)(2,1)}), bf16[16,832,128]{2,1,0:T(8,128)(2,1)}, u32[]{:S(2)}, u32[]{:S(2)}) async-start(bf16[16,832,128]{2,1,0:T(8,128)(2,1)} %pad_maximum_fusion.1), calls=%async_computation.2 | async-start | bytes 6815744 | tf_op jit(solution)/shard_map/all_to_all | solution.py:127
  24.5 1.0 copy-start.2
  27.6 53.6 %copy-start.12 = (s32[2]{0:T(128)S(1)}, s32[2]{0:T(128)}, u32[]{:S(2)}) copy-start(s32[2]{0:T(128)} %param.12) | copy-start | bytes 28
  76.6 61.4 %all-to-all-start = ((bf16[16,832,128]{2,1,0:T(8,128)(2,1)}), bf16[16,832,128]{2,1,0:T(8,128)(2,1)}, u32[]{:S(2)}, u32[]{:S(2)}) async-start(bf16[16,832,128]{2,1,0:T(8,128)(2,1)} %pad_maximum_fusion), calls=%async_computation | async-start | bytes 6815744 | tf_op jit(solution)/shard_map/all_to_all | solution.py:127
  81.9 67.0 %copy-start.5 = (f32[1,2,3,3072]{3,1,2,0:T(2,128)S(1)}, f32[1,2,3,3072]{3,1,2,0:T(2,128)}, u32[]{:S(2)}) copy-start(f32[1,2,3,3072]{3,1,2,0:T(2,128)} %param.15) | copy-start | bytes 221188
  137.9 45.7 %all-to-all-start.3 = ((bf16[16,256,128]{2,1,0:T(8,128)(2,1)}), bf16[16,256,128]{2,1,0:T(8,128)(2,1)S(1)}, u32[]{:S(2)}, u32[]{:S(2)}) async-start(bf16[16,256,128]{2,1,0:T(8,128)(2,1)} %get-tuple-element.8), calls=%async_computation.3 | async-start | bytes 2097152 | tf_op jit(solution)/shard_map/all_to_all | solution.py:131
  183.7 7.3 %copy-start.1 = (bf16[16,256,128]{2,1,0:T(8,128)(2,1)}, bf16[16,256,128]{2,1,0:T(8,128)(2,1)S(1)}, u32[]{:S(2)}) copy-start(bf16[16,256,128]{2,1,0:T(8,128)(2,1)S(1)} %all-to-all-done.3) | copy-start | bytes 3145732
  183.7 21.3 %all-to-all-start.1 = ((bf16[16,256,128]{2,1,0:T(8,128)(2,1)}), bf16[16,256,128]{2,1,0:T(8,128)(2,1)}, u32[]{:S(2)}, u32[]{:S(2)}) async-start(bf16[16,256,128]{2,1,0:T(8,128)(2,1)} %get-tuple-element.7), calls=%async_computation.1 | async-start | bytes 2097152 | tf_op jit(solution)/shard_map/all_to_all | solution.py:131
  212.2 0.7 copy-start.10
  212.3 0.7 copy-start.11
  212.3 0.7 copy-start.13
  213.0 0.8 copy-start.9
  213.7 0.9 copy-start.4
  213.8 1.0 copy-start.15
  213.8 1.0 copy-start.8
  213.8 1.6 copy-start.7
  213.8 2.2 copy-start.14
  213.8 8.5 %copy-start.6 = (f32[2,256,32]{1,2,0:T(8,128)S(1)}, f32[2,256,32]{1,2,0:T(8,128)}, u32[]{:S(2)}) copy-start(f32[2,256,32]{1,2,0:T(8,128)} %param.17) | copy-start | bytes 196612
  214.6 1.3 collective-permute-start
  218.9 10.9 %all-to-all-start.4 = ((f32[16,1,4]{2,1,0:T(1,128)}), f32[16,1,4]{2,1,0:T(1,128)S(1)}, u32[]{:S(2)}, u32[]{:S(2)}) async-start(f32[16,1,4]{2,1,0:T(1,128)} %broadcast_in_dim.8), calls=%async_computation.4 | async-start | bytes 16384 | tf_op jit(solution)/shard_map/all_to_all | solution.py:163
Sparse Core Ops, SparseCore 0:
  11.1 136.6 all-gather.1

commit v9 on v8

--- a/solution.py
+++ b/solution.py
@@ -12,7 +12,7 @@
 HD = 128
 STEPS = 4
 BQ = 1024
-CK = 512
+CK = 2048
 
 
 time_shift = 1.15

time: 239 us -> 237 us (level)
  Pallas kernels: 68.4 us -> 65.9 us
    pallas_call x2, Pallas kernels: 68.4 us -> 65.9 us  [attention(): pl.pallas_call(attn_kernel, grid_spec=grid_spec, out_shape=[jax.ShapeDtyp...]
  transfers between devices with their start and end apart: 7 -> 7, of which waited for: 4 -> 4; matrix products, arithmetic and copies ran while one was open for 10% -> 10% of each run, Pallas kernels for 29% -> 28%
where the time goes in v9:
time: 237 us
  waiting for transfers between devices  85.2 us (36%)
  Pallas kernels  65.9 us (28%)
  starting transfers between devices  34.4 us (15%)
  matrix products  15.9 us (7%)
  between operations  14.4 us (6%)
  other arithmetic  11.6 us (5%)
  local copies, waits for them, and re-layouts  9.24 us (4%)
    all_to_all x2, waiting for transfers between devices, shards(): lax.all_to_all(jnp.concatenate([joined, text_rows], axis=1), 'seq', 0, 0,...  72 us
    pallas_call x2, Pallas kernels, attention(): pl.pallas_call(attn_kernel, grid_spec=grid_spec, out_shape=[jax.ShapeDtyp...  65.9 us
    all_to_all x2, starting transfers between devices, shards(): outs.append(lax.all_to_all(head_rows, 'seq', 0, 0, tiled=True)[:, None])  18.2 us
    dot_general x2, matrix products, shards(): jnp.einsum('htd,hdo->to', outs[p][:, 0], weight, preferred_element_type=j...  14.4 us
    all_to_all x2, starting transfers between devices, shards(): lax.all_to_all(jnp.concatenate([joined, text_rows], axis=1), 'seq', 0, 0,...  12.6 us
    all_to_all x1, waiting for transfers between devices, shards(): lax.all_to_all(jnp.broadcast_to(stats[None], (seq, stats.shape[0])), 'seq...  6.81 us
    unnamed x38, local copies, waits for them, and re-layouts  6.14 us
    all_to_all x2, waiting for transfers between devices, shards(): outs.append(lax.all_to_all(head_rows, 'seq', 0, 0, tiled=True)[:, None])  5.71 us
  transfers between devices with their start and end apart: 7, of which 4 were waited for; matrix products, arithmetic and copies ran while one was open for 10% of the time, Pallas kernels for 28%

profile of v9, /device:TPU:8, one launch (start us, length us, event | category | flops | bytes accessed | tf_op | source)
XLA Modules:
  0.0 236.6 jit_solution(5396256200550309369)
XLA Ops:
  7.2 0.0 copy-start
  7.2 0.0 all-gather.2.cloned.1.call-start
  7.2 0.7 all-gather.2.cloned.1.call-update
  7.9 3.3 %slice_bitcast_fusion = (bf16[32,8,48,128]{3,1,2,0:T(8,128)(2,1)S(1)}, bf16[32,8,48,128]{3,1,2,0:T(8,128)(2,1)S(1)}) fusion(bf16[1,2,256,6144]{3,2,1,0:T(8,128)(2,1)} %param.10), kind=kLoop, calls=%fused_computation.10 | loop fusion | bytes 12582912
  11.2 0.7 copy.24
  11.9 0.0 copy-start.3
  11.9 0.8 copy.19
  12.7 0.2 copy-done.3
  12.9 0.7 slice_bitcast_fusion.2
  13.7 0.1 copy.20
  13.8 2.0 pad_maximum_fusion.1
  15.8 7.9 %all-to-all-start.2 = ((bf16[16,832,128]{2,1,0:T(8,128)(2,1)}), bf16[16,832,128]{2,1,0:T(8,128)(2,1)}, u32[]{:S(2)}, u32[]{:S(2)}) async-start(bf16[16,832,128]{2,1,0:T(8,128)(2,1)} %pad_maximum_fusion.1), calls=%async_computation.2 | async-start | bytes 6815744 | tf_op jit(solution)/shard_map/all_to_all | solution.py:127
  23.8 0.7 copy.22
  24.5 0.0 copy-start.2
  24.5 0.8 copy.17
  25.3 0.1 copy-done.2
  25.5 0.1 copy.18
  25.6 2.0 pad_maximum_fusion
  27.6 48.9 %all-to-all-done.2.q_ref.kt_ref.vt_ref.ki_ref.vi_ref = bf16[16,832,128]{2,1,0:T(8,128)(2,1)} async-done(((bf16[16,832,128]{2,1,0:T(8,128)(2,1)}), bf16[16,832,128]{2,1,0:T(8,128)(2,1)}, u32[]{:S(2)}, u32[]{:S(2)}) %all-to-all-start.2) | async-done | bytes 3407904 | tf_op jit(solution)/shard_map/all_to_all | solution.py:127
  76.6 4.7 %all-to-all-start = ((bf16[16,832,128]{2,1,0:T(8,128)(2,1)}), bf16[16,832,128]{2,1,0:T(8,128)(2,1)}, u32[]{:S(2)}, u32[]{:S(2)}) async-start(bf16[16,832,128]{2,1,0:T(8,128)(2,1)} %pad_maximum_fusion), calls=%async_computation | async-start | bytes 6815744 | tf_op jit(solution)/shard_map/all_to_all | solution.py:127
  81.3 0.0 copy-done.12
  81.3 0.6 fusion.10
  81.9 33.0 %shard_map.122 = (bf16[16,256,128]{2,1,0:T(8,128)(2,1)}, f32[4,8,128]{2,1,0:T(8,128)}) custom-call(s32[1]{0:T(128)} %get-tuple-element.25.tl_ref, bf16[16,832,128]{2,1,0:T(8,128)(2,1)} %all-to-all-done.2.q_ref.kt_ref.vt_ref.ki_ref.vi_ref, bf16[16,832,128]{2,1,0:T(8,128)(2,1)} %all-to-all-done.2.q_ref.kt_ref.vt_ref.ki_ref.vi_ref, ...), custom_call_target="tpu_custom_call" | custom-call | flops 9663676416 | bytes 4456448 | tf_op jit(solution)/shard_map/pallas_call | solution.py:87
  114.9 23.1 %all-to-all-done.q_ref.kt_ref.vt_ref.ki_ref.vi_ref = bf16[16,832,128]{2,1,0:T(8,128)(2,1)} async-done(((bf16[16,832,128]{2,1,0:T(8,128)(2,1)}), bf16[16,832,128]{2,1,0:T(8,128)(2,1)}, u32[]{:S(2)}, u32[]{:S(2)}) %all-to-all-start) | async-done | bytes 3407904 | tf_op jit(solution)/shard_map/all_to_all | solution.py:127
  137.9 10.9 %all-to-all-start.3 = ((bf16[16,256,128]{2,1,0:T(8,128)(2,1)}), bf16[16,256,128]{2,1,0:T(8,128)(2,1)S(1)}, u32[]{:S(2)}, u32[]{:S(2)}) async-start(bf16[16,256,128]{2,1,0:T(8,128)(2,1)} %get-tuple-element.8), calls=%async_computation.3 | async-start | bytes 2097152 | tf_op jit(solution)/shard_map/all_to_all | solution.py:131
  148.9 0.0 copy-done.5
  148.9 0.7 slice_add_fusion
  149.6 32.8 %shard_map.121 = (bf16[16,256,128]{2,1,0:T(8,128)(2,1)}, f32[4,8,128]{2,1,0:T(8,128)}) custom-call(s32[1]{0:T(128)} %get-tuple-element.26.tl_ref, bf16[16,832,128]{2,1,0:T(8,128)(2,1)} %all-to-all-done.q_ref.kt_ref.vt_ref.ki_ref.vi_ref, bf16[16,832,128]{2,1,0:T(8,128)(2,1)} %all-to-all-done.q_ref.kt_ref.vt_ref.ki_ref.vi_ref, ...), custom_call_target="tpu_custom_call" | custom-call | flops 9663676416 | bytes 4456448 | tf_op jit(solution)/shard_map/pallas_call | solution.py:87
  182.4 0.0 all-to-all-done.3
  182.4 0.0 copy-start.1
  182.4 7.3 %all-to-all-start.1 = ((bf16[16,256,128]{2,1,0:T(8,128)(2,1)}), bf16[16,256,128]{2,1,0:T(8,128)(2,1)}, u32[]{:S(2)}, u32[]{:S(2)}) async-start(bf16[16,256,128]{2,1,0:T(8,128)(2,1)} %get-tuple-element.7), calls=%async_computation.1 | async-start | bytes 2097152 | tf_op jit(solution)/shard_map/all_to_all | solution.py:131
  189.7 0.0 all-gather.2.cloned.1.call-done
  189.8 0.0 copy-done.1
  189.8 7.2 %fusion.12 = (f32[256]{0:T(256)S(1)}, f32[256,3072]{1,0:T(8,128)S(1)}) fusion(bf16[16,256,128]{2,1,0:T(8,128)(2,1)} %copy-done.1, bf16[16,128,3072]{2,1,0:T(8,128)(2,1)} %bitcast.95, f32[3072]{0:T(1024)} %bitcast.92, bf16[1,2,256,3072]{3,2,1,0:T(8,128)(2,1)} %param.16), kind=kOutput, calls=%fused_computation.42 | convolution fusion | flops 3224370944 | bytes 18363392 | tf_op jit(solution)/shard_map/htd,hdo->to/dot_general | solution.py:139
  197.0 0.5 multiply_reduce_fusion
  197.4 0.6 add_sqrt_fusion
  198.1 5.7 %all-to-all-done.1 = bf16[16,256,128]{2,1,0:T(8,128)(2,1)} async-done(((bf16[16,256,128]{2,1,0:T(8,128)(2,1)}), bf16[16,256,128]{2,1,0:T(8,128)(2,1)}, u32[]{:S(2)}, u32[]{:S(2)}) %all-to-all-start.1) | async-done | bytes 1048608 | tf_op jit(solution)/shard_map/all_to_all | solution.py:131
  203.8 7.2 %fusion.11 = (f32[256]{0:T(256)S(1)}, f32[256,3072]{1,0:T(8,128)S(1)}) fusion(bf16[16,256,128]{2,1,0:T(8,128)(2,1)} %all-to-all-done.1, bf16[16,128,3072]{2,1,0:T(8,128)(2,1)} %bitcast.96, f32[3072]{0:T(1024)} %bitcast.91, bf16[1,2,256,3072]{3,2,1,0:T(8,128)(2,1)} %param.16), kind=kOutput, calls=%fused_computation.41 | convolution fusion | flops 3224370944 | bytes 18363392 | tf_op jit(solution)/shard_map/htd,hdo->to/dot_general | solution.py:139
  211.0 0.0 copy-start.10
  211.0 0.5 multiply_reduce_fusion.1
  211.5 0.2 copy-done.10
  211.7 0.0 copy-done.11
  211.7 0.7 fusion.6
  212.5 0.0 copy-start.4
  212.5 0.0 copy-start.15
  212.5 0.0 copy-start.14
  212.5 0.0 copy-start.6
  212.5 0.8 fusion.7
  213.3 0.0 copy-done.4
  213.3 0.1 collective-permute-start
  213.5 0.6 reduce_max.27
  214.1 0.0 copy-done.7
  214.1 0.6 reduce_max.28
  214.7 0.0 collective-permute-done
  214.7 0.9 multiply_reduce_fusion.2
  215.6 1.4 pad_maximum_fusion.2
  217.0 0.6 broadcast_in_dim.8
  217.6 3.4 %all-to-all-start.4 = ((f32[16,1,4]{2,1,0:T(1,128)}), f32[16,1,4]{2,1,0:T(1,128)S(1)}, u32[]{:S(2)}, u32[]{:S(2)}) async-start(f32[16,1,4]{2,1,0:T(1,128)} %broadcast_in_dim.8), calls=%async_computation.4 | async-start | bytes 16384 | tf_op jit(solution)/shard_map/all_to_all | solution.py:163
  221.0 0.0 copy-done.6
  221.0 0.7 multiply_add_fusion
  221.7 6.8 %all-to-all-done.4 = f32[16,1,4]{2,1,0:T(1,128)S(1)} async-done(((f32[16,1,4]{2,1,0:T(1,128)}), f32[16,1,4]{2,1,0:T(1,128)S(1)}, u32[]{:S(2)}, u32[]{:S(2)}) %all-to-all-start.4) | async-done | bytes 288 | tf_op jit(solution)/shard_map/all_to_all | solution.py:163
  228.5 0.1 copy.21
  228.6 0.6 slice_reduce_fusion
  229.3 0.5 sqrt_bitcast_fusion
  (20 shorter events, 0.2 us)
Async XLA Ops:
  7.2 204.3 %copy-start = (bf16[3072,64]{0,1:T(8,128)(2,1)S(1)}, bf16[3072,64]{0,1:T(8,128)(2,1)}, u32[]{:S(2)}) copy-start(bf16[3072,64]{0,1:T(8,128)(2,1)} %param.19) | copy-start | bytes 1179652
  7.2 182.6 %all-gather.2.cloned.1.call-start = ((), (), s32[]{:S(2)}) async-start(), calls=%async_computation.5 | async-start | bytes 12681216 | tf_op jit(solution)/shard_map/all_gather | solution.py:134
  11.9 1.0 copy-start.3
  15.8 60.7 %all-to-all-start.2 = ((bf16[16,832,128]{2,1,0:T(8,128)(2,1)}), bf16[16,832,128]{2,1,0:T(8,128)(2,1)}, u32[]{:S(2)}, u32[]{:S(2)}) async-start(bf16[16,832,128]{2,1,0:T(8,128)(2,1)} %pad_maximum_fusion.1), calls=%async_computation.2 | async-start | bytes 6815744 | tf_op jit(solution)/shard_map/all_to_all | solution.py:127
  24.5 1.0 copy-start.2
  27.6 53.6 %copy-start.12 = (s32[2]{0:T(128)S(1)}, s32[2]{0:T(128)}, u32[]{:S(2)}) copy-start(s32[2]{0:T(128)} %param.12) | copy-start | bytes 28
  76.6 61.4 %all-to-all-start = ((bf16[16,832,128]{2,1,0:T(8,128)(2,1)}), bf16[16,832,128]{2,1,0:T(8,128)(2,1)}, u32[]{:S(2)}, u32[]{:S(2)}) async-start(bf16[16,832,128]{2,1,0:T(8,128)(2,1)} %pad_maximum_fusion), calls=%async_computation | async-start | bytes 6815744 | tf_op jit(solution)/shard_map/all_to_all | solution.py:127
  81.9 67.0 %copy-start.5 = (f32[1,2,3,3072]{3,1,2,0:T(2,128)S(1)}, f32[1,2,3,3072]{3,1,2,0:T(2,128)}, u32[]{:S(2)}) copy-start(f32[1,2,3,3072]{3,1,2,0:T(2,128)} %param.15) | copy-start | bytes 221188
  137.9 44.5 %all-to-all-start.3 = ((bf16[16,256,128]{2,1,0:T(8,128)(2,1)}), bf16[16,256,128]{2,1,0:T(8,128)(2,1)S(1)}, u32[]{:S(2)}, u32[]{:S(2)}) async-start(bf16[16,256,128]{2,1,0:T(8,128)(2,1)} %get-tuple-element.8), calls=%async_computation.3 | async-start | bytes 2097152 | tf_op jit(solution)/shard_map/all_to_all | solution.py:131
  182.4 7.3 %copy-start.1 = (bf16[16,256,128]{2,1,0:T(8,128)(2,1)}, bf16[16,256,128]{2,1,0:T(8,128)(2,1)S(1)}, u32[]{:S(2)}) copy-start(bf16[16,256,128]{2,1,0:T(8,128)(2,1)S(1)} %all-to-all-done.3) | copy-start | bytes 3145732
  182.4 21.3 %all-to-all-start.1 = ((bf16[16,256,128]{2,1,0:T(8,128)(2,1)}), bf16[16,256,128]{2,1,0:T(8,128)(2,1)}, u32[]{:S(2)}, u32[]{:S(2)}) async-start(bf16[16,256,128]{2,1,0:T(8,128)(2,1)} %get-tuple-element.7), calls=%async_computation.1 | async-start | bytes 2097152 | tf_op jit(solution)/shard_map/all_to_all | solution.py:131
  211.0 0.7 copy-start.10
  211.0 0.7 copy-start.11
  211.0 0.7 copy-start.13
  211.7 0.8 copy-start.9
  212.5 0.9 copy-start.4
  212.5 1.0 copy-start.15
  212.5 1.0 copy-start.8
  212.5 1.6 copy-start.7
  212.5 2.2 copy-start.14
  212.5 8.5 %copy-start.6 = (f32[2,256,32]{1,2,0:T(8,128)S(1)}, f32[2,256,32]{1,2,0:T(8,128)}, u32[]{:S(2)}) copy-start(f32[2,256,32]{1,2,0:T(8,128)} %param.17) | copy-start | bytes 196612
  213.3 1.3 collective-permute-start
  217.6 10.9 %all-to-all-start.4 = ((f32[16,1,4]{2,1,0:T(1,128)}), f32[16,1,4]{2,1,0:T(1,128)S(1)}, u32[]{:S(2)}, u32[]{:S(2)}) async-start(f32[16,1,4]{2,1,0:T(1,128)} %broadcast_in_dim.8), calls=%async_computation.4 | async-start | bytes 16384 | tf_op jit(solution)/shard_map/all_to_all | solution.py:163
Sparse Core Ops, SparseCore 0:
  11.1 136.6 all-gather.1
